TPU v7x, 256 devices: a whole 4x4x8 slice. The times are simulated.
256 devices in a mesh: dp: 16 (over x, y), tensor: 16 (over z, core).
Axes of the slice: x: 4, y: 4, z: 8, core: 2. Of those that a mesh axis runs over, the one named last changes fastest.
Arguments:
- attention_output: bfloat16 [2048, 8192], P('dp', 'tensor'), may hold values from -6 to 6
- residual: bfloat16 [2048, 8192], P('dp', 'tensor'), may hold values from -6 to 6
- output_weight: bfloat16 [8192, 8192], P('tensor'), may hold values from -0.09375 to 0.09375
- down_factors: bfloat16 [1024, 8192, 16], P('dp', 'tensor'), may hold values from -0.0625 to 0.0625
- up_factors: bfloat16 [1024, 16, 8192], P('dp', None, 'tensor'), may hold values from -1.5 to 1.5
- adapter_index: int32 [2048], P('dp'), may hold values from 0 to 1023, as said below
Outputs:
- layer_out: bfloat16 [2048, 8192], P('dp', 'tensor')
Inputs may be any that keep to these rules, and one draw needn't show every extreme that they name: adapter_index // 64 is the request group that owns the adapter. Of one group's 128 rows at most 16 use adapters owned by one group, and in every draw some group owns the adapters of exactly 16 rows of every group.
All inputs are finite; a program needn't handle non-finite values.
Results may differ from a plain program's by a relative error of at most 0.0041.
Values may be sent and summed in bfloat16 or wider, within the bound.
No kernel may reach another device: no remote copies, remote signals or barrier semaphores. Data moves between devices by JAX's collectives and lax.ppermute only.
A program may use at most 64 MiB of HBM per device.

v0:
```python
import jax
import jax.numpy as jnp
from jax import lax
from jax.sharding import PartitionSpec as P


def gathered_total(x, axis):
    return lax.all_gather(x, axis).sum(0)


def body(attention_output, residual, output_weight, down_factors, up_factors, adapter_index):
    row_count = attention_output.shape[0]
    portion_width = attention_output.shape[1]
    column_count = output_weight.shape[1] // lax.axis_size("tensor")
    owned_total = down_factors.shape[0]
    rank_extent = down_factors.shape[2]
    groups = lax.axis_size("dp")
    capacity = 2 * row_count // groups
    slot_count = groups * capacity
    base_out = lax.psum_scatter(
        lax.dot_general(
            output_weight,
            attention_output,
            (((0,), (1,)), ((), ())),
            preferred_element_type=jnp.float32,
        ),
        "tensor",
        scatter_dimension=0,
        tiled=True,
    ).T
    owner_group = adapter_index // owned_total
    local_index = adapter_index % owned_total
    owner_hot = (owner_group[:, None] == jnp.arange(groups)[None, :]).astype(jnp.int32)
    slot_ids = jnp.arange(slot_count)
    rank_rows = jnp.cumsum(owner_hot, axis=0) - owner_hot
    row_slot = jnp.sum(rank_rows * owner_hot, axis=1) + owner_group * capacity
    placing = slot_ids[:, None] == row_slot[None, :]
    request = jnp.sum(jnp.where(placing, (local_index + 1)[None, :], 0), axis=1)
    request = request.astype(jnp.bfloat16).reshape(groups, capacity)
    numbers = (jnp.arange(owned_total) + 1).astype(jnp.bfloat16)
    outgoing = jnp.dot(
        placing.astype(jnp.bfloat16), attention_output, preferred_element_type=jnp.float32
    ).astype(jnp.bfloat16)
    outgoing = outgoing.reshape(groups, capacity, portion_width)
    x_slots = lax.all_to_all(outgoing, "dp", split_axis=0, concat_axis=0, tiled=True)
    wanted = lax.all_to_all(request, "dp", split_axis=0, concat_axis=0, tiled=True)
    per_source = x_slots.shape[1]
    slot_total = groups * per_source
    flat_rows = x_slots.reshape(slot_total, portion_width)
    chosen = (wanted.reshape(slot_total, 1) == numbers[None, :]).astype(jnp.bfloat16)
    all_terms = jnp.einsum(
        "nk,akj->naj", flat_rows, down_factors, preferred_element_type=jnp.float32
    )
    shrink = jnp.sum(all_terms * chosen.astype(jnp.float32)[:, :, None], axis=1)
    shrink = gathered_total(shrink, "tensor").astype(jnp.bfloat16)
    spread = (chosen[:, :, None] * shrink[:, None, :]).reshape(
        slot_total, owned_total * rank_extent
    )
    expand = jnp.dot(
        spread,
        up_factors.reshape(owned_total * rank_extent, column_count),
        preferred_element_type=jnp.float32,
    )
    expand = expand.astype(jnp.bfloat16).reshape(groups, per_source, column_count)
    returned = lax.all_to_all(expand, "dp", split_axis=0, concat_axis=0, tiled=True)
    branch_out = jnp.take(returned.reshape(slot_count, column_count), row_slot, axis=0).astype(
        jnp.float32
    )
    total = residual.astype(jnp.float32) + base_out + branch_out
    return total.astype(jnp.bfloat16)


def solution(mesh):
    return jax.shard_map(
        body,
        mesh=mesh,
        in_specs=(
            P("dp", "tensor"),
            P("dp", "tensor"),
            P("tensor", None),
            P("dp", "tensor", None),
            P("dp", None, "tensor"),
            P("dp"),
        ),
        out_specs=P("dp", "tensor"),
        check_vma=False,
    )
```

profile of v0, /device:TPU:14, one launch (start us, length us, event | category | flops | bytes accessed | tf_op | source)
XLA Modules:
  0.0 89.7 jit_solution(10961618333260080511)
XLA Ops:
  6.5 0.0 copy-start
  6.5 0.0 reduce-scatter.2.cloned.1.call-start
  6.6 7.8 %fusion.13 = f32[8192,128]{1,0:T(8,128)} fusion(bf16[512,8192]{1,0:T(8,128)(2,1)} %param.8, bf16[128,512]{1,0:T(8,128)(2,1)} %param.6), kind=kOutput, calls=%fused_computation.34 | convolution fusion | flops 1073741824 | bytes 12713984 | tf_op jit(solution)/shard_map/dot_general | solution.py:21
  14.4 0.0 reduce-scatter.2.cloned.1.call-update
  14.5 0.0 copy-done.4
  14.5 0.1 fusion.10
  14.6 0.2 reduce_window_sum.11
  14.7 0.2 select_reduce_fusion.1
  14.9 0.1 select_reduce_fusion
  15.1 0.7 convert_element_type.76
  15.8 7.3 %all-to-all-start = ((bf16[16,1,16]{2,1,0:T(2,128)(2,1)}), bf16[16,1,16]{2,1,0:T(2,128)(2,1)S(1)}, u32[]{:S(2)}, u32[]{:S(2)}) async-start(bf16[16,1,16]{2,1,0:T(2,128)(2,1)} %convert_element_type.76), calls=%async_computation.1 | async-start | bytes 16384 | tf_op jit(solution)/shard_map/all_to_all | solution.py:46
  23.1 0.0 copy-done.1
  23.1 0.9 %convolution_convert_fusion = bf16[256,512]{1,0:T(8,128)(2,1)} fusion(bf16[128,512]{1,0:T(8,128)(2,1)S(1)} %copy-done.1, s32[128]{0:T(128)S(1)} %get-tuple-element.6), kind=kOutput, calls=%fused_computation.4 | convolution fusion | flops 33718272 | bytes 393728 | tf_op jit(solution)/shard_map/dot_general | solution.py:41
  24.0 3.7 %all-to-all-done = bf16[16,1,16]{2,1,0:T(2,128)(2,1)S(1)} async-done(((bf16[16,1,16]{2,1,0:T(2,128)(2,1)}), bf16[16,1,16]{2,1,0:T(2,128)(2,1)S(1)}, u32[]{:S(2)}, u32[]{:S(2)}) %all-to-all-start) | async-done | bytes 544 | tf_op jit(solution)/shard_map/all_to_all | solution.py:46
  27.7 6.4 %all-to-all-start.1 = ((bf16[16,16,512]{2,1,0:T(8,128)(2,1)}), bf16[16,16,512]{2,1,0:T(8,128)(2,1)S(1)}, u32[]{:S(2)}, u32[]{:S(2)}) async-start(bf16[16,16,512]{2,1,0:T(8,128)(2,1)} %bitcast.1), calls=%async_computation.2 | async-start | bytes 524288 | tf_op jit(solution)/shard_map/all_to_all | solution.py:45
  34.1 0.0 copy-done.2
  34.1 0.1 copy.23
  34.2 0.1 eq.56
  34.3 0.1 compare_convert_fusion
  34.4 5.1 %all-to-all-done.1 = bf16[16,16,512]{2,1,0:T(8,128)(2,1)S(1)} async-done(((bf16[16,16,512]{2,1,0:T(8,128)(2,1)}), bf16[16,16,512]{2,1,0:T(8,128)(2,1)S(1)}, u32[]{:S(2)}, u32[]{:S(2)}) %all-to-all-start.1) | async-done | bytes 262176 | tf_op jit(solution)/shard_map/all_to_all | solution.py:45
  39.6 0.0 copy-done.3
  39.6 1.3 %fusion = f32[256,16]{0,1:T(8,128)S(1)} fusion(bf16[256,512,1]{1,0,2:T(8,128)(2,1)S(1)} %bitcast.27, bf16[64,512,16]{1,2,0:T(8,128)(2,1)S(1)} %copy-done.3, f32[256,64]{0,1:T(8,128)S(1)} %get-tuple-element.8), kind=kOutput, calls=%fused_computation.2 | convolution fusion | flops 268955648 | bytes 1392640 | tf_op jit(solution)/shard_map/nk,akj->naj/dot_general | solution.py:51
  40.9 21.0 %all-gather = f32[4096,16]{0,1:T(8,128)S(1)} all-gather(f32[256,16]{0,1:T(8,128)S(1)} %fusion), channel_id=2, replica_groups=mesh['dp'=16,'tensor'=16] {'tensor'}, dimensions={0}, use_global_device_ids=true | all-gather | bytes 278528 | tf_op jit(solution)/shard_map/all_gather | solution.py:8
  61.9 0.1 copy.29
  62.1 2.0 %fusion.1 = bf16[256,512]{1,0:T(8,128)(2,1)} fusion(bf16[64,16,512]{2,1,0:T(8,128)(2,1)S(1)} %copy-done, bf16[256,16]{0,1:T(8,128)(2,1)S(1)} %bitcast_reduce_fusion, bf16[256,64]{0,1:T(8,128)(2,1)S(1)} %get-tuple-element.7), kind=kOutput, calls=%fused_computation.5 | convolution fusion | flops 268828672 | bytes 1351680 | tf_op jit(solution)/shard_map/dot_general | solution.py:59
  64.1 6.7 %all-to-all-start.2 = ((bf16[16,16,512]{2,1,0:T(8,128)(2,1)}), bf16[16,16,512]{2,1,0:T(8,128)(2,1)S(1)}, u32[]{:S(2)}, u32[]{:S(2)}) async-start(bf16[16,16,512]{2,1,0:T(8,128)(2,1)} %bitcast.5), calls=%async_computation.3 | async-start | bytes 524288 | tf_op jit(solution)/shard_map/all_to_all | solution.py:65
  70.8 6.0 %all-to-all-done.2 = bf16[16,16,512]{2,1,0:T(8,128)(2,1)S(1)} async-done(((bf16[16,16,512]{2,1,0:T(8,128)(2,1)}), bf16[16,16,512]{2,1,0:T(8,128)(2,1)S(1)}, u32[]{:S(2)}, u32[]{:S(2)}) %all-to-all-start.2) | async-done | bytes 262176 | tf_op jit(solution)/shard_map/all_to_all | solution.py:65
  76.8 0.8 gather_fusion
  77.6 0.1 copy.27
  77.7 3.3 %reduce-scatter.2.cloned.1.call-done = f32[512,128]{1,0:T(8,128)} async-done(((f32[8192,128]{1,0:T(8,128)}), f32[512,128]{1,0:T(8,128)}) %reduce-scatter.2.cloned.1.call-update) | async-done | bytes 262160 | tf_op jit(solution)/shard_map/reduce_scatter | solution.py:20
  81.0 1.0 %fusion.6 = bf16[128,512]{0,1:T(8,128)(2,1)S(1)} fusion(f32[512,128]{1,0:T(8,128)} %reduce-scatter.2.cloned.1.call-done, bf16[128,512]{0,1:T(8,128)(2,1)S(1)} %copy.23, bf16[128,512]{0,1:T(8,128)(2,1)S(1)} %copy.27, pred[128]{0:T(512)(128)(4,1)S(1)} %get-tuple-element.5), kind=kLoop, calls=%fused_computation.12 | loop fusion | flops 393216 | bytes 655488 | tf_op jit(solution)/shard_map/convert_element_type | solution.py:70
  82.0 0.8 copy.28
  (13 shorter events, 0.1 us)
Async XLA Ops:
  6.5 55.5 %copy-start = (bf16[64,16,512]{2,1,0:T(8,128)(2,1)S(1)}, bf16[64,16,512]{2,1,0:T(8,128)(2,1)}, u32[]{:S(2)}) copy-start(bf16[64,16,512]{2,1,0:T(8,128)(2,1)} %param.10) | copy-start | bytes 3145732
  6.5 16.5 %copy-start.1 = (bf16[128,512]{1,0:T(8,128)(2,1)S(1)}, bf16[128,512]{1,0:T(8,128)(2,1)}, u32[]{:S(2)}) copy-start(bf16[128,512]{1,0:T(8,128)(2,1)} %param.6) | copy-start | bytes 393220
  6.5 7.9 %copy-start.4 = (s32[128]{0:T(128)S(1)}, s32[128]{0:T(128)}, u32[]{:S(2)}) copy-start(s32[128]{0:T(128)} %param.11) | copy-start | bytes 1540
  6.5 27.5 %copy-start.2 = (bf16[128,512]{1,0:T(8,128)(2,1)S(1)}, bf16[128,512]{1,0:T(8,128)(2,1)}, u32[]{:S(2)}) copy-start(bf16[128,512]{1,0:T(8,128)(2,1)} %param.7) | copy-start | bytes 393220
  6.5 33.0 %copy-start.3 = (bf16[64,512,16]{1,2,0:T(8,128)(2,1)S(1)}, bf16[64,512,16]{1,2,0:T(8,128)(2,1)}, u32[]{:S(2)}) copy-start(bf16[64,512,16]{1,2,0:T(8,128)(2,1)} %param.9) | copy-start | bytes 3145732
  6.5 74.5 %reduce-scatter.2.cloned.1.call-start = ((), (), s32[]{:S(2)}) async-start(), calls=%async_computation.4 | async-start | bytes 4456448 | tf_op jit(solution)/shard_map/reduce_scatter | solution.py:20
  15.8 11.9 %all-to-all-start = ((bf16[16,1,16]{2,1,0:T(2,128)(2,1)}), bf16[16,1,16]{2,1,0:T(2,128)(2,1)S(1)}, u32[]{:S(2)}, u32[]{:S(2)}) async-start(bf16[16,1,16]{2,1,0:T(2,128)(2,1)} %convert_element_type.76), calls=%async_computation.1 | async-start | bytes 16384 | tf_op jit(solution)/shard_map/all_to_all | solution.py:46
  27.7 11.9 %all-to-all-start.1 = ((bf16[16,16,512]{2,1,0:T(8,128)(2,1)}), bf16[16,16,512]{2,1,0:T(8,128)(2,1)S(1)}, u32[]{:S(2)}, u32[]{:S(2)}) async-start(bf16[16,16,512]{2,1,0:T(8,128)(2,1)} %bitcast.1), calls=%async_computation.2 | async-start | bytes 524288 | tf_op jit(solution)/shard_map/all_to_all | solution.py:45
  64.1 12.7 %all-to-all-start.2 = ((bf16[16,16,512]{2,1,0:T(8,128)(2,1)}), bf16[16,16,512]{2,1,0:T(8,128)(2,1)S(1)}, u32[]{:S(2)}, u32[]{:S(2)}) async-start(bf16[16,16,512]{2,1,0:T(8,128)(2,1)} %bitcast.5), calls=%async_computation.3 | async-start | bytes 524288 | tf_op jit(solution)/shard_map/all_to_all | solution.py:65
Sparse Core Ops, SparseCore 0:
  14.6 66.3 reduce-scatter.1
where the time goes:
time: 90.1 us; the launch traced here: 89.7 us
  blocking collectives  21 us (23%)
  starting transfers between devices  20.4 us (23%)
  waiting for transfers between devices  18.1 us (20%)
  between operations  13.5 us (15%)
  matrix products  12.1 us (13%)
  local copies, waits for them, and re-layouts  2.73 us (3%)
  other arithmetic  1.77 us (2%)
    all_gather x1, blocking collectives, gathered_total(): return lax.all_gather(x, axis).sum(0)  21 us
    dot_general x1, matrix products, body(): lax.dot_general(output_weight, attention_output, (((0,), (1,)), ((), ()))...  7.84 us
    all_to_all x1, starting transfers between devices, body(): lax.all_to_all(request, 'dp', split_axis=0, concat_axis=0, tiled=True)  7.31 us
    all_to_all x1, starting transfers between devices, body(): lax.all_to_all(expand, 'dp', split_axis=0, concat_axis=0, tiled=True)  6.67 us
    all_to_all x1, starting transfers between devices, body(): lax.all_to_all(outgoing, 'dp', split_axis=0, concat_axis=0, tiled=True)  6.37 us
    all_to_all x1, waiting for transfers between devices, body(): lax.all_to_all(expand, 'dp', split_axis=0, concat_axis=0, tiled=True)  5.98 us
    all_to_all x1, waiting for transfers between devices, body(): lax.all_to_all(outgoing, 'dp', split_axis=0, concat_axis=0, tiled=True)  5.13 us
    all_to_all x1, waiting for transfers between devices, body(): lax.all_to_all(request, 'dp', split_axis=0, concat_axis=0, tiled=True)  3.68 us
  transfers between devices with their start and end apart: 4, of which 4 were waited for; matrix products, arithmetic and copies ran while one was open for 8% of the time, Pallas kernels for 0%

commit v1 on v0

v1 whole, which is shorter than its diff:
```python
import functools

import jax
import jax.numpy as jnp
from jax import lax
from jax.experimental import pallas as pl
from jax.experimental.pallas import tpu as pltpu
from jax.sharding import PartitionSpec as P

BF16 = jnp.bfloat16
F32 = jnp.float32
LANES = 128
RIGHT = (1, 4, -2)
LEFT = (-1, 2)
KEEP = (0, 3, -3)
GRANT = pltpu.CompilerParams(vmem_limit_bytes=16 * 2**20)


def vmem_specs(count):
    return [pl.BlockSpec(memory_space=pltpu.VMEM)] * count


def slots_of(index_row, owned, capacity):
    rows = index_row.shape[1]
    owner = index_row // owned
    owner_across = jnp.broadcast_to(owner, (rows, rows))
    owner_down = owner_across.T
    earlier = lax.broadcasted_iota(jnp.int32, (rows, rows), 0) < lax.broadcasted_iota(
        jnp.int32, (rows, rows), 1
    )
    same = jnp.where((owner_down == owner_across) & earlier, 1, 0)
    rank = jnp.sum(same, axis=0, keepdims=True)
    return owner * capacity + rank


def dispatch_kernel(owned, capacity, index_ref, x_ref, out_ref):
    index_row = index_ref[...]
    rows, width = x_ref.shape
    slot_count = out_ref.shape[0]
    slot = slots_of(index_row, owned, capacity)
    placing = lax.broadcasted_iota(jnp.int32, (slot_count, rows), 0) == slot
    out_ref[:, :width] = jnp.dot(
        jnp.where(placing, 1.0, 0.0).astype(BF16), x_ref[...], preferred_element_type=F32
    ).astype(BF16)
    number = (index_row % owned + 1).astype(F32)
    asked = jnp.sum(jnp.where(placing, number, 0.0), axis=1, keepdims=True)
    out_ref[:, width:] = jnp.broadcast_to(asked, (slot_count, LANES)).astype(BF16)


def dispatch(index_row, x, owned, capacity, slot_count):
    rows, width = x.shape
    return pl.pallas_call(
        functools.partial(dispatch_kernel, owned, capacity),
        out_shape=jax.ShapeDtypeStruct((slot_count, width + LANES), BF16),
        in_specs=vmem_specs(2),
        out_specs=pl.BlockSpec(memory_space=pltpu.VMEM),
        cost_estimate=pl.CostEstimate(
            flops=2 * slot_count * rows * width, bytes_accessed=2 * slot_count * width, transcendentals=0
        ),
        compiler_params=GRANT,
        name="dispatch",
    )(index_row, x)


def product_kernel(half_ref, x_ref, w_ref, out_ref):
    out_ref[0] = jnp.dot(x_ref[...], w_ref[...], preferred_element_type=F32).astype(out_ref.dtype)


def half_product(x, w, parity, chips, out_dtype, name):
    rows, depth = x.shape
    block = w.shape[1] // (2 * chips)
    return pl.pallas_call(
        product_kernel,
        out_shape=jax.ShapeDtypeStruct((chips, rows, block), out_dtype),
        grid_spec=pltpu.PrefetchScalarGridSpec(
            num_scalar_prefetch=1,
            grid=(chips,),
            in_specs=[
                pl.BlockSpec((rows, depth), lambda i, half: (0, 0)),
                pl.BlockSpec((depth, block), lambda i, half: (0, 2 * i + half[0])),
            ],
            out_specs=pl.BlockSpec((1, rows, block), lambda i, half: (i, 0, 0)),
        ),
        cost_estimate=pl.CostEstimate(
            flops=2 * rows * depth * block * chips,
            bytes_accessed=2 * depth * block * chips,
            transcendentals=0,
        ),
        compiler_params=pltpu.CompilerParams(vmem_limit_bytes=56 * 2**20),
        name=name,
    )(parity, x, w)


def pair_kernel(chips, z_ref, mine_ref, other_ref, right_ref, left_ref, keep_ref):
    z = z_ref[0]
    for refs, steps in ((right_ref, RIGHT), (left_ref, LEFT), (keep_ref, KEEP)):
        for place, step in enumerate(steps):
            at = lax.rem(z + (step + chips), chips)
            total = mine_ref[at] + other_ref[at].astype(F32)
            refs[place] = total.astype(refs.dtype)


def pair_sum(z, mine, other):
    chips, rows, block = mine.shape
    return pl.pallas_call(
        functools.partial(pair_kernel, chips),
        out_shape=(
            jax.ShapeDtypeStruct((len(RIGHT), rows, block), BF16),
            jax.ShapeDtypeStruct((len(LEFT), rows, block), BF16),
            jax.ShapeDtypeStruct((len(KEEP), rows, block), F32),
        ),
        in_specs=[pl.BlockSpec(memory_space=pltpu.SMEM)] + vmem_specs(2),
        out_specs=tuple(vmem_specs(3)),
        cost_estimate=pl.CostEstimate(flops=mine.size, bytes_accessed=8 * mine.size, transcendentals=0),
        compiler_params=GRANT,
        name="pair_sum",
    )(z, mine, other)


def relay_kernel(keep_ref, right_ref, left_ref, here_ref, far_right_ref, far_left_ref):
    here_ref[...] = keep_ref[0] + right_ref[0].astype(F32) + left_ref[0].astype(F32)
    far_right_ref[...] = (
        keep_ref[1] + right_ref[1].astype(F32) + left_ref[1].astype(F32)
    ).astype(BF16)
    far_left_ref[...] = (keep_ref[2] + right_ref[2].astype(F32)).astype(BF16)


def relay(keep, right, left):
    _, rows, block = keep.shape
    return pl.pallas_call(
        relay_kernel,
        out_shape=(
            jax.ShapeDtypeStruct((rows, block), F32),
            jax.ShapeDtypeStruct((rows, block), BF16),
            jax.ShapeDtypeStruct((rows, block), BF16),
        ),
        in_specs=vmem_specs(3),
        out_specs=tuple(vmem_specs(3)),
        cost_estimate=pl.CostEstimate(flops=5 * rows * block, bytes_accessed=4 * keep.size, transcendentals=0),
        compiler_params=GRANT,
        name="relay",
    )(keep, right, left)


def wanted_row(slots_ref, width):
    tags = slots_ref[:, width:].astype(F32)
    return tags.T[0:1, :]


def shrink_kernel(owned, copies, slots_ref, down_ref, out_ref):
    slot_total = slots_ref.shape[0]
    width = down_ref.shape[1]
    rank = down_ref.shape[0] // owned
    terms = lax.dot_general(
        down_ref[...], slots_ref[:, :width], (((1,), (1,)), ((), ())), preferred_element_type=F32
    )
    wanted = wanted_row(slots_ref, width)
    total = jnp.zeros((rank, slot_total), F32)
    for adapter in range(owned):
        total += jnp.where(wanted == adapter + 1, terms[adapter * rank : (adapter + 1) * rank], 0.0)
    for copy in range(copies):
        out_ref[copy] = total


def shrink_terms(slots, down, owned, copies):
    slot_total = slots.shape[0]
    rank = down.shape[0] // owned
    return pl.pallas_call(
        functools.partial(shrink_kernel, owned, copies),
        out_shape=jax.ShapeDtypeStruct((copies, rank, slot_total), F32),
        in_specs=vmem_specs(2),
        out_specs=pl.BlockSpec(memory_space=pltpu.VMEM),
        cost_estimate=pl.CostEstimate(
            flops=2 * slot_total * down.size, bytes_accessed=2 * down.size, transcendentals=0
        ),
        compiler_params=GRANT,
        name="shrink",
    )(slots, down)


def expand_kernel(owned, parts_ref, slots_ref, up_ref, out_ref):
    slot_total = slots_ref.shape[0]
    copies, rank, _ = parts_ref.shape
    total = parts_ref[0]
    for copy in range(1, copies):
        total += parts_ref[copy]
    shrink = total.astype(BF16).astype(F32)
    wanted = wanted_row(slots_ref, slots_ref.shape[1] - LANES)
    spread = jnp.concatenate(
        [jnp.where(wanted == adapter + 1, shrink, 0.0).astype(BF16) for adapter in range(owned)], axis=0
    )
    out_ref[...] = lax.dot_general(
        spread, up_ref[...], (((0,), (0,)), ((), ())), preferred_element_type=F32
    ).astype(BF16)


def expand_rows(parts, slots, up, owned):
    slot_total = slots.shape[0]
    return pl.pallas_call(
        functools.partial(expand_kernel, owned),
        out_shape=jax.ShapeDtypeStruct((slot_total, up.shape[1]), BF16),
        in_specs=vmem_specs(3),
        out_specs=pl.BlockSpec(memory_space=pltpu.VMEM),
        cost_estimate=pl.CostEstimate(
            flops=2 * slot_total * up.size, bytes_accessed=2 * up.size, transcendentals=0
        ),
        compiler_params=GRANT,
        name="expand",
    )(parts, slots, up)


def finish_kernel(
    owned, capacity, index_ref, residual_ref, here_ref, right_ref, left_ref, returned_ref, out_ref
):
    rows = residual_ref.shape[0]
    slot_count = returned_ref.shape[0]
    slot = slots_of(index_ref[...], owned, capacity)
    placing = lax.broadcasted_iota(jnp.int32, (slot_count, rows), 0) == slot
    branch = lax.dot_general(
        jnp.where(placing, 1.0, 0.0).astype(BF16),
        returned_ref[...],
        (((0,), (0,)), ((), ())),
        preferred_element_type=F32,
    )
    base = here_ref[...] + right_ref[...].astype(F32) + left_ref[...].astype(F32)
    out_ref[...] = (residual_ref[...].astype(F32) + base + branch).astype(BF16)


def finish(index_row, residual, sums, returned, owned, capacity):
    return pl.pallas_call(
        functools.partial(finish_kernel, owned, capacity),
        out_shape=jax.ShapeDtypeStruct(residual.shape, BF16),
        in_specs=vmem_specs(6),
        out_specs=pl.BlockSpec(memory_space=pltpu.VMEM),
        cost_estimate=pl.CostEstimate(
            flops=2 * returned.size * residual.shape[0], bytes_accessed=8 * residual.size, transcendentals=0
        ),
        compiler_params=GRANT,
        name="finish",
    )(index_row, residual, *sums, returned)


def body(attention_output, residual, output_weight, down_factors, up_factors, adapter_index):
    rows, width = attention_output.shape
    owned, _, rank = down_factors.shape
    columns = up_factors.shape[2]
    groups = lax.axis_size("dp")
    shards = lax.axis_size("tensor")
    chips = shards // 2
    capacity = 2 * rows // groups
    slot_count = groups * capacity
    place = lax.axis_index("tensor")
    z, core = (place >> 1).reshape(1), (place & 1).reshape(1)
    siblings = [(i, i ^ 1) for i in range(shards)]

    def along_z(array, step):
        return lax.ppermute(array, "tensor", [(i, (i + 2 * step) % shards) for i in range(shards)])

    index_row = adapter_index.reshape(1, rows)
    outgoing = dispatch(index_row, attention_output, owned, capacity, slot_count)
    outgoing, x = lax.optimization_barrier((outgoing, attention_output))
    outgoing = outgoing.reshape(groups, capacity, width + LANES)
    slots = lax.all_to_all(outgoing, "dp", split_axis=0, concat_axis=0, tiled=True)

    theirs = half_product(x, output_weight, 1 - core, chips, BF16, "product_theirs")
    other = lax.ppermute(theirs, "tensor", siblings)
    mine = half_product(x, output_weight, core, chips, F32, "product_mine")
    to_right, to_left, keep = pair_sum(z, mine, other)
    from_left, from_right = along_z(to_right, 1), along_z(to_left, -1)

    slots, keep = lax.optimization_barrier((slots, keep))
    slots = slots.reshape(slot_count, width + LANES)
    down = down_factors.transpose(0, 2, 1).reshape(owned * rank, width)
    parts = shrink_terms(slots, down, owned, shards)
    parts = lax.all_to_all(parts, "tensor", split_axis=0, concat_axis=0, tiled=True)
    here, far_right, far_left = relay(keep, from_left, from_right)
    sums = (here, along_z(far_right, 3), along_z(far_left, -3))
    expand = expand_rows(parts, slots, up_factors.reshape(owned * rank, columns), owned)
    expand = expand.reshape(groups, capacity, columns)
    returned = lax.all_to_all(expand, "dp", split_axis=0, concat_axis=0, tiled=True)
    returned = returned.reshape(slot_count, columns)
    return finish(index_row, residual, sums, returned, owned, capacity)


def solution(mesh):
    return jax.shard_map(
        body,
        mesh=mesh,
        in_specs=(
            P("dp", "tensor"),
            P("dp", "tensor"),
            P("tensor", None),
            P("dp", "tensor", None),
            P("dp", None, "tensor"),
            P("dp"),
        ),
        out_specs=P("dp", "tensor"),
        check_vma=False,
    )
```

time: 90.1 us -> 75.9 us (0.84)
  the two profiles are of different devices: /device:TPU:14 before, /device:TPU:32 now
where the time goes in v1:
time: 75.9 us; the launch traced here: 74.7 us
  starting transfers between devices  30.1 us (40%)
  waiting for transfers between devices  18.6 us (25%)
  Pallas kernels  18.4 us (24%)
  local copies, waits for them, and re-layouts  7.55 us (10%)
    pallas_call x2, Pallas kernels, half_product(): pl.pallas_call(product_kernel, out_shape=jax.ShapeDtypeStruct((chips, row...  13.6 us
    ppermute x4, waiting for transfers between devices, along_z(): lax.ppermute(array, 'tensor', [(i, (i + 2 * step) % shards) for i in rang...  10.9 us
    all_to_all x1, starting transfers between devices, body(): lax.all_to_all(parts, 'tensor', split_axis=0, concat_axis=0, tiled=True)  8.59 us
    all_to_all x1, waiting for transfers between devices, body(): lax.all_to_all(parts, 'tensor', split_axis=0, concat_axis=0, tiled=True)  7.62 us
    unnamed x22, local copies, waits for them, and re-layouts  7.55 us
    all_to_all x1, starting transfers between devices, body(): lax.all_to_all(expand, 'dp', split_axis=0, concat_axis=0, tiled=True)  7.21 us
    all_to_all x1, starting transfers between devices, body(): lax.all_to_all(outgoing, 'dp', split_axis=0, concat_axis=0, tiled=True)  7.19 us
    ppermute x4, starting transfers between devices, along_z(): lax.ppermute(array, 'tensor', [(i, (i + 2 * step) % shards) for i in rang...  7.14 us
  transfers between devices with their start and end apart: 8, of which 3 were waited for; matrix products, arithmetic and copies ran while one was open for 0% of the time, Pallas kernels for 11%

profile of v1, /device:TPU:32, one launch (start us, length us, event | category | flops | bytes accessed | tf_op | source)
XLA Modules:
  0.0 74.7 jit_solution(17615554163052171997)
XLA Ops:
  0.0 0.9 %copy-done.1 = bf16[128,512]{1,0:T(8,128)(2,1)S(1)} copy-done((bf16[128,512]{1,0:T(8,128)(2,1)S(1)}, bf16[128,512]{1,0:T(8,128)(2,1)}, u32[]{:S(2)}) %copy-start.1) | copy-done | bytes 131096
  0.9 0.7 copy-done.7
  1.6 1.1 %dispatch.1 = bf16[256,640]{1,0:T(8,128)(2,1)} custom-call(s32[1,128]{1,0:T(1,128)S(1)} %bitcast.16, bf16[128,512]{1,0:T(8,128)(2,1)S(1)} %copy-done.1), custom_call_target="tpu_custom_call" | custom-call | flops 33554432 | bytes 262144 | tf_op jit(solution)/shard_map/dispatch/pallas_call | solution.py:52
  2.6 6.7 %product_theirs.1 = bf16[8,128,512]{2,1,0:T(8,128)(2,1)} custom-call(s32[1]{0:T(128)S(6)} %sub.3.half_ref, bf16[128,512]{1,0:T(8,128)(2,1)} %x_ref.3, bf16[512,8192]{1,0:T(8,128)(2,1)} %w_ref.3), custom_call_target="tpu_custom_call" | custom-call | flops 536870912 | bytes 4194304 | tf_op jit(solution)/shard_map/product_theirs/pallas_call | solution.py:72
  9.3 0.0 collective-permute-start
  9.3 7.2 %all-to-all-start = ((bf16[16,16,640]{2,1,0:T(8,128)(2,1)}), bf16[16,16,640]{2,1,0:T(8,128)(2,1)S(1)}, u32[]{:S(2)}, u32[]{:S(2)}) async-start(bf16[16,16,640]{2,1,0:T(8,128)(2,1)} %bitcast.1), calls=%async_computation | async-start | bytes 655360 | tf_op jit(solution)/shard_map/all_to_all | solution.py:263
  16.5 0.0 copy-start.8
  16.5 6.9 %product_mine.1.mine_ref = f32[8,128,512]{2,1,0:T(8,128)} custom-call(s32[1]{0:T(128)} %bitcast.3.half_ref, bf16[128,512]{1,0:T(8,128)(2,1)} %x_ref.3, bf16[512,8192]{1,0:T(8,128)(2,1)} %w_ref.3), custom_call_target="tpu_custom_call" | custom-call | flops 536870912 | bytes 4194304 | tf_op jit(solution)/shard_map/product_mine/pallas_call | solution.py:72
  23.4 0.0 collective-permute-done.other_ref
  23.4 1.6 %copy-done = f32[8,128,512]{2,1,0:T(8,128)S(1)} copy-done((f32[8,128,512]{2,1,0:T(8,128)S(1)}, f32[8,128,512]{2,1,0:T(8,128)}, u32[]{:S(2)}) %copy-start) | copy-done | bytes 2097176
  25.0 0.2 pair_sum.1
  25.2 0.9 %copy-done.4 = f32[3,128,512]{2,1,0:T(8,128)} copy-done((f32[3,128,512]{2,1,0:T(8,128)}, f32[3,128,512]{2,1,0:T(8,128)S(1)}, u32[]{:S(2)}) %copy-start.4) | copy-done | bytes 786456
  26.1 0.8 %copy-done.9 = bf16[3,128,512]{2,1,0:T(8,128)(2,1)} copy-done((bf16[3,128,512]{2,1,0:T(8,128)(2,1)}, bf16[3,128,512]{2,1,0:T(8,128)(2,1)S(1)}, u32[]{:S(2)}) %copy-start.9) | copy-done | bytes 393240
  26.8 0.7 copy-done.10
  27.5 0.0 all-to-all-done
  27.5 1.2 %shrink.1 = f32[16,16,256]{2,1,0:T(8,128)} custom-call(bf16[256,640]{1,0:T(8,128)(2,1)S(1)} %bitcast.11, bf16[1024,512]{1,0:T(8,128)(2,1)S(1)} %bitcast.13), custom_call_target="tpu_custom_call" | custom-call | flops 268435456 | bytes 1048576 | tf_op jit(solution)/shard_map/shrink/pallas_call | solution.py:168
  28.8 8.6 %all-to-all-start.1 = ((f32[16,16,256]{2,1,0:T(8,128)}), f32[16,16,256]{2,1,0:T(8,128)S(1)}, u32[]{:S(2)}, u32[]{:S(2)}) async-start(f32[16,16,256]{2,1,0:T(8,128)} %shrink.1), calls=%async_computation.1 | async-start | bytes 524288 | tf_op jit(solution)/shard_map/all_to_all | solution.py:275
  37.3 1.5 %collective-permute-start.1 = (bf16[3,128,512]{2,1,0:T(8,128)(2,1)}, bf16[3,128,512]{2,1,0:T(8,128)(2,1)S(1)}, u32[]{:S(2)}, u32[]{:S(2)}) collective-permute-start(bf16[3,128,512]{2,1,0:T(8,128)(2,1)} %copy-done.9), channel_id=1, source_target_pairs={{0,2},{1,3},{2,4},{3,5},{4,6},{5,7},{6,8},{7,9},{8,10},{9,11},{10,... | collective-permute-start | bytes 1179656 | tf_op jit(solution)/shard_map/ppermute | solution.py:257
  38.8 0.6 collective-permute-start.2
  39.4 7.6 %all-to-all-done.1.parts_ref = f32[16,16,256]{2,1,0:T(8,128)S(1)} async-done(((f32[16,16,256]{2,1,0:T(8,128)}), f32[16,16,256]{2,1,0:T(8,128)S(1)}, u32[]{:S(2)}, u32[]{:S(2)}) %all-to-all-start.1) | async-done | bytes 262176 | tf_op jit(solution)/shard_map/all_to_all | solution.py:275
  47.0 1.3 %expand.1 = bf16[256,512]{1,0:T(8,128)(2,1)} custom-call(f32[16,16,256]{2,1,0:T(8,128)S(1)} %all-to-all-done.1.parts_ref, bf16[256,640]{1,0:T(8,128)(2,1)S(1)} %bitcast.12, bf16[1024,512]{1,0:T(8,128)(2,1)S(1)} %bitcast.14), custom_call_target="tpu_custom_call" | custom-call | flops 268435456 | bytes 1048576 | tf_op jit(solution)/shard_map/expand/pallas_call | solution.py:199
  48.3 7.2 %all-to-all-start.2 = ((bf16[16,16,512]{2,1,0:T(8,128)(2,1)}), bf16[16,16,512]{2,1,0:T(8,128)(2,1)S(1)}, u32[]{:S(2)}, u32[]{:S(2)}) async-start(bf16[16,16,512]{2,1,0:T(8,128)(2,1)} %bitcast.8), calls=%async_computation.2 | async-start | bytes 524288 | tf_op jit(solution)/shard_map/all_to_all | solution.py:280
  55.5 0.0 collective-permute-done.2.left_ref
  55.5 0.0 collective-permute-done.1.right_ref
  55.5 1.1 %copy-done.5 = f32[3,128,512]{2,1,0:T(8,128)S(1)} copy-done((f32[3,128,512]{2,1,0:T(8,128)S(1)}, f32[3,128,512]{2,1,0:T(8,128)}, u32[]{:S(2)}) %copy-start.5) | copy-done | bytes 786456
  56.6 0.1 relay.1
  56.7 2.6 %collective-permute-start.3 = (bf16[128,512]{1,0:T(8,128)(2,1)S(1)}, bf16[128,512]{1,0:T(8,128)(2,1)S(1)}, u32[]{:S(2)}, u32[]{:S(2)}) collective-permute-start(bf16[128,512]{1,0:T(8,128)(2,1)S(1)} %get-tuple-element.22), channel_id=1, source_target_pairs={{0,6},{1,7},{2,8},{3,9},{4,10},{5,11},{6,12},{7,13},{8,14},{9,15},... | collective-permute-start | bytes 393224 | tf_op jit(solution)/shard_map/ppermute | solution.py:257
  59.3 2.5 %collective-permute-start.4 = (bf16[128,512]{1,0:T(8,128)(2,1)S(1)}, bf16[128,512]{1,0:T(8,128)(2,1)S(1)}, u32[]{:S(2)}, u32[]{:S(2)}) collective-permute-start(bf16[128,512]{1,0:T(8,128)(2,1)S(1)} %get-tuple-element.23), channel_id=1, source_target_pairs={{0,10},{1,11},{2,12},{3,13},{4,14},{5,15},{6,0},{7,1},{8,2},{9,3},... | collective-permute-start | bytes 393224 | tf_op jit(solution)/shard_map/ppermute | solution.py:257
  61.8 8.6 %collective-permute-done.3.right_ref = bf16[128,512]{1,0:T(8,128)(2,1)S(1)} collective-permute-done((bf16[128,512]{1,0:T(8,128)(2,1)S(1)}, bf16[128,512]{1,0:T(8,128)(2,1)S(1)}, u32[]{:S(2)}, u32[]{:S(2)}) %collective-permute-start.3) | collective-permute-done | bytes 131104 | tf_op jit(solution)/shard_map/ppermute | solution.py:257
  70.4 2.4 %collective-permute-done.4.left_ref = bf16[128,512]{1,0:T(8,128)(2,1)S(1)} collective-permute-done((bf16[128,512]{1,0:T(8,128)(2,1)S(1)}, bf16[128,512]{1,0:T(8,128)(2,1)S(1)}, u32[]{:S(2)}, u32[]{:S(2)}) %collective-permute-start.4) | collective-permute-done | bytes 131104 | tf_op jit(solution)/shard_map/ppermute | solution.py:257
  72.8 0.9 %copy-done.6 = bf16[128,512]{1,0:T(8,128)(2,1)S(1)} copy-done((bf16[128,512]{1,0:T(8,128)(2,1)S(1)}, bf16[128,512]{1,0:T(8,128)(2,1)}, u32[]{:S(2)}) %copy-start.6) | copy-done | bytes 131096
  73.7 1.0 %finish.1 = bf16[128,512]{1,0:T(8,128)(2,1)} custom-call(s32[1,128]{1,0:T(1,128)S(1)} %bitcast.17, bf16[128,512]{1,0:T(8,128)(2,1)S(1)} %copy-done.6, f32[128,512]{1,0:T(8,128)S(1)} %get-tuple-element.21.here_ref, bf16[128,512]{1,0:T(8,128)(2,1)S(1)} %collective-permute-done.3.right_ref, bf16[128,512]{1,0:T(8,128)(2,1)S(1)} %collective-permute-done.4.left_ref, ...), custom_call_target="tpu_custom_call" | custom-call | flops 33554432 | bytes 524288 | tf_op jit(solution)/shard_map/finish/pallas_call | solution.py:230
  (14 shorter events, 0.0 us)
Async XLA Ops:
  0.0 0.9 %copy-start.1 = (bf16[128,512]{1,0:T(8,128)(2,1)S(1)}, bf16[128,512]{1,0:T(8,128)(2,1)}, u32[]{:S(2)}) copy-start(bf16[128,512]{1,0:T(8,128)(2,1)} %x_ref.3) | copy-start | bytes 393220
  0.9 0.7 copy-start.7
  9.3 18.2 %copy-start.2 = (bf16[64,512,16]{1,2,0:T(8,128)(2,1)S(1)}, bf16[64,512,16]{1,2,0:T(8,128)(2,1)}, u32[]{:S(2)}) copy-start(bf16[64,512,16]{1,2,0:T(8,128)(2,1)} %param.9) | copy-start | bytes 3145732
  9.3 37.7 %copy-start.3 = (bf16[64,16,512]{2,1,0:T(8,128)(2,1)S(1)}, bf16[64,16,512]{2,1,0:T(8,128)(2,1)}, u32[]{:S(2)}) copy-start(bf16[64,16,512]{2,1,0:T(8,128)(2,1)} %param.10) | copy-start | bytes 3145732
  9.3 14.1 %collective-permute-start = (bf16[8,128,512]{2,1,0:T(8,128)(2,1)}, bf16[8,128,512]{2,1,0:T(8,128)(2,1)S(1)}, u32[]{:S(2)}, u32[]{:S(2)}) collective-permute-start(bf16[8,128,512]{2,1,0:T(8,128)(2,1)} %product_theirs.1), channel_id=1, source_target_pairs={{0,1},{1,0},{2,3},{3,2},{4,5},{5,4},{6,7},{7,6},{8,9},{9,8},{10,11... | collective-permute-start | bytes 3145736 | tf_op jit(solution)/shard_map/ppermute | solution.py:266
  9.3 18.2 %all-to-all-start = ((bf16[16,16,640]{2,1,0:T(8,128)(2,1)}), bf16[16,16,640]{2,1,0:T(8,128)(2,1)S(1)}, u32[]{:S(2)}, u32[]{:S(2)}) async-start(bf16[16,16,640]{2,1,0:T(8,128)(2,1)} %bitcast.1), calls=%async_computation | async-start | bytes 655360 | tf_op jit(solution)/shard_map/all_to_all | solution.py:263
  16.5 56.3 %copy-start.8 = (s32[128]{0:T(128)S(1)}, s32[128]{0:T(128)}, u32[]{:S(2)}) copy-start(s32[128]{0:T(128)} %param.11) | copy-start | bytes 1540
  23.4 1.6 %copy-start = (f32[8,128,512]{2,1,0:T(8,128)S(1)}, f32[8,128,512]{2,1,0:T(8,128)}, u32[]{:S(2)}) copy-start(f32[8,128,512]{2,1,0:T(8,128)} %product_mine.1.mine_ref) | copy-start | bytes 6291460
  25.2 0.9 %copy-start.4 = (f32[3,128,512]{2,1,0:T(8,128)}, f32[3,128,512]{2,1,0:T(8,128)S(1)}, u32[]{:S(2)}) copy-start(f32[3,128,512]{2,1,0:T(8,128)S(1)} %get-tuple-element.18.keep_ref) | copy-start | bytes 2359300
  26.1 0.8 %copy-start.9 = (bf16[3,128,512]{2,1,0:T(8,128)(2,1)}, bf16[3,128,512]{2,1,0:T(8,128)(2,1)S(1)}, u32[]{:S(2)}) copy-start(bf16[3,128,512]{2,1,0:T(8,128)(2,1)S(1)} %get-tuple-element.19) | copy-start | bytes 1179652
  26.8 0.7 copy-start.10
  28.8 18.2 %all-to-all-start.1 = ((f32[16,16,256]{2,1,0:T(8,128)}), f32[16,16,256]{2,1,0:T(8,128)S(1)}, u32[]{:S(2)}, u32[]{:S(2)}) async-start(f32[16,16,256]{2,1,0:T(8,128)} %shrink.1), calls=%async_computation.1 | async-start | bytes 524288 | tf_op jit(solution)/shard_map/all_to_all | solution.py:275
  37.3 18.1 %collective-permute-start.1 = (bf16[3,128,512]{2,1,0:T(8,128)(2,1)}, bf16[3,128,512]{2,1,0:T(8,128)(2,1)S(1)}, u32[]{:S(2)}, u32[]{:S(2)}) collective-permute-start(bf16[3,128,512]{2,1,0:T(8,128)(2,1)} %copy-done.9), channel_id=1, source_target_pairs={{0,2},{1,3},{2,4},{3,5},{4,6},{5,7},{6,8},{7,9},{8,10},{9,11},{10,... | collective-permute-start | bytes 1179656 | tf_op jit(solution)/shard_map/ppermute | solution.py:257
  38.8 16.7 %collective-permute-start.2 = (bf16[2,128,512]{2,1,0:T(8,128)(2,1)}, bf16[2,128,512]{2,1,0:T(8,128)(2,1)S(1)}, u32[]{:S(2)}, u32[]{:S(2)}) collective-permute-start(bf16[2,128,512]{2,1,0:T(8,128)(2,1)} %copy-done.10), channel_id=1, source_target_pairs={{0,14},{1,15},{2,0},{3,1},{4,2},{5,3},{6,4},{7,5},{8,6},{9,7},{10,... | collective-permute-start | bytes 786440 | tf_op jit(solution)/shard_map/ppermute | solution.py:257
  48.3 24.5 %all-to-all-start.2 = ((bf16[16,16,512]{2,1,0:T(8,128)(2,1)}), bf16[16,16,512]{2,1,0:T(8,128)(2,1)S(1)}, u32[]{:S(2)}, u32[]{:S(2)}) async-start(bf16[16,16,512]{2,1,0:T(8,128)(2,1)} %bitcast.8), calls=%async_computation.2 | async-start | bytes 524288 | tf_op jit(solution)/shard_map/all_to_all | solution.py:280
  55.5 1.1 %copy-start.5 = (f32[3,128,512]{2,1,0:T(8,128)S(1)}, f32[3,128,512]{2,1,0:T(8,128)}, u32[]{:S(2)}) copy-start(f32[3,128,512]{2,1,0:T(8,128)} %copy-done.4) | copy-start | bytes 2359300
  56.7 13.7 %collective-permute-start.3 = (bf16[128,512]{1,0:T(8,128)(2,1)S(1)}, bf16[128,512]{1,0:T(8,128)(2,1)S(1)}, u32[]{:S(2)}, u32[]{:S(2)}) collective-permute-start(bf16[128,512]{1,0:T(8,128)(2,1)S(1)} %get-tuple-element.22), channel_id=1, source_target_pairs={{0,6},{1,7},{2,8},{3,9},{4,10},{5,11},{6,12},{7,13},{8,14},{9,15},... | collective-permute-start | bytes 393224 | tf_op jit(solution)/shard_map/ppermute | solution.py:257
  59.3 13.5 %collective-permute-start.4 = (bf16[128,512]{1,0:T(8,128)(2,1)S(1)}, bf16[128,512]{1,0:T(8,128)(2,1)S(1)}, u32[]{:S(2)}, u32[]{:S(2)}) collective-permute-start(bf16[128,512]{1,0:T(8,128)(2,1)S(1)} %get-tuple-element.23), channel_id=1, source_target_pairs={{0,10},{1,11},{2,12},{3,13},{4,14},{5,15},{6,0},{7,1},{8,2},{9,3},... | collective-permute-start | bytes 393224 | tf_op jit(solution)/shard_map/ppermute | solution.py:257
  72.8 0.9 %copy-start.6 = (bf16[128,512]{1,0:T(8,128)(2,1)S(1)}, bf16[128,512]{1,0:T(8,128)(2,1)}, u32[]{:S(2)}) copy-start(bf16[128,512]{1,0:T(8,128)(2,1)} %residual_ref.1) | copy-start | bytes 393220

commit v2 on v1

v2 whole, which is shorter than its diff:
```python
import functools

import jax
import jax.numpy as jnp
from jax import lax
from jax.experimental import pallas as pl
from jax.experimental.pallas import tpu as pltpu
from jax.sharding import PartitionSpec as P

BF16 = jnp.bfloat16
F32 = jnp.float32
LANES = 128
RIGHT = (1, -2)
LEFT = (-1, 2)
KEEP = (0, 3, -3)
PIECES = 8
GRANT = pltpu.CompilerParams(vmem_limit_bytes=16 * 2**20)
WHOLE = pltpu.CompilerParams(vmem_limit_bytes=60 * 2**20)


def vmem_specs(count):
    return [pl.BlockSpec(memory_space=pltpu.VMEM)] * count


def slots_of(index_row, owned, capacity):
    rows = index_row.shape[1]
    owner = index_row // owned
    owner_across = jnp.broadcast_to(owner, (rows, rows))
    owner_down = owner_across.T
    earlier = lax.broadcasted_iota(jnp.int32, (rows, rows), 0) < lax.broadcasted_iota(
        jnp.int32, (rows, rows), 1
    )
    same = jnp.where((owner_down == owner_across) & earlier, 1, 0)
    rank = jnp.sum(same, axis=0, keepdims=True)
    return owner * capacity + rank


def dispatch_kernel(owned, capacity, index_ref, x_ref, out_ref):
    index_row = index_ref[...]
    rows, width = x_ref.shape
    slot_count = out_ref.shape[0]
    slot = slots_of(index_row, owned, capacity)
    placing = lax.broadcasted_iota(jnp.int32, (slot_count, rows), 0) == slot
    out_ref[:, :width] = jnp.dot(
        jnp.where(placing, 1.0, 0.0).astype(BF16), x_ref[...], preferred_element_type=F32
    ).astype(BF16)
    number = (index_row % owned + 1).astype(F32)
    asked = jnp.sum(jnp.where(placing, number, 0.0), axis=1, keepdims=True)
    out_ref[:, width:] = jnp.broadcast_to(asked, (slot_count, LANES)).astype(BF16)


def dispatch(index_row, x, owned, capacity, slot_count):
    rows, width = x.shape
    return pl.pallas_call(
        functools.partial(dispatch_kernel, owned, capacity),
        out_shape=jax.ShapeDtypeStruct((slot_count, width + LANES), BF16),
        in_specs=vmem_specs(2),
        out_specs=pl.BlockSpec(memory_space=pltpu.VMEM),
        cost_estimate=pl.CostEstimate(
            flops=2 * slot_count * rows * width, bytes_accessed=2 * slot_count * width, transcendentals=0
        ),
        compiler_params=WHOLE,
        name="dispatch",
    )(index_row, x)


def product_kernel(
    core_ref, x_ref, w_hbm, theirs_hbm, mine_hbm, w_ref, theirs_ref, mine_ref, in_sems, theirs_sems, mine_sems
):
    first = core_ref[0] == 0
    chips, _, block = mine_ref.shape
    depth = w_ref.shape[0] // PIECES
    loads = []
    for piece in range(PIECES):
        part = slice(piece * depth, (piece + 1) * depth)
        loads.append(pltpu.make_async_copy(w_hbm.at[part], w_ref.at[part], in_sems.at[piece]))
        loads[piece].start()
    for load in loads:
        load.wait()
    stores = []
    for z in range(chips):
        both = jnp.dot(
            x_ref[...], w_ref[:, 2 * z * block : 2 * (z + 1) * block], preferred_element_type=F32
        )
        low, high = both[:, :block], both[:, block:]
        theirs_ref[z] = jnp.where(first, high, low).astype(BF16)
        mine_ref[z] = jnp.where(first, low, high)
        for ref, hbm, sems in ((theirs_ref, theirs_hbm, theirs_sems), (mine_ref, mine_hbm, mine_sems)):
            stores.append(pltpu.make_async_copy(ref.at[z], hbm.at[z], sems.at[z]))
            stores[-1].start()
    for store in stores:
        store.wait()


def product(core, x, w, chips):
    rows, depth = x.shape
    block = w.shape[1] // (2 * chips)
    return pl.pallas_call(
        product_kernel,
        out_shape=(
            jax.ShapeDtypeStruct((chips, rows, block), BF16),
            jax.ShapeDtypeStruct((chips, rows, block), F32),
        ),
        in_specs=[
            pl.BlockSpec(memory_space=pltpu.SMEM),
            pl.BlockSpec(memory_space=pltpu.VMEM),
            pl.BlockSpec(memory_space=pl.ANY),
        ],
        out_specs=(pl.BlockSpec(memory_space=pl.ANY), pl.BlockSpec(memory_space=pl.ANY)),
        scratch_shapes=[
            pltpu.VMEM(w.shape, BF16),
            pltpu.VMEM((chips, rows, block), BF16),
            pltpu.VMEM((chips, rows, block), F32),
            pltpu.SemaphoreType.DMA((PIECES,)),
            pltpu.SemaphoreType.DMA((chips,)),
            pltpu.SemaphoreType.DMA((chips,)),
        ],
        cost_estimate=pl.CostEstimate(
            flops=2 * rows * w.size, bytes_accessed=2 * w.size, transcendentals=0
        ),
        compiler_params=WHOLE,
        name="product",
    )(core, x, w)


def pair_kernel(chips, z_ref, mine_ref, other_ref, right_ref, left_ref, keep_ref):
    z = z_ref[0]
    rows = keep_ref.shape[1]
    half = rows // 2

    def total(step, first, last):
        at = lax.rem(z + (step + chips), chips)
        return mine_ref[at, first:last] + other_ref[at, first:last].astype(F32)

    for ref, steps, first in ((right_ref, RIGHT, 0), (left_ref, LEFT, half)):
        for place, step in enumerate(steps):
            ref[place * rows : (place + 1) * rows] = total(step, 0, rows).astype(BF16)
        ref[len(steps) * rows :] = total(chips // 2, first, first + half).astype(BF16)
    for place, step in enumerate(KEEP):
        keep_ref[place] = total(step, 0, rows)


def pair_sum(z, mine, other):
    chips, rows, block = mine.shape
    sent = len(RIGHT) * rows + rows // 2
    return pl.pallas_call(
        functools.partial(pair_kernel, chips),
        out_shape=(
            jax.ShapeDtypeStruct((sent, block), BF16),
            jax.ShapeDtypeStruct((sent, block), BF16),
            jax.ShapeDtypeStruct((len(KEEP), rows, block), F32),
        ),
        in_specs=[pl.BlockSpec(memory_space=pltpu.SMEM)] + vmem_specs(2),
        out_specs=tuple(vmem_specs(3)),
        cost_estimate=pl.CostEstimate(flops=mine.size, bytes_accessed=8 * mine.size, transcendentals=0),
        compiler_params=GRANT,
        name="pair_sum",
    )(z, mine, other)


def relay_kernel(residual_ref, keep_ref, right_ref, left_ref, here_ref, far_right_ref, far_left_ref):
    rows = here_ref.shape[0]
    half = rows // 2

    def part(ref, place, first, last):
        return ref[place * rows + first : place * rows + last].astype(F32)

    here_ref[...] = (
        residual_ref[...].astype(F32)
        + keep_ref[0]
        + part(right_ref, 0, 0, rows)
        + part(left_ref, 0, 0, rows)
    )
    for first, last in ((0, half), (half, rows)):
        right = keep_ref[1, first:last] + part(left_ref, 1, first, last)
        left = keep_ref[2, first:last] + part(right_ref, 1, first, last)
        if first == 0:
            right += part(right_ref, 2, 0, half)
        else:
            left += part(left_ref, 2, 0, half)
        far_right_ref[first:last] = right.astype(BF16)
        far_left_ref[first:last] = left.astype(BF16)


def relay(residual, keep, right, left):
    _, rows, block = keep.shape
    return pl.pallas_call(
        relay_kernel,
        out_shape=(
            jax.ShapeDtypeStruct((rows, block), F32),
            jax.ShapeDtypeStruct((rows, block), BF16),
            jax.ShapeDtypeStruct((rows, block), BF16),
        ),
        in_specs=vmem_specs(4),
        out_specs=tuple(vmem_specs(3)),
        cost_estimate=pl.CostEstimate(flops=5 * rows * block, bytes_accessed=4 * keep.size, transcendentals=0),
        compiler_params=GRANT,
        name="relay",
    )(residual, keep, right, left)


def wanted_row(slots_ref, width):
    tags = slots_ref[:, width:].astype(F32)
    return tags.T[0:1, :]


def shrink_kernel(owned, slots_ref, down_ref, out_ref):
    slot_total = slots_ref.shape[0]
    width = down_ref.shape[1]
    rank = down_ref.shape[0] // owned
    terms = lax.dot_general(
        down_ref[...], slots_ref[:, :width], (((1,), (1,)), ((), ())), preferred_element_type=F32
    )
    wanted = wanted_row(slots_ref, width)
    total = jnp.zeros((rank, slot_total), F32)
    for adapter in range(owned):
        total += jnp.where(wanted == adapter + 1, terms[adapter * rank : (adapter + 1) * rank], 0.0)
    out_ref[...] = total


def shrink_terms(slots, down, owned):
    slot_total = slots.shape[0]
    rank = down.shape[0] // owned
    return pl.pallas_call(
        functools.partial(shrink_kernel, owned),
        out_shape=jax.ShapeDtypeStruct((rank, slot_total), F32),
        in_specs=vmem_specs(2),
        out_specs=pl.BlockSpec(memory_space=pltpu.VMEM),
        cost_estimate=pl.CostEstimate(
            flops=2 * slot_total * down.size, bytes_accessed=2 * down.size, transcendentals=0
        ),
        compiler_params=GRANT,
        name="shrink",
    )(slots, down)


def expand_kernel(owned, three_ref, right_ref, left_ref, slots_ref, up_ref, out_ref):
    total = three_ref[...] + right_ref[...] + left_ref[...]
    shrink = total.astype(BF16).astype(F32)
    wanted = wanted_row(slots_ref, slots_ref.shape[1] - LANES)
    spread = jnp.concatenate(
        [jnp.where(wanted == adapter + 1, shrink, 0.0).astype(BF16) for adapter in range(owned)], axis=0
    )
    out_ref[...] = lax.dot_general(
        spread, up_ref[...], (((0,), (0,)), ((), ())), preferred_element_type=F32
    ).astype(BF16)


def expand_rows(three, right, left, slots, up, owned):
    slot_total = slots.shape[0]
    return pl.pallas_call(
        functools.partial(expand_kernel, owned),
        out_shape=jax.ShapeDtypeStruct((slot_total, up.shape[1]), BF16),
        in_specs=vmem_specs(5),
        out_specs=pl.BlockSpec(memory_space=pltpu.VMEM),
        cost_estimate=pl.CostEstimate(
            flops=2 * slot_total * up.size, bytes_accessed=2 * up.size, transcendentals=0
        ),
        compiler_params=GRANT,
        name="expand",
    )(three, right, left, slots, up)


def finish_kernel(
    owned, capacity, index_ref, here_ref, right_ref, left_ref, returned_ref, out_ref
):
    rows = here_ref.shape[0]
    slot_count = returned_ref.shape[0]
    slot = slots_of(index_ref[...], owned, capacity)
    placing = lax.broadcasted_iota(jnp.int32, (slot_count, rows), 0) == slot
    branch = lax.dot_general(
        jnp.where(placing, 1.0, 0.0).astype(BF16),
        returned_ref[...],
        (((0,), (0,)), ((), ())),
        preferred_element_type=F32,
    )
    base = here_ref[...] + right_ref[...].astype(F32) + left_ref[...].astype(F32)
    out_ref[...] = (base + branch).astype(BF16)


def finish(index_row, sums, returned, owned, capacity):
    return pl.pallas_call(
        functools.partial(finish_kernel, owned, capacity),
        out_shape=jax.ShapeDtypeStruct(sums[0].shape, BF16),
        in_specs=vmem_specs(5),
        out_specs=pl.BlockSpec(memory_space=pltpu.VMEM),
        cost_estimate=pl.CostEstimate(
            flops=2 * returned.size * sums[0].shape[0], bytes_accessed=8 * sums[0].size, transcendentals=0
        ),
        compiler_params=GRANT,
        name="finish",
    )(index_row, *sums, returned)


def body(attention_output, residual, output_weight, down_factors, up_factors, adapter_index):
    rows, width = attention_output.shape
    owned, _, rank = down_factors.shape
    columns = up_factors.shape[2]
    groups = lax.axis_size("dp")
    shards = lax.axis_size("tensor")
    chips = shards // 2
    capacity = 2 * rows // groups
    slot_count = groups * capacity
    place = lax.axis_index("tensor")
    z, core = (place >> 1).reshape(1), (place & 1).reshape(1)
    siblings = [(i, i ^ 1) for i in range(shards)]

    def along_z(array, step):
        return lax.ppermute(array, "tensor", [(i, (i + 2 * step) % shards) for i in range(shards)])

    index_row = adapter_index.reshape(1, rows)
    outgoing = dispatch(index_row, attention_output, owned, capacity, slot_count)
    outgoing, x = lax.optimization_barrier((outgoing, attention_output))
    outgoing = outgoing.reshape(groups, capacity, width + LANES)
    slots = lax.all_to_all(outgoing, "dp", split_axis=0, concat_axis=0, tiled=True)

    theirs, mine = product(core, x, output_weight, chips)
    slots, theirs, mine = lax.optimization_barrier((slots, theirs, mine))
    other = lax.ppermute(theirs, "tensor", siblings)

    slots = slots.reshape(slot_count, width + LANES)
    down = down_factors.transpose(0, 2, 1).reshape(owned * rank, width)
    shrink = shrink_terms(slots, down, owned)
    both = shrink + lax.ppermute(shrink, "tensor", siblings)
    two = both + along_z(both, 1)
    three = two + along_z(both, -1)
    three_left, two_right = along_z(three, 3), along_z(two, -3)

    to_right, to_left, keep = pair_sum(z, mine, other)
    from_left, from_right = along_z(to_right, 1), along_z(to_left, -1)
    here, far_right, far_left = relay(residual, keep, from_left, from_right)
    sums = (here, along_z(far_right, 3), along_z(far_left, -3))
    up = up_factors.reshape(owned * rank, columns)
    expand = expand_rows(three, three_left, two_right, slots, up, owned)
    expand = expand.reshape(groups, capacity, columns)
    returned = lax.all_to_all(expand, "dp", split_axis=0, concat_axis=0, tiled=True)
    returned = returned.reshape(slot_count, columns)
    return finish(index_row, sums, returned, owned, capacity)


def solution(mesh):
    return jax.shard_map(
        body,
        mesh=mesh,
        in_specs=(
            P("dp", "tensor"),
            P("dp", "tensor"),
            P("tensor", None),
            P("dp", "tensor", None),
            P("dp", None, "tensor"),
            P("dp"),
        ),
        out_specs=P("dp", "tensor"),
        check_vma=False,
    )
```

time: 75.9 us -> 64.8 us (0.85)
  Pallas kernels: 18.4 us -> 12.7 us
  local copies, waits for them, and re-layouts: 7.55 us -> 2.5 us
  waiting for transfers between devices: 18.6 us -> 20.1 us
  starting transfers between devices: 30.1 us -> 28.8 us
    ppermute x4 -> x8, starting transfers between devices: 7.14 us -> 16.4 us  [along_z(): lax.ppermute(array, 'tensor', [(i, (i + 2 * step) % shards) for i in rang...]
    all_to_all x1 -> x0, starting transfers between devices: 8.59 us -> none  [body(): lax.all_to_all(parts, 'tensor', split_axis=0, concat_axis=0, tiled=True)]
    pallas_call x3 -> x2, Pallas kernels: 14.8 us -> 7.05 us  [the longest x1 6.59 us: product(): pl.pallas_call(product_kernel, out_shape=(jax.ShapeDtypeStruct((chips, ro...]
    all_to_all x1 -> x0, waiting for transfers between devices: 7.62 us -> none  [body(): lax.all_to_all(parts, 'tensor', split_axis=0, concat_axis=0, tiled=True)]
    unnamed x22 -> x10, local copies, waits for them, and re-layouts: 7.55 us -> 2.5 us
    ppermute x4 -> x8, waiting for transfers between devices: 10.9 us -> 13.6 us  [along_z(): lax.ppermute(array, 'tensor', [(i, (i + 2 * step) % shards) for i in rang...]
    all_to_all x1, waiting for transfers between devices: 0.01 us -> 2.55 us  [body(): lax.all_to_all(outgoing, 'dp', split_axis=0, concat_axis=0, tiled=True)]
    all_to_all x1, starting transfers between devices: 7.21 us -> 4.77 us  [body(): lax.all_to_all(expand, 'dp', split_axis=0, concat_axis=0, tiled=True)]
  transfers between devices with their start and end apart: 8 -> 12, of which waited for: 3 -> 6; matrix products, arithmetic and copies ran while one was open for 0% -> 0% of each run, Pallas kernels for 11% -> 15%
where the time goes in v2:
time: 64.8 us; the launch traced here: 64.1 us
  starting transfers between devices  28.8 us (44%)
  waiting for transfers between devices  20.1 us (31%)
  Pallas kernels  12.7 us (20%)
  local copies, waits for them, and re-layouts  2.5 us (4%)
    ppermute x8, starting transfers between devices, along_z(): lax.ppermute(array, 'tensor', [(i, (i + 2 * step) % shards) for i in rang...  16.4 us
    ppermute x8, waiting for transfers between devices, along_z(): lax.ppermute(array, 'tensor', [(i, (i + 2 * step) % shards) for i in rang...  13.6 us
    all_to_all x1, starting transfers between devices, body(): lax.all_to_all(outgoing, 'dp', split_axis=0, concat_axis=0, tiled=True)  7.03 us
    pallas_call x1, Pallas kernels, product(): pl.pallas_call(product_kernel, out_shape=(jax.ShapeDtypeStruct((chips, ro...  6.59 us
    all_to_all x1, starting transfers between devices, body(): lax.all_to_all(expand, 'dp', split_axis=0, concat_axis=0, tiled=True)  4.77 us
    all_to_all x1, waiting for transfers between devices, body(): lax.all_to_all(outgoing, 'dp', split_axis=0, concat_axis=0, tiled=True)  2.55 us
    unnamed x10, local copies, waits for them, and re-layouts  2.5 us
    all_to_all x1, waiting for transfers between devices, body(): lax.all_to_all(expand, 'dp', split_axis=0, concat_axis=0, tiled=True)  2.31 us
  transfers between devices with their start and end apart: 12, of which 6 were waited for; matrix products, arithmetic and copies ran while one was open for 0% of the time, Pallas kernels for 15%

profile of v2, /device:TPU:32, one launch (start us, length us, event | category | flops | bytes accessed | tf_op | source)
XLA Modules:
  0.0 64.1 jit_solution(646433072482888495)
XLA Ops:
  0.0 2.1 %dispatch.1 = bf16[256,640]{1,0:T(8,128)(2,1)} custom-call(s32[1,128]{1,0:T(1,128)} %bitcast.16, bf16[128,512]{1,0:T(8,128)(2,1)} %x_ref.2), custom_call_target="tpu_custom_call" | custom-call | flops 33554432 | bytes 262144 | tf_op jit(solution)/shard_map/dispatch/pallas_call | solution.py:54
  2.1 7.0 %all-to-all-start = ((bf16[16,16,640]{2,1,0:T(8,128)(2,1)}), bf16[16,16,640]{2,1,0:T(8,128)(2,1)S(1)}, u32[]{:S(2)}, u32[]{:S(2)}) async-start(bf16[16,16,640]{2,1,0:T(8,128)(2,1)} %bitcast.18), calls=%async_computation | async-start | bytes 655360 | tf_op jit(solution)/shard_map/all_to_all | solution.py:315
  9.2 0.0 copy-start.4
  9.2 6.6 %product.1 = (bf16[8,128,512]{2,1,0:T(8,128)(2,1)}, f32[8,128,512]{2,1,0:T(8,128)}) custom-call(s32[1]{0:T(128)} %bitcast.3.core_ref, bf16[128,512]{1,0:T(8,128)(2,1)} %x_ref.2, bf16[512,8192]{1,0:T(8,128)(2,1)} %w_hbm.1), custom_call_target="tpu_custom_call" | custom-call | flops 1073741824 | bytes 8388608 | tf_op jit(solution)/shard_map/product/pallas_call | solution.py:98
  15.8 2.5 %all-to-all-done = bf16[16,16,640]{2,1,0:T(8,128)(2,1)S(1)} async-done(((bf16[16,16,640]{2,1,0:T(8,128)(2,1)}), bf16[16,16,640]{2,1,0:T(8,128)(2,1)S(1)}, u32[]{:S(2)}, u32[]{:S(2)}) %all-to-all-start) | async-done | bytes 327712 | tf_op jit(solution)/shard_map/all_to_all | solution.py:315
  18.3 0.5 shrink.1
  18.8 0.6 collective-permute-start.5
  19.4 1.6 %collective-permute-done.5 = f32[16,256]{1,0:T(8,128)S(1)} collective-permute-done((f32[16,256]{1,0:T(8,128)S(1)}, f32[16,256]{1,0:T(8,128)S(1)}, u32[]{:S(2)}, u32[]{:S(2)}) %collective-permute-start.5) | collective-permute-done | bytes 16416 | tf_op jit(solution)/shard_map/ppermute | solution.py:324
  21.0 0.1 collective-permute-start.7
  21.1 1.9 %collective-permute-start.6 = (f32[16,256]{1,0:T(8,128)S(1)}, f32[16,256]{1,0:T(8,128)S(1)}, u32[]{:S(2)}, u32[]{:S(2)}) collective-permute-start(f32[16,256]{1,0:T(8,128)S(1)} %add.9), channel_id=1, source_target_pairs={{0,2},{1,3},{2,4},{3,5},{4,6},{5,7},{6,8},{7,9},{8,10},{9,11},{10,... | collective-permute-start | bytes 49160 | tf_op jit(solution)/shard_map/ppermute | solution.py:309
  23.1 0.0 collective-permute-done.other_ref
  23.1 1.6 %copy-done = f32[8,128,512]{2,1,0:T(8,128)S(1)} copy-done((f32[8,128,512]{2,1,0:T(8,128)S(1)}, f32[8,128,512]{2,1,0:T(8,128)}, u32[]{:S(2)}) %copy-start) | copy-done | bytes 2097176
  24.6 1.1 %pair_sum.1 = (bf16[320,512]{1,0:T(8,128)(2,1)}, bf16[320,512]{1,0:T(8,128)(2,1)}, f32[3,128,512]{2,1,0:T(8,128)S(1)}) custom-call(s32[1]{0:T(128)} %bitcast.1.z_ref, f32[8,128,512]{2,1,0:T(8,128)S(1)} %copy-done, bf16[8,128,512]{2,1,0:T(8,128)(2,1)S(1)} %collective-permute-done.other_ref), custom_call_target="tpu_custom_call" | custom-call | flops 524288 | bytes 4194304 | tf_op jit(solution)/shard_map/pair_sum/pallas_call | solution.py:146
  25.8 1.9 %collective-permute-start.1 = (bf16[320,512]{1,0:T(8,128)(2,1)}, bf16[320,512]{1,0:T(8,128)(2,1)S(1)}, u32[]{:S(2)}, u32[]{:S(2)}) collective-permute-start(bf16[320,512]{1,0:T(8,128)(2,1)} %get-tuple-element.25), channel_id=1, source_target_pairs={{0,2},{1,3},{2,4},{3,5},{4,6},{5,7},{6,8},{7,9},{8,10},{9,11},{10,... | collective-permute-start | bytes 983048 | tf_op jit(solution)/shard_map/ppermute | solution.py:309
  27.7 2.0 %collective-permute-start.2 = (bf16[320,512]{1,0:T(8,128)(2,1)}, bf16[320,512]{1,0:T(8,128)(2,1)S(1)}, u32[]{:S(2)}, u32[]{:S(2)}) collective-permute-start(bf16[320,512]{1,0:T(8,128)(2,1)} %get-tuple-element.26), channel_id=1, source_target_pairs={{0,14},{1,15},{2,0},{3,1},{4,2},{5,3},{6,4},{7,5},{8,6},{9,7},{10,... | collective-permute-start | bytes 983048 | tf_op jit(solution)/shard_map/ppermute | solution.py:309
  29.7 4.2 %collective-permute-start.9 = (f32[16,256]{1,0:T(8,128)S(1)}, f32[16,256]{1,0:T(8,128)S(1)}, u32[]{:S(2)}, u32[]{:S(2)}) collective-permute-start(f32[16,256]{1,0:T(8,128)S(1)} %get-tuple-element.32), channel_id=1, source_target_pairs={{0,10},{1,11},{2,12},{3,13},{4,14},{5,15},{6,0},{7,1},{8,2},{9,3},... | collective-permute-start | bytes 49160 | tf_op jit(solution)/shard_map/ppermute | solution.py:309
  33.9 1.1 %collective-permute-start.8 = (f32[16,256]{1,0:T(8,128)S(1)}, f32[16,256]{1,0:T(8,128)S(1)}, u32[]{:S(2)}, u32[]{:S(2)}) collective-permute-start(f32[16,256]{1,0:T(8,128)S(1)} %get-tuple-element.31.three_ref), channel_id=1, source_target_pairs={{0,6},{1,7},{2,8},{3,9},{4,10},{5,11},{6,12},{7,13},{8,14},{9,15},... | collective-permute-start | bytes 49160 | tf_op jit(solution)/shard_map/ppermute | solution.py:309
  35.0 8.0 %collective-permute-done.9.left_ref = f32[16,256]{1,0:T(8,128)S(1)} collective-permute-done((f32[16,256]{1,0:T(8,128)S(1)}, f32[16,256]{1,0:T(8,128)S(1)}, u32[]{:S(2)}, u32[]{:S(2)}) %collective-permute-start.9) | collective-permute-done | bytes 16416 | tf_op jit(solution)/shard_map/ppermute | solution.py:309
  43.0 0.0 collective-permute-done.8.right_ref
  43.0 1.3 %expand.1 = bf16[256,512]{1,0:T(8,128)(2,1)} custom-call(f32[16,256]{1,0:T(8,128)S(1)} %get-tuple-element.31.three_ref, f32[16,256]{1,0:T(8,128)S(1)} %collective-permute-done.8.right_ref, f32[16,256]{1,0:T(8,128)S(1)} %collective-permute-done.9.left_ref, bf16[256,640]{1,0:T(8,128)(2,1)S(1)} %bitcast.12, bf16[1024,512]{1,0:T(8,128)(2,1)S(1)} %bitcast.15), custom_call_target="tpu_custom_call" | custom-call | flops 268435456 | bytes 1048576 | tf_op jit(solution)/shard_map/expand/pallas_call | solution.py:251
  44.3 4.8 %all-to-all-start.1 = ((bf16[16,16,512]{2,1,0:T(8,128)(2,1)}), bf16[16,16,512]{2,1,0:T(8,128)(2,1)S(1)}, u32[]{:S(2)}, u32[]{:S(2)}) async-start(bf16[16,16,512]{2,1,0:T(8,128)(2,1)} %bitcast.8), calls=%async_computation.1 | async-start | bytes 524288 | tf_op jit(solution)/shard_map/all_to_all | solution.py:336
  49.0 0.0 collective-permute-done.1.right_ref
  49.0 0.0 collective-permute-done.2.left_ref
  49.1 0.0 copy-start.3
  49.1 0.9 %copy-done.3 = bf16[128,512]{1,0:T(8,128)(2,1)S(1)} copy-done((bf16[128,512]{1,0:T(8,128)(2,1)S(1)}, bf16[128,512]{1,0:T(8,128)(2,1)}, u32[]{:S(2)}) %copy-start.3) | copy-done | bytes 131096
  50.0 0.1 relay.1
  50.1 1.8 %collective-permute-start.3 = (bf16[128,512]{1,0:T(8,128)(2,1)S(1)}, bf16[128,512]{1,0:T(8,128)(2,1)S(1)}, u32[]{:S(2)}, u32[]{:S(2)}) collective-permute-start(bf16[128,512]{1,0:T(8,128)(2,1)S(1)} %get-tuple-element.28), channel_id=1, source_target_pairs={{0,6},{1,7},{2,8},{3,9},{4,10},{5,11},{6,12},{7,13},{8,14},{9,15},... | collective-permute-start | bytes 393224 | tf_op jit(solution)/shard_map/ppermute | solution.py:309
  51.9 3.3 %collective-permute-start.4 = (bf16[128,512]{1,0:T(8,128)(2,1)S(1)}, bf16[128,512]{1,0:T(8,128)(2,1)S(1)}, u32[]{:S(2)}, u32[]{:S(2)}) collective-permute-start(bf16[128,512]{1,0:T(8,128)(2,1)S(1)} %get-tuple-element.29), channel_id=1, source_target_pairs={{0,10},{1,11},{2,12},{3,13},{4,14},{5,15},{6,0},{7,1},{8,2},{9,3},... | collective-permute-start | bytes 393224 | tf_op jit(solution)/shard_map/ppermute | solution.py:309
  55.2 2.3 %all-to-all-done.1 = bf16[16,16,512]{2,1,0:T(8,128)(2,1)S(1)} async-done(((bf16[16,16,512]{2,1,0:T(8,128)(2,1)}), bf16[16,16,512]{2,1,0:T(8,128)(2,1)S(1)}, u32[]{:S(2)}, u32[]{:S(2)}) %all-to-all-start.1) | async-done | bytes 262176 | tf_op jit(solution)/shard_map/all_to_all | solution.py:336
  57.5 2.6 %collective-permute-done.3.right_ref = bf16[128,512]{1,0:T(8,128)(2,1)S(1)} collective-permute-done((bf16[128,512]{1,0:T(8,128)(2,1)S(1)}, bf16[128,512]{1,0:T(8,128)(2,1)S(1)}, u32[]{:S(2)}, u32[]{:S(2)}) %collective-permute-start.3) | collective-permute-done | bytes 131104 | tf_op jit(solution)/shard_map/ppermute | solution.py:309
  60.2 3.0 %collective-permute-done.4.left_ref = bf16[128,512]{1,0:T(8,128)(2,1)S(1)} collective-permute-done((bf16[128,512]{1,0:T(8,128)(2,1)S(1)}, bf16[128,512]{1,0:T(8,128)(2,1)S(1)}, u32[]{:S(2)}, u32[]{:S(2)}) %collective-permute-start.4) | collective-permute-done | bytes 131104 | tf_op jit(solution)/shard_map/ppermute | solution.py:309
  63.1 1.0 %finish.1 = bf16[128,512]{1,0:T(8,128)(2,1)} custom-call(s32[1,128]{1,0:T(1,128)S(1)} %bitcast.17, f32[128,512]{1,0:T(8,128)S(1)} %get-tuple-element.27.here_ref, bf16[128,512]{1,0:T(8,128)(2,1)S(1)} %collective-permute-done.3.right_ref, bf16[128,512]{1,0:T(8,128)(2,1)S(1)} %collective-permute-done.4.left_ref, bf16[256,512]{1,0:T(8,128)(2,1)S(1)} %bitcast.13), custom_call_target="tpu_custom_call" | custom-call | flops 33554432 | bytes 524288 | tf_op jit(solution)/shard_map/finish/pallas_call | solution.py:282
  (11 shorter events, 0.0 us)
Async XLA Ops:
  0.0 18.3 %copy-start.1 = (bf16[64,512,16]{1,2,0:T(8,128)(2,1)S(1)}, bf16[64,512,16]{1,2,0:T(8,128)(2,1)}, u32[]{:S(2)}) copy-start(bf16[64,512,16]{1,2,0:T(8,128)(2,1)} %param.9) | copy-start | bytes 3145732
  0.0 43.0 %copy-start.2 = (bf16[64,16,512]{2,1,0:T(8,128)(2,1)S(1)}, bf16[64,16,512]{2,1,0:T(8,128)(2,1)}, u32[]{:S(2)}) copy-start(bf16[64,16,512]{2,1,0:T(8,128)(2,1)} %param.10) | copy-start | bytes 3145732
  2.1 16.2 %all-to-all-start = ((bf16[16,16,640]{2,1,0:T(8,128)(2,1)}), bf16[16,16,640]{2,1,0:T(8,128)(2,1)S(1)}, u32[]{:S(2)}, u32[]{:S(2)}) async-start(bf16[16,16,640]{2,1,0:T(8,128)(2,1)} %bitcast.18), calls=%async_computation | async-start | bytes 655360 | tf_op jit(solution)/shard_map/all_to_all | solution.py:315
  9.2 53.9 %copy-start.4 = (s32[128]{0:T(128)S(1)}, s32[128]{0:T(128)}, u32[]{:S(2)}) copy-start(s32[128]{0:T(128)} %param.11) | copy-start | bytes 1540
  18.3 4.7 %collective-permute-start = (bf16[8,128,512]{2,1,0:T(8,128)(2,1)}, bf16[8,128,512]{2,1,0:T(8,128)(2,1)S(1)}, u32[]{:S(2)}, u32[]{:S(2)}) collective-permute-start(bf16[8,128,512]{2,1,0:T(8,128)(2,1)} %get-tuple-element.23), channel_id=1, source_target_pairs={{0,1},{1,0},{2,3},{3,2},{4,5},{5,4},{6,7},{7,6},{8,9},{9,8},{10,11... | collective-permute-start | bytes 3145736 | tf_op jit(solution)/shard_map/ppermute | solution.py:319
  18.8 2.2 %collective-permute-start.5 = (f32[16,256]{1,0:T(8,128)S(1)}, f32[16,256]{1,0:T(8,128)S(1)}, u32[]{:S(2)}, u32[]{:S(2)}) collective-permute-start(f32[16,256]{1,0:T(8,128)S(1)} %shrink.1), channel_id=1, source_target_pairs={{0,1},{1,0},{2,3},{3,2},{4,5},{5,4},{6,7},{7,6},{8,9},{9,8},{10,11... | collective-permute-start | bytes 49160 | tf_op jit(solution)/shard_map/ppermute | solution.py:324
  21.0 8.7 %collective-permute-start.7 = (f32[16,256]{1,0:T(8,128)S(1)}, f32[16,256]{1,0:T(8,128)S(1)}, u32[]{:S(2)}, u32[]{:S(2)}) collective-permute-start(f32[16,256]{1,0:T(8,128)S(1)} %add.9), channel_id=1, source_target_pairs={{0,14},{1,15},{2,0},{3,1},{4,2},{5,3},{6,4},{7,5},{8,6},{9,7},{10,... | collective-permute-start | bytes 49160 | tf_op jit(solution)/shard_map/ppermute | solution.py:309
  21.1 8.6 %collective-permute-start.6 = (f32[16,256]{1,0:T(8,128)S(1)}, f32[16,256]{1,0:T(8,128)S(1)}, u32[]{:S(2)}, u32[]{:S(2)}) collective-permute-start(f32[16,256]{1,0:T(8,128)S(1)} %add.9), channel_id=1, source_target_pairs={{0,2},{1,3},{2,4},{3,5},{4,6},{5,7},{6,8},{7,9},{8,10},{9,11},{10,... | collective-permute-start | bytes 49160 | tf_op jit(solution)/shard_map/ppermute | solution.py:309
  23.1 1.6 %copy-start = (f32[8,128,512]{2,1,0:T(8,128)S(1)}, f32[8,128,512]{2,1,0:T(8,128)}, u32[]{:S(2)}) copy-start(f32[8,128,512]{2,1,0:T(8,128)} %get-tuple-element.22.mine_ref) | copy-start | bytes 6291460
  25.8 23.3 %collective-permute-start.1 = (bf16[320,512]{1,0:T(8,128)(2,1)}, bf16[320,512]{1,0:T(8,128)(2,1)S(1)}, u32[]{:S(2)}, u32[]{:S(2)}) collective-permute-start(bf16[320,512]{1,0:T(8,128)(2,1)} %get-tuple-element.25), channel_id=1, source_target_pairs={{0,2},{1,3},{2,4},{3,5},{4,6},{5,7},{6,8},{7,9},{8,10},{9,11},{10,... | collective-permute-start | bytes 983048 | tf_op jit(solution)/shard_map/ppermute | solution.py:309
  27.7 21.4 %collective-permute-start.2 = (bf16[320,512]{1,0:T(8,128)(2,1)}, bf16[320,512]{1,0:T(8,128)(2,1)S(1)}, u32[]{:S(2)}, u32[]{:S(2)}) collective-permute-start(bf16[320,512]{1,0:T(8,128)(2,1)} %get-tuple-element.26), channel_id=1, source_target_pairs={{0,14},{1,15},{2,0},{3,1},{4,2},{5,3},{6,4},{7,5},{8,6},{9,7},{10,... | collective-permute-start | bytes 983048 | tf_op jit(solution)/shard_map/ppermute | solution.py:309
  29.7 13.3 %collective-permute-start.9 = (f32[16,256]{1,0:T(8,128)S(1)}, f32[16,256]{1,0:T(8,128)S(1)}, u32[]{:S(2)}, u32[]{:S(2)}) collective-permute-start(f32[16,256]{1,0:T(8,128)S(1)} %get-tuple-element.32), channel_id=1, source_target_pairs={{0,10},{1,11},{2,12},{3,13},{4,14},{5,15},{6,0},{7,1},{8,2},{9,3},... | collective-permute-start | bytes 49160 | tf_op jit(solution)/shard_map/ppermute | solution.py:309
  33.9 9.0 %collective-permute-start.8 = (f32[16,256]{1,0:T(8,128)S(1)}, f32[16,256]{1,0:T(8,128)S(1)}, u32[]{:S(2)}, u32[]{:S(2)}) collective-permute-start(f32[16,256]{1,0:T(8,128)S(1)} %get-tuple-element.31.three_ref), channel_id=1, source_target_pairs={{0,6},{1,7},{2,8},{3,9},{4,10},{5,11},{6,12},{7,13},{8,14},{9,15},... | collective-permute-start | bytes 49160 | tf_op jit(solution)/shard_map/ppermute | solution.py:309
  44.3 13.2 %all-to-all-start.1 = ((bf16[16,16,512]{2,1,0:T(8,128)(2,1)}), bf16[16,16,512]{2,1,0:T(8,128)(2,1)S(1)}, u32[]{:S(2)}, u32[]{:S(2)}) async-start(bf16[16,16,512]{2,1,0:T(8,128)(2,1)} %bitcast.8), calls=%async_computation.1 | async-start | bytes 524288 | tf_op jit(solution)/shard_map/all_to_all | solution.py:336
  49.1 0.9 %copy-start.3 = (bf16[128,512]{1,0:T(8,128)(2,1)S(1)}, bf16[128,512]{1,0:T(8,128)(2,1)}, u32[]{:S(2)}) copy-start(bf16[128,512]{1,0:T(8,128)(2,1)} %residual_ref.1) | copy-start | bytes 393220
  50.1 10.1 %collective-permute-start.3 = (bf16[128,512]{1,0:T(8,128)(2,1)S(1)}, bf16[128,512]{1,0:T(8,128)(2,1)S(1)}, u32[]{:S(2)}, u32[]{:S(2)}) collective-permute-start(bf16[128,512]{1,0:T(8,128)(2,1)S(1)} %get-tuple-element.28), channel_id=1, source_target_pairs={{0,6},{1,7},{2,8},{3,9},{4,10},{5,11},{6,12},{7,13},{8,14},{9,15},... | collective-permute-start | bytes 393224 | tf_op jit(solution)/shard_map/ppermute | solution.py:309
  51.9 11.2 %collective-permute-start.4 = (bf16[128,512]{1,0:T(8,128)(2,1)S(1)}, bf16[128,512]{1,0:T(8,128)(2,1)S(1)}, u32[]{:S(2)}, u32[]{:S(2)}) collective-permute-start(bf16[128,512]{1,0:T(8,128)(2,1)S(1)} %get-tuple-element.29), channel_id=1, source_target_pairs={{0,10},{1,11},{2,12},{3,13},{4,14},{5,15},{6,0},{7,1},{8,2},{9,3},... | collective-permute-start | bytes 393224 | tf_op jit(solution)/shard_map/ppermute | solution.py:309

commit v3 on v2

--- a/solution.py
+++ b/solution.py
@@ -13,7 +13,7 @@
 RIGHT = (1, -2)
 LEFT = (-1, 2)
 KEEP = (0, 3, -3)
-PIECES = 8
+PIECES = 2
 GRANT = pltpu.CompilerParams(vmem_limit_bytes=16 * 2**20)
 WHOLE = pltpu.CompilerParams(vmem_limit_bytes=60 * 2**20)
 
@@ -65,28 +65,32 @@
 
 
 def product_kernel(
-    core_ref, x_ref, w_hbm, theirs_hbm, mine_hbm, w_ref, theirs_ref, mine_ref, in_sems, theirs_sems, mine_sems
+    core_ref, x_hbm, w_hbm, theirs_hbm, mine_hbm, x_ref, w_ref, theirs_ref, mine_ref, x_sem, w_sems, out_sems
 ):
     first = core_ref[0] == 0
     chips, _, block = mine_ref.shape
-    depth = w_ref.shape[0] // PIECES
-    loads = []
+    loads = [pltpu.make_async_copy(x_hbm, x_ref, x_sem)]
+    part = w_ref.shape[1] // PIECES
     for piece in range(PIECES):
-        part = slice(piece * depth, (piece + 1) * depth)
-        loads.append(pltpu.make_async_copy(w_hbm.at[part], w_ref.at[part], in_sems.at[piece]))
-        loads[piece].start()
+        columns = slice(piece * part, (piece + 1) * part)
+        loads.append(
+            pltpu.make_async_copy(w_hbm.at[:, columns], w_ref.at[:, columns], w_sems.at[piece])
+        )
     for load in loads:
-        load.wait()
+        load.start()
+    loads[0].wait()
     stores = []
     for z in range(chips):
+        if z % (chips // PIECES) == 0:
+            loads[1 + z // (chips // PIECES)].wait()
         both = jnp.dot(
             x_ref[...], w_ref[:, 2 * z * block : 2 * (z + 1) * block], preferred_element_type=F32
         )
         low, high = both[:, :block], both[:, block:]
         theirs_ref[z] = jnp.where(first, high, low).astype(BF16)
         mine_ref[z] = jnp.where(first, low, high)
-        for ref, hbm, sems in ((theirs_ref, theirs_hbm, theirs_sems), (mine_ref, mine_hbm, mine_sems)):
-            stores.append(pltpu.make_async_copy(ref.at[z], hbm.at[z], sems.at[z]))
+        for place, (ref, hbm) in enumerate(((theirs_ref, theirs_hbm), (mine_ref, mine_hbm))):
+            stores.append(pltpu.make_async_copy(ref.at[z], hbm.at[z], out_sems.at[place, z]))
             stores[-1].start()
     for store in stores:
         store.wait()
@@ -95,25 +99,23 @@
 def product(core, x, w, chips):
     rows, depth = x.shape
     block = w.shape[1] // (2 * chips)
+    anywhere = pl.BlockSpec(memory_space=pl.ANY)
     return pl.pallas_call(
         product_kernel,
         out_shape=(
             jax.ShapeDtypeStruct((chips, rows, block), BF16),
             jax.ShapeDtypeStruct((chips, rows, block), F32),
         ),
-        in_specs=[
-            pl.BlockSpec(memory_space=pltpu.SMEM),
-            pl.BlockSpec(memory_space=pltpu.VMEM),
-            pl.BlockSpec(memory_space=pl.ANY),
-        ],
-        out_specs=(pl.BlockSpec(memory_space=pl.ANY), pl.BlockSpec(memory_space=pl.ANY)),
+        in_specs=[pl.BlockSpec(memory_space=pltpu.SMEM), anywhere, anywhere],
+        out_specs=(anywhere, anywhere),
         scratch_shapes=[
+            pltpu.VMEM(x.shape, BF16),
             pltpu.VMEM(w.shape, BF16),
             pltpu.VMEM((chips, rows, block), BF16),
             pltpu.VMEM((chips, rows, block), F32),
+            pltpu.SemaphoreType.DMA,
             pltpu.SemaphoreType.DMA((PIECES,)),
-            pltpu.SemaphoreType.DMA((chips,)),
-            pltpu.SemaphoreType.DMA((chips,)),
+            pltpu.SemaphoreType.DMA((2, chips)),
         ],
         cost_estimate=pl.CostEstimate(
             flops=2 * rows * w.size, bytes_accessed=2 * w.size, transcendentals=0
@@ -123,7 +125,7 @@
     )(core, x, w)
 
 
-def pair_kernel(chips, z_ref, mine_ref, other_ref, right_ref, left_ref, keep_ref):
+def pair_kernel(chips, z_ref, residual_ref, mine_ref, other_ref, right_ref, left_ref, keep_ref):
     z = z_ref[0]
     rows = keep_ref.shape[1]
     half = rows // 2
@@ -138,9 +140,10 @@
         ref[len(steps) * rows :] = total(chips // 2, first, first + half).astype(BF16)
     for place, step in enumerate(KEEP):
         keep_ref[place] = total(step, 0, rows)
-
-
-def pair_sum(z, mine, other):
+    keep_ref[0] += residual_ref[...].astype(F32)
+
+
+def pair_sum(z, residual, mine, other):
     chips, rows, block = mine.shape
     sent = len(RIGHT) * rows + rows // 2
     return pl.pallas_call(
@@ -150,27 +153,22 @@
             jax.ShapeDtypeStruct((sent, block), BF16),
             jax.ShapeDtypeStruct((len(KEEP), rows, block), F32),
         ),
-        in_specs=[pl.BlockSpec(memory_space=pltpu.SMEM)] + vmem_specs(2),
+        in_specs=[pl.BlockSpec(memory_space=pltpu.SMEM)] + vmem_specs(3),
         out_specs=tuple(vmem_specs(3)),
         cost_estimate=pl.CostEstimate(flops=mine.size, bytes_accessed=8 * mine.size, transcendentals=0),
         compiler_params=GRANT,
         name="pair_sum",
-    )(z, mine, other)
-
-
-def relay_kernel(residual_ref, keep_ref, right_ref, left_ref, here_ref, far_right_ref, far_left_ref):
+    )(z, residual, mine, other)
+
+
+def relay_kernel(keep_ref, right_ref, left_ref, here_ref, far_right_ref, far_left_ref):
     rows = here_ref.shape[0]
     half = rows // 2
 
     def part(ref, place, first, last):
         return ref[place * rows + first : place * rows + last].astype(F32)
 
-    here_ref[...] = (
-        residual_ref[...].astype(F32)
-        + keep_ref[0]
-        + part(right_ref, 0, 0, rows)
-        + part(left_ref, 0, 0, rows)
-    )
+    here_ref[...] = keep_ref[0] + part(right_ref, 0, 0, rows) + part(left_ref, 0, 0, rows)
     for first, last in ((0, half), (half, rows)):
         right = keep_ref[1, first:last] + part(left_ref, 1, first, last)
         left = keep_ref[2, first:last] + part(right_ref, 1, first, last)
@@ -182,7 +180,7 @@
         far_left_ref[first:last] = left.astype(BF16)
 
 
-def relay(residual, keep, right, left):
+def relay(keep, right, left):
     _, rows, block = keep.shape
     return pl.pallas_call(
         relay_kernel,
@@ -191,12 +189,12 @@
             jax.ShapeDtypeStruct((rows, block), BF16),
             jax.ShapeDtypeStruct((rows, block), BF16),
         ),
-        in_specs=vmem_specs(4),
+        in_specs=vmem_specs(3),
         out_specs=tuple(vmem_specs(3)),
         cost_estimate=pl.CostEstimate(flops=5 * rows * block, bytes_accessed=4 * keep.size, transcendentals=0),
         compiler_params=GRANT,
         name="relay",
-    )(residual, keep, right, left)
+    )(keep, right, left)
 
 
 def wanted_row(slots_ref, width):
@@ -254,7 +252,7 @@
         in_specs=vmem_specs(5),
         out_specs=pl.BlockSpec(memory_space=pltpu.VMEM),
         cost_estimate=pl.CostEstimate(
-            flops=2 * slot_total * up.size, bytes_accessed=2 * up.size, transcendentals=0
+            flops=10**11, bytes_accessed=10**9, transcendentals=0
         ),
         compiler_params=GRANT,
         name="expand",
@@ -324,11 +322,10 @@
     both = shrink + lax.ppermute(shrink, "tensor", siblings)
     two = both + along_z(both, 1)
     three = two + along_z(both, -1)
+    to_right, to_left, keep = pair_sum(z, residual, mine, other)
     three_left, two_right = along_z(three, 3), along_z(two, -3)
-
-    to_right, to_left, keep = pair_sum(z, mine, other)
     from_left, from_right = along_z(to_right, 1), along_z(to_left, -1)
-    here, far_right, far_left = relay(residual, keep, from_left, from_right)
+    here, far_right, far_left = relay(keep, from_left, from_right)
     sums = (here, along_z(far_right, 3), along_z(far_left, -3))
     up = up_factors.reshape(owned * rank, columns)
     expand = expand_rows(three, three_left, two_right, slots, up, owned)

time: 64.8 us -> 60.3 us (0.931)
  starting transfers between devices: 28.8 us -> 25.7 us
  Pallas kernels: 12.7 us -> 10.3 us
  waiting for transfers between devices: 20.1 us -> 21 us
    ppermute x8, starting transfers between devices: 16.4 us -> 14.4 us  [along_z(): lax.ppermute(array, 'tensor', [(i, (i + 2 * step) % shards) for i in rang...]
    all_to_all x1, waiting for transfers between devices: 2.55 us -> 3.97 us  [body(): lax.all_to_all(outgoing, 'dp', split_axis=0, concat_axis=0, tiled=True)]
    pallas_call x1, Pallas kernels: 6.59 us -> 5.19 us  [product(): pl.pallas_call(product_kernel, out_shape=(jax.ShapeDtypeStruct((chips, ro...]
    ppermute x8, waiting for transfers between devices: 13.6 us -> 12.2 us  [along_z(): lax.ppermute(array, 'tensor', [(i, (i + 2 * step) % shards) for i in rang...]
    all_to_all x1, starting transfers between devices: 4.77 us -> 3.67 us  [body(): lax.all_to_all(expand, 'dp', split_axis=0, concat_axis=0, tiled=True)]
    all_to_all x1, waiting for transfers between devices: 2.31 us -> 3.23 us  [body(): lax.all_to_all(expand, 'dp', split_axis=0, concat_axis=0, tiled=True)]
    pallas_call x1, Pallas kernels: 1.1 us -> 0.22 us  [pair_sum(): pl.pallas_call(functools.partial(pair_kernel, chips), out_shape=(jax.Shap...]
  transfers between devices with their start and end apart: 12 -> 12, of which waited for: 6 -> 8; matrix products, arithmetic and copies ran while one was open for 0% -> 0% of each run, Pallas kernels for 15% -> 12%
where the time goes in v3:
time: 60.3 us; the launch traced here: 59.9 us
  starting transfers between devices  25.7 us (43%)
  waiting for transfers between devices  21 us (35%)
  Pallas kernels  10.3 us (17%)
  local copies, waits for them, and re-layouts  2.83 us (5%)
    ppermute x8, starting transfers between devices, along_z(): lax.ppermute(array, 'tensor', [(i, (i + 2 * step) % shards) for i in rang...  14.4 us
    ppermute x8, waiting for transfers between devices, along_z(): lax.ppermute(array, 'tensor', [(i, (i + 2 * step) % shards) for i in rang...  12.2 us
    all_to_all x1, starting transfers between devices, body(): lax.all_to_all(outgoing, 'dp', split_axis=0, concat_axis=0, tiled=True)  7.03 us
    pallas_call x1, Pallas kernels, product(): pl.pallas_call(product_kernel, out_shape=(jax.ShapeDtypeStruct((chips, ro...  5.19 us
    all_to_all x1, waiting for transfers between devices, body(): lax.all_to_all(outgoing, 'dp', split_axis=0, concat_axis=0, tiled=True)  3.97 us
    all_to_all x1, starting transfers between devices, body(): lax.all_to_all(expand, 'dp', split_axis=0, concat_axis=0, tiled=True)  3.67 us
    all_to_all x1, waiting for transfers between devices, body(): lax.all_to_all(expand, 'dp', split_axis=0, concat_axis=0, tiled=True)  3.23 us
    unnamed x10, local copies, waits for them, and re-layouts  2.83 us
  transfers between devices with their start and end apart: 12, of which 8 were waited for; matrix products, arithmetic and copies ran while one was open for 0% of the time, Pallas kernels for 12%

profile of v3, /device:TPU:32, one launch (start us, length us, event | category | flops | bytes accessed | tf_op | source)
XLA Modules:
  0.0 59.9 jit_solution(2069220183807212139)
XLA Ops:
  0.0 2.1 %dispatch.1 = bf16[256,640]{1,0:T(8,128)(2,1)} custom-call(s32[1,128]{1,0:T(1,128)} %bitcast.15, bf16[128,512]{1,0:T(8,128)(2,1)} %x_hbm), custom_call_target="tpu_custom_call" | custom-call | flops 33554432 | bytes 262144 | tf_op jit(solution)/shard_map/dispatch/pallas_call | solution.py:54
  2.1 7.0 %all-to-all-start = ((bf16[16,16,640]{2,1,0:T(8,128)(2,1)}), bf16[16,16,640]{2,1,0:T(8,128)(2,1)S(1)}, u32[]{:S(2)}, u32[]{:S(2)}) async-start(bf16[16,16,640]{2,1,0:T(8,128)(2,1)} %bitcast.18), calls=%async_computation | async-start | bytes 655360 | tf_op jit(solution)/shard_map/all_to_all | solution.py:313
  9.1 5.2 %product.1 = (bf16[8,128,512]{2,1,0:T(8,128)(2,1)}, f32[8,128,512]{2,1,0:T(8,128)}) custom-call(s32[1]{0:T(128)} %bitcast.3.core_ref, bf16[128,512]{1,0:T(8,128)(2,1)} %x_hbm, bf16[512,8192]{1,0:T(8,128)(2,1)} %w_hbm.1), custom_call_target="tpu_custom_call" | custom-call | flops 1073741824 | bytes 8388608 | tf_op jit(solution)/shard_map/product/pallas_call | solution.py:103
  14.3 4.0 %all-to-all-done = bf16[16,16,640]{2,1,0:T(8,128)(2,1)S(1)} async-done(((bf16[16,16,640]{2,1,0:T(8,128)(2,1)}), bf16[16,16,640]{2,1,0:T(8,128)(2,1)S(1)}, u32[]{:S(2)}, u32[]{:S(2)}) %all-to-all-start) | async-done | bytes 327712 | tf_op jit(solution)/shard_map/all_to_all | solution.py:313
  18.3 0.0 collective-permute-start
  18.3 0.5 shrink.1
  18.8 0.6 %collective-permute-start.5 = (f32[16,256]{1,0:T(8,128)S(1)}, f32[16,256]{1,0:T(8,128)S(1)}, u32[]{:S(2)}, u32[]{:S(2)}) collective-permute-start(f32[16,256]{1,0:T(8,128)S(1)} %shrink.1), channel_id=1, source_target_pairs={{0,1},{1,0},{2,3},{3,2},{4,5},{5,4},{6,7},{7,6},{8,9},{9,8},{10,11... | collective-permute-start | bytes 49160 | tf_op jit(solution)/shard_map/ppermute | solution.py:322
  19.4 1.6 %collective-permute-done.5 = f32[16,256]{1,0:T(8,128)S(1)} collective-permute-done((f32[16,256]{1,0:T(8,128)S(1)}, f32[16,256]{1,0:T(8,128)S(1)}, u32[]{:S(2)}, u32[]{:S(2)}) %collective-permute-start.5) | collective-permute-done | bytes 16416 | tf_op jit(solution)/shard_map/ppermute | solution.py:322
  21.0 0.1 collective-permute-start.7
  21.1 1.9 %collective-permute-start.6 = (f32[16,256]{1,0:T(8,128)S(1)}, f32[16,256]{1,0:T(8,128)S(1)}, u32[]{:S(2)}, u32[]{:S(2)}) collective-permute-start(f32[16,256]{1,0:T(8,128)S(1)} %add.9), channel_id=1, source_target_pairs={{0,2},{1,3},{2,4},{3,5},{4,6},{5,7},{6,8},{7,9},{8,10},{9,11},{10,... | collective-permute-start | bytes 49160 | tf_op jit(solution)/shard_map/ppermute | solution.py:307
  23.0 1.7 %collective-permute-done.7 = f32[16,256]{1,0:T(8,128)S(1)} collective-permute-done((f32[16,256]{1,0:T(8,128)S(1)}, f32[16,256]{1,0:T(8,128)S(1)}, u32[]{:S(2)}, u32[]{:S(2)}) %collective-permute-start.7) | collective-permute-done | bytes 16416 | tf_op jit(solution)/shard_map/ppermute | solution.py:307
  24.7 3.9 %collective-permute-done.6 = f32[16,256]{1,0:T(8,128)S(1)} collective-permute-done((f32[16,256]{1,0:T(8,128)S(1)}, f32[16,256]{1,0:T(8,128)S(1)}, u32[]{:S(2)}, u32[]{:S(2)}) %collective-permute-start.6) | collective-permute-done | bytes 16416 | tf_op jit(solution)/shard_map/ppermute | solution.py:307
  28.7 2.9 %collective-permute-start.9 = (f32[16,256]{1,0:T(8,128)S(1)}, f32[16,256]{1,0:T(8,128)S(1)}, u32[]{:S(2)}, u32[]{:S(2)}) collective-permute-start(f32[16,256]{1,0:T(8,128)S(1)} %get-tuple-element.32), channel_id=1, source_target_pairs={{0,10},{1,11},{2,12},{3,13},{4,14},{5,15},{6,0},{7,1},{8,2},{9,3},... | collective-permute-start | bytes 49160 | tf_op jit(solution)/shard_map/ppermute | solution.py:307
  31.6 2.1 %collective-permute-start.8 = (f32[16,256]{1,0:T(8,128)S(1)}, f32[16,256]{1,0:T(8,128)S(1)}, u32[]{:S(2)}, u32[]{:S(2)}) collective-permute-start(f32[16,256]{1,0:T(8,128)S(1)} %get-tuple-element.31.three_ref), channel_id=1, source_target_pairs={{0,6},{1,7},{2,8},{3,9},{4,10},{5,11},{6,12},{7,13},{8,14},{9,15},... | collective-permute-start | bytes 49160 | tf_op jit(solution)/shard_map/ppermute | solution.py:307
  33.7 0.0 collective-permute-done.other_ref
  33.7 1.6 %copy-done = f32[8,128,512]{2,1,0:T(8,128)S(1)} copy-done((f32[8,128,512]{2,1,0:T(8,128)S(1)}, f32[8,128,512]{2,1,0:T(8,128)}, u32[]{:S(2)}) %copy-start) | copy-done | bytes 2097176
  35.3 0.2 pair_sum.1
  35.5 0.1 collective-permute-start.1
  35.6 2.1 %collective-permute-start.2 = (bf16[320,512]{1,0:T(8,128)(2,1)S(1)}, bf16[320,512]{1,0:T(8,128)(2,1)S(1)}, u32[]{:S(2)}, u32[]{:S(2)}) collective-permute-start(bf16[320,512]{1,0:T(8,128)(2,1)S(1)} %get-tuple-element.26), channel_id=1, source_target_pairs={{0,14},{1,15},{2,0},{3,1},{4,2},{5,3},{6,4},{7,5},{8,6},{9,7},{10,... | collective-permute-start | bytes 983048 | tf_op jit(solution)/shard_map/ppermute | solution.py:307
  37.7 0.0 collective-permute-done.9.left_ref
  37.7 0.8 %collective-permute-done.8.right_ref = f32[16,256]{1,0:T(8,128)S(1)} collective-permute-done((f32[16,256]{1,0:T(8,128)S(1)}, f32[16,256]{1,0:T(8,128)S(1)}, u32[]{:S(2)}, u32[]{:S(2)}) %collective-permute-start.8) | collective-permute-done | bytes 16416 | tf_op jit(solution)/shard_map/ppermute | solution.py:307
  38.5 1.2 %copy-done.4 = bf16[64,16,512]{2,1,0:T(8,128)(2,1)S(1)} copy-done((bf16[64,16,512]{2,1,0:T(8,128)(2,1)S(1)}, bf16[64,16,512]{2,1,0:T(8,128)(2,1)}, u32[]{:S(2)}) %copy-start.4) | copy-done | bytes 1048600
  39.7 1.3 %expand.1 = bf16[256,512]{1,0:T(8,128)(2,1)} custom-call(f32[16,256]{1,0:T(8,128)S(1)} %get-tuple-element.31.three_ref, f32[16,256]{1,0:T(8,128)S(1)} %collective-permute-done.8.right_ref, f32[16,256]{1,0:T(8,128)S(1)} %collective-permute-done.9.left_ref, bf16[256,640]{1,0:T(8,128)(2,1)S(1)} %bitcast.12, bf16[1024,512]{1,0:T(8,128)(2,1)S(1)} %bitcast.17), custom_call_target="tpu_custom_call" | custom-call | flops 99999997952 | bytes 1000000000 | tf_op jit(solution)/shard_map/expand/pallas_call | solution.py:249
  41.0 3.7 %all-to-all-start.1 = ((bf16[16,16,512]{2,1,0:T(8,128)(2,1)}), bf16[16,16,512]{2,1,0:T(8,128)(2,1)S(1)}, u32[]{:S(2)}, u32[]{:S(2)}) async-start(bf16[16,16,512]{2,1,0:T(8,128)(2,1)} %bitcast.8), calls=%async_computation.1 | async-start | bytes 524288 | tf_op jit(solution)/shard_map/all_to_all | solution.py:333
  44.7 0.0 collective-permute-done.1.right_ref
  44.7 0.1 relay.1
  44.8 2.7 %collective-permute-start.3 = (bf16[128,512]{1,0:T(8,128)(2,1)S(1)}, bf16[128,512]{1,0:T(8,128)(2,1)S(1)}, u32[]{:S(2)}, u32[]{:S(2)}) collective-permute-start(bf16[128,512]{1,0:T(8,128)(2,1)S(1)} %get-tuple-element.28), channel_id=1, source_target_pairs={{0,6},{1,7},{2,8},{3,9},{4,10},{5,11},{6,12},{7,13},{8,14},{9,15},... | collective-permute-start | bytes 393224 | tf_op jit(solution)/shard_map/ppermute | solution.py:307
  47.5 2.4 %collective-permute-start.4 = (bf16[128,512]{1,0:T(8,128)(2,1)S(1)}, bf16[128,512]{1,0:T(8,128)(2,1)S(1)}, u32[]{:S(2)}, u32[]{:S(2)}) collective-permute-start(bf16[128,512]{1,0:T(8,128)(2,1)S(1)} %get-tuple-element.29), channel_id=1, source_target_pairs={{0,10},{1,11},{2,12},{3,13},{4,14},{5,15},{6,0},{7,1},{8,2},{9,3},... | collective-permute-start | bytes 393224 | tf_op jit(solution)/shard_map/ppermute | solution.py:307
  49.9 3.2 %all-to-all-done.1 = bf16[16,16,512]{2,1,0:T(8,128)(2,1)S(1)} async-done(((bf16[16,16,512]{2,1,0:T(8,128)(2,1)}), bf16[16,16,512]{2,1,0:T(8,128)(2,1)S(1)}, u32[]{:S(2)}, u32[]{:S(2)}) %all-to-all-start.1) | async-done | bytes 262176 | tf_op jit(solution)/shard_map/all_to_all | solution.py:333
  53.1 2.6 %collective-permute-done.3.right_ref = bf16[128,512]{1,0:T(8,128)(2,1)S(1)} collective-permute-done((bf16[128,512]{1,0:T(8,128)(2,1)S(1)}, bf16[128,512]{1,0:T(8,128)(2,1)S(1)}, u32[]{:S(2)}, u32[]{:S(2)}) %collective-permute-start.3) | collective-permute-done | bytes 131104 | tf_op jit(solution)/shard_map/ppermute | solution.py:307
  55.7 3.2 %collective-permute-done.4.left_ref = bf16[128,512]{1,0:T(8,128)(2,1)S(1)} collective-permute-done((bf16[128,512]{1,0:T(8,128)(2,1)S(1)}, bf16[128,512]{1,0:T(8,128)(2,1)S(1)}, u32[]{:S(2)}, u32[]{:S(2)}) %collective-permute-start.4) | collective-permute-done | bytes 131104 | tf_op jit(solution)/shard_map/ppermute | solution.py:307
  58.9 1.0 %finish.1 = bf16[128,512]{1,0:T(8,128)(2,1)} custom-call(s32[1,128]{1,0:T(1,128)S(1)} %bitcast.16, f32[128,512]{1,0:T(8,128)S(1)} %get-tuple-element.27.here_ref, bf16[128,512]{1,0:T(8,128)(2,1)S(1)} %collective-permute-done.3.right_ref, bf16[128,512]{1,0:T(8,128)(2,1)S(1)} %collective-permute-done.4.left_ref, bf16[256,512]{1,0:T(8,128)(2,1)S(1)} %bitcast.13), custom_call_target="tpu_custom_call" | custom-call | flops 33554432 | bytes 524288 | tf_op jit(solution)/shard_map/finish/pallas_call | solution.py:280
  (11 shorter events, 0.0 us)
Async XLA Ops:
  0.0 18.3 %copy-start.1 = (bf16[64,512,16]{1,2,0:T(8,128)(2,1)S(1)}, bf16[64,512,16]{1,2,0:T(8,128)(2,1)}, u32[]{:S(2)}) copy-start(bf16[64,512,16]{1,2,0:T(8,128)(2,1)} %param.9) | copy-start | bytes 3145732
  0.0 33.7 %copy-start.2 = (bf16[128,512]{1,0:T(8,128)(2,1)S(1)}, bf16[128,512]{1,0:T(8,128)(2,1)}, u32[]{:S(2)}) copy-start(bf16[128,512]{1,0:T(8,128)(2,1)} %residual_ref.1) | copy-start | bytes 393220
  2.1 16.2 %all-to-all-start = ((bf16[16,16,640]{2,1,0:T(8,128)(2,1)}), bf16[16,16,640]{2,1,0:T(8,128)(2,1)S(1)}, u32[]{:S(2)}, u32[]{:S(2)}) async-start(bf16[16,16,640]{2,1,0:T(8,128)(2,1)} %bitcast.18), calls=%async_computation | async-start | bytes 655360 | tf_op jit(solution)/shard_map/all_to_all | solution.py:313
  18.3 15.4 %collective-permute-start = (bf16[8,128,512]{2,1,0:T(8,128)(2,1)}, bf16[8,128,512]{2,1,0:T(8,128)(2,1)S(1)}, u32[]{:S(2)}, u32[]{:S(2)}) collective-permute-start(bf16[8,128,512]{2,1,0:T(8,128)(2,1)} %get-tuple-element.23), channel_id=1, source_target_pairs={{0,1},{1,0},{2,3},{3,2},{4,5},{5,4},{6,7},{7,6},{8,9},{9,8},{10,11... | collective-permute-start | bytes 3145736 | tf_op jit(solution)/shard_map/ppermute | solution.py:317
  18.8 2.2 %collective-permute-start.5 = (f32[16,256]{1,0:T(8,128)S(1)}, f32[16,256]{1,0:T(8,128)S(1)}, u32[]{:S(2)}, u32[]{:S(2)}) collective-permute-start(f32[16,256]{1,0:T(8,128)S(1)} %shrink.1), channel_id=1, source_target_pairs={{0,1},{1,0},{2,3},{3,2},{4,5},{5,4},{6,7},{7,6},{8,9},{9,8},{10,11... | collective-permute-start | bytes 49160 | tf_op jit(solution)/shard_map/ppermute | solution.py:322
  21.0 3.7 %collective-permute-start.7 = (f32[16,256]{1,0:T(8,128)S(1)}, f32[16,256]{1,0:T(8,128)S(1)}, u32[]{:S(2)}, u32[]{:S(2)}) collective-permute-start(f32[16,256]{1,0:T(8,128)S(1)} %add.9), channel_id=1, source_target_pairs={{0,14},{1,15},{2,0},{3,1},{4,2},{5,3},{6,4},{7,5},{8,6},{9,7},{10,... | collective-permute-start | bytes 49160 | tf_op jit(solution)/shard_map/ppermute | solution.py:307
  21.1 7.6 %collective-permute-start.6 = (f32[16,256]{1,0:T(8,128)S(1)}, f32[16,256]{1,0:T(8,128)S(1)}, u32[]{:S(2)}, u32[]{:S(2)}) collective-permute-start(f32[16,256]{1,0:T(8,128)S(1)} %add.9), channel_id=1, source_target_pairs={{0,2},{1,3},{2,4},{3,5},{4,6},{5,7},{6,8},{7,9},{8,10},{9,11},{10,... | collective-permute-start | bytes 49160 | tf_op jit(solution)/shard_map/ppermute | solution.py:307
  28.7 9.1 %collective-permute-start.9 = (f32[16,256]{1,0:T(8,128)S(1)}, f32[16,256]{1,0:T(8,128)S(1)}, u32[]{:S(2)}, u32[]{:S(2)}) collective-permute-start(f32[16,256]{1,0:T(8,128)S(1)} %get-tuple-element.32), channel_id=1, source_target_pairs={{0,10},{1,11},{2,12},{3,13},{4,14},{5,15},{6,0},{7,1},{8,2},{9,3},... | collective-permute-start | bytes 49160 | tf_op jit(solution)/shard_map/ppermute | solution.py:307
  31.6 6.9 %collective-permute-start.8 = (f32[16,256]{1,0:T(8,128)S(1)}, f32[16,256]{1,0:T(8,128)S(1)}, u32[]{:S(2)}, u32[]{:S(2)}) collective-permute-start(f32[16,256]{1,0:T(8,128)S(1)} %get-tuple-element.31.three_ref), channel_id=1, source_target_pairs={{0,6},{1,7},{2,8},{3,9},{4,10},{5,11},{6,12},{7,13},{8,14},{9,15},... | collective-permute-start | bytes 49160 | tf_op jit(solution)/shard_map/ppermute | solution.py:307
  33.7 1.6 %copy-start = (f32[8,128,512]{2,1,0:T(8,128)S(1)}, f32[8,128,512]{2,1,0:T(8,128)}, u32[]{:S(2)}) copy-start(f32[8,128,512]{2,1,0:T(8,128)} %get-tuple-element.22.mine_ref) | copy-start | bytes 6291460
  35.5 9.1 %collective-permute-start.1 = (bf16[320,512]{1,0:T(8,128)(2,1)S(1)}, bf16[320,512]{1,0:T(8,128)(2,1)S(1)}, u32[]{:S(2)}, u32[]{:S(2)}) collective-permute-start(bf16[320,512]{1,0:T(8,128)(2,1)S(1)} %get-tuple-element.25), channel_id=1, source_target_pairs={{0,2},{1,3},{2,4},{3,5},{4,6},{5,7},{6,8},{7,9},{8,10},{9,11},{10,... | collective-permute-start | bytes 983048 | tf_op jit(solution)/shard_map/ppermute | solution.py:307
  35.6 9.1 %collective-permute-start.2 = (bf16[320,512]{1,0:T(8,128)(2,1)S(1)}, bf16[320,512]{1,0:T(8,128)(2,1)S(1)}, u32[]{:S(2)}, u32[]{:S(2)}) collective-permute-start(bf16[320,512]{1,0:T(8,128)(2,1)S(1)} %get-tuple-element.26), channel_id=1, source_target_pairs={{0,14},{1,15},{2,0},{3,1},{4,2},{5,3},{6,4},{7,5},{8,6},{9,7},{10,... | collective-permute-start | bytes 983048 | tf_op jit(solution)/shard_map/ppermute | solution.py:307
  38.5 1.2 %copy-start.4 = (bf16[64,16,512]{2,1,0:T(8,128)(2,1)S(1)}, bf16[64,16,512]{2,1,0:T(8,128)(2,1)}, u32[]{:S(2)}) copy-start(bf16[64,16,512]{2,1,0:T(8,128)(2,1)} %param.10) | copy-start | bytes 3145732
  39.7 19.2 %copy-start.3 = (s32[128]{0:T(128)S(1)}, s32[128]{0:T(128)}, u32[]{:S(2)}) copy-start(s32[128]{0:T(128)} %param.11) | copy-start | bytes 1540
  41.0 12.1 %all-to-all-start.1 = ((bf16[16,16,512]{2,1,0:T(8,128)(2,1)}), bf16[16,16,512]{2,1,0:T(8,128)(2,1)S(1)}, u32[]{:S(2)}, u32[]{:S(2)}) async-start(bf16[16,16,512]{2,1,0:T(8,128)(2,1)} %bitcast.8), calls=%async_computation.1 | async-start | bytes 524288 | tf_op jit(solution)/shard_map/all_to_all | solution.py:333
  44.8 10.9 %collective-permute-start.3 = (bf16[128,512]{1,0:T(8,128)(2,1)S(1)}, bf16[128,512]{1,0:T(8,128)(2,1)S(1)}, u32[]{:S(2)}, u32[]{:S(2)}) collective-permute-start(bf16[128,512]{1,0:T(8,128)(2,1)S(1)} %get-tuple-element.28), channel_id=1, source_target_pairs={{0,6},{1,7},{2,8},{3,9},{4,10},{5,11},{6,12},{7,13},{8,14},{9,15},... | collective-permute-start | bytes 393224 | tf_op jit(solution)/shard_map/ppermute | solution.py:307
  47.5 11.4 %collective-permute-start.4 = (bf16[128,512]{1,0:T(8,128)(2,1)S(1)}, bf16[128,512]{1,0:T(8,128)(2,1)S(1)}, u32[]{:S(2)}, u32[]{:S(2)}) collective-permute-start(bf16[128,512]{1,0:T(8,128)(2,1)S(1)} %get-tuple-element.29), channel_id=1, source_target_pairs={{0,10},{1,11},{2,12},{3,13},{4,14},{5,15},{6,0},{7,1},{8,2},{9,3},... | collective-permute-start | bytes 393224 | tf_op jit(solution)/shard_map/ppermute | solution.py:307

commit v4 on v3

--- a/solution.py
+++ b/solution.py
@@ -10,9 +10,9 @@
 BF16 = jnp.bfloat16
 F32 = jnp.float32
 LANES = 128
-RIGHT = (1, -2)
-LEFT = (-1, 2)
-KEEP = (0, 3, -3)
+RIGHT = (1, 3)
+LEFT = (-1, -3)
+KEEP = (0, 2, -2)
 PIECES = 2
 GRANT = pltpu.CompilerParams(vmem_limit_bytes=16 * 2**20)
 WHOLE = pltpu.CompilerParams(vmem_limit_bytes=60 * 2**20)
@@ -65,9 +65,23 @@
 
 
 def product_kernel(
-    core_ref, x_hbm, w_hbm, theirs_hbm, mine_hbm, x_ref, w_ref, theirs_ref, mine_ref, x_sem, w_sems, out_sems
+    place_ref,
+    x_hbm,
+    residual_hbm,
+    w_hbm,
+    theirs_hbm,
+    mine_hbm,
+    x_ref,
+    residual_ref,
+    w_ref,
+    theirs_ref,
+    mine_ref,
+    x_sem,
+    residual_sem,
+    w_sems,
+    out_sems,
 ):
-    first = core_ref[0] == 0
+    here, first = place_ref[0] >> 1, (place_ref[0] & 1) == 0
     chips, _, block = mine_ref.shape
     loads = [pltpu.make_async_copy(x_hbm, x_ref, x_sem)]
     part = w_ref.shape[1] // PIECES
@@ -78,17 +92,21 @@
         )
     for load in loads:
         load.start()
+    residual_load = pltpu.make_async_copy(residual_hbm, residual_ref, residual_sem)
+    residual_load.start()
     loads[0].wait()
     stores = []
     for z in range(chips):
         if z % (chips // PIECES) == 0:
             loads[1 + z // (chips // PIECES)].wait()
+        if z == 0:
+            residual_load.wait()
         both = jnp.dot(
             x_ref[...], w_ref[:, 2 * z * block : 2 * (z + 1) * block], preferred_element_type=F32
         )
         low, high = both[:, :block], both[:, block:]
         theirs_ref[z] = jnp.where(first, high, low).astype(BF16)
-        mine_ref[z] = jnp.where(first, low, high)
+        mine_ref[z] = jnp.where(first, low, high) + jnp.where(here == z, residual_ref[...].astype(F32), 0.0)
         for place, (ref, hbm) in enumerate(((theirs_ref, theirs_hbm), (mine_ref, mine_hbm))):
             stores.append(pltpu.make_async_copy(ref.at[z], hbm.at[z], out_sems.at[place, z]))
             stores[-1].start()
@@ -96,7 +114,7 @@
         store.wait()
 
 
-def product(core, x, w, chips):
+def product(place, x, residual, w, chips):
     rows, depth = x.shape
     block = w.shape[1] // (2 * chips)
     anywhere = pl.BlockSpec(memory_space=pl.ANY)
@@ -106,14 +124,16 @@
             jax.ShapeDtypeStruct((chips, rows, block), BF16),
             jax.ShapeDtypeStruct((chips, rows, block), F32),
         ),
-        in_specs=[pl.BlockSpec(memory_space=pltpu.SMEM), anywhere, anywhere],
+        in_specs=[pl.BlockSpec(memory_space=pltpu.SMEM), anywhere, anywhere, anywhere],
         out_specs=(anywhere, anywhere),
         scratch_shapes=[
             pltpu.VMEM(x.shape, BF16),
+            pltpu.VMEM(residual.shape, BF16),
             pltpu.VMEM(w.shape, BF16),
             pltpu.VMEM((chips, rows, block), BF16),
             pltpu.VMEM((chips, rows, block), F32),
             pltpu.SemaphoreType.DMA,
+            pltpu.SemaphoreType.DMA,
             pltpu.SemaphoreType.DMA((PIECES,)),
             pltpu.SemaphoreType.DMA((2, chips)),
         ],
@@ -122,10 +142,12 @@
         ),
         compiler_params=WHOLE,
         name="product",
-    )(core, x, w)
-
-
-def pair_kernel(chips, z_ref, residual_ref, mine_ref, other_ref, right_ref, left_ref, keep_ref):
+    )(place, x, residual, w)
+
+
+def pair_kernel(
+    chips, z_ref, mine_ref, other_ref, right_ref, left_ref, half_right_ref, half_left_ref, keep_ref
+):
     z = z_ref[0]
     rows = keep_ref.shape[1]
     half = rows // 2
@@ -134,53 +156,52 @@
         at = lax.rem(z + (step + chips), chips)
         return mine_ref[at, first:last] + other_ref[at, first:last].astype(F32)
 
-    for ref, steps, first in ((right_ref, RIGHT, 0), (left_ref, LEFT, half)):
+    for ref, steps in ((right_ref, RIGHT), (left_ref, LEFT)):
         for place, step in enumerate(steps):
-            ref[place * rows : (place + 1) * rows] = total(step, 0, rows).astype(BF16)
-        ref[len(steps) * rows :] = total(chips // 2, first, first + half).astype(BF16)
+            ref[place] = total(step, 0, rows).astype(BF16)
+    half_right_ref[...] = total(chips // 2, 0, half).astype(BF16)
+    half_left_ref[...] = total(chips // 2, half, rows).astype(BF16)
     for place, step in enumerate(KEEP):
         keep_ref[place] = total(step, 0, rows)
-    keep_ref[0] += residual_ref[...].astype(F32)
-
-
-def pair_sum(z, residual, mine, other):
+
+
+def pair_sum(z, mine, other):
     chips, rows, block = mine.shape
-    sent = len(RIGHT) * rows + rows // 2
     return pl.pallas_call(
         functools.partial(pair_kernel, chips),
         out_shape=(
-            jax.ShapeDtypeStruct((sent, block), BF16),
-            jax.ShapeDtypeStruct((sent, block), BF16),
+            jax.ShapeDtypeStruct((len(RIGHT), rows, block), BF16),
+            jax.ShapeDtypeStruct((len(LEFT), rows, block), BF16),
+            jax.ShapeDtypeStruct((rows // 2, block), BF16),
+            jax.ShapeDtypeStruct((rows // 2, block), BF16),
             jax.ShapeDtypeStruct((len(KEEP), rows, block), F32),
         ),
-        in_specs=[pl.BlockSpec(memory_space=pltpu.SMEM)] + vmem_specs(3),
-        out_specs=tuple(vmem_specs(3)),
+        in_specs=[pl.BlockSpec(memory_space=pltpu.SMEM)] + vmem_specs(2),
+        out_specs=tuple(vmem_specs(5)),
         cost_estimate=pl.CostEstimate(flops=mine.size, bytes_accessed=8 * mine.size, transcendentals=0),
         compiler_params=GRANT,
         name="pair_sum",
-    )(z, residual, mine, other)
-
-
-def relay_kernel(keep_ref, right_ref, left_ref, here_ref, far_right_ref, far_left_ref):
+    )(z, mine, other)
+
+
+def relay_kernel(
+    keep_ref, right_ref, left_ref, half_right_ref, half_left_ref, here_ref, far_right_ref, far_left_ref
+):
     rows = here_ref.shape[0]
     half = rows // 2
-
-    def part(ref, place, first, last):
-        return ref[place * rows + first : place * rows + last].astype(F32)
-
-    here_ref[...] = keep_ref[0] + part(right_ref, 0, 0, rows) + part(left_ref, 0, 0, rows)
+    here_ref[...] = keep_ref[0] + right_ref[0].astype(F32) + left_ref[0].astype(F32)
     for first, last in ((0, half), (half, rows)):
-        right = keep_ref[1, first:last] + part(left_ref, 1, first, last)
-        left = keep_ref[2, first:last] + part(right_ref, 1, first, last)
+        right = keep_ref[1, first:last] + right_ref[1, first:last].astype(F32)
+        left = keep_ref[2, first:last] + left_ref[1, first:last].astype(F32)
         if first == 0:
-            right += part(right_ref, 2, 0, half)
+            right += half_right_ref[...].astype(F32)
         else:
-            left += part(left_ref, 2, 0, half)
+            left += half_left_ref[...].astype(F32)
         far_right_ref[first:last] = right.astype(BF16)
         far_left_ref[first:last] = left.astype(BF16)
 
 
-def relay(keep, right, left):
+def relay(keep, right, left, half_right, half_left):
     _, rows, block = keep.shape
     return pl.pallas_call(
         relay_kernel,
@@ -189,12 +210,12 @@
             jax.ShapeDtypeStruct((rows, block), BF16),
             jax.ShapeDtypeStruct((rows, block), BF16),
         ),
-        in_specs=vmem_specs(3),
+        in_specs=vmem_specs(5),
         out_specs=tuple(vmem_specs(3)),
         cost_estimate=pl.CostEstimate(flops=5 * rows * block, bytes_accessed=4 * keep.size, transcendentals=0),
         compiler_params=GRANT,
         name="relay",
-    )(keep, right, left)
+    )(keep, right, left, half_right, half_left)
 
 
 def wanted_row(slots_ref, width):
@@ -300,7 +321,7 @@
     capacity = 2 * rows // groups
     slot_count = groups * capacity
     place = lax.axis_index("tensor")
-    z, core = (place >> 1).reshape(1), (place & 1).reshape(1)
+    z, place = (place >> 1).reshape(1), place.reshape(1)
     siblings = [(i, i ^ 1) for i in range(shards)]
 
     def along_z(array, step):
@@ -312,7 +333,7 @@
     outgoing = outgoing.reshape(groups, capacity, width + LANES)
     slots = lax.all_to_all(outgoing, "dp", split_axis=0, concat_axis=0, tiled=True)
 
-    theirs, mine = product(core, x, output_weight, chips)
+    theirs, mine = product(place, x, residual, output_weight, chips)
     slots, theirs, mine = lax.optimization_barrier((slots, theirs, mine))
     other = lax.ppermute(theirs, "tensor", siblings)
 
@@ -320,13 +341,17 @@
     down = down_factors.transpose(0, 2, 1).reshape(owned * rank, width)
     shrink = shrink_terms(slots, down, owned)
     both = shrink + lax.ppermute(shrink, "tensor", siblings)
-    two = both + along_z(both, 1)
-    three = two + along_z(both, -1)
-    to_right, to_left, keep = pair_sum(z, residual, mine, other)
+    *moving, keep = pair_sum(z, mine, other)
+    before, after = along_z(both, 1), along_z(both, -1)
+    before, after, *moving = lax.optimization_barrier((before, after, *moving))
+    two = both + before
+    three = two + after
     three_left, two_right = along_z(three, 3), along_z(two, -3)
-    from_left, from_right = along_z(to_right, 1), along_z(to_left, -1)
-    here, far_right, far_left = relay(keep, from_left, from_right)
-    sums = (here, along_z(far_right, 3), along_z(far_left, -3))
+    halves = along_z(moving[2], 2), along_z(moving[3], -2)
+    three_left, *halves = lax.optimization_barrier((three_left, *halves))
+    arrived = along_z(moving[0], 1), along_z(moving[1], -1), *halves
+    here, far_right, far_left = relay(keep, *arrived)
+    sums = (here, along_z(far_right, 2), along_z(far_left, -2))
     up = up_factors.reshape(owned * rank, columns)
     expand = expand_rows(three, three_left, two_right, slots, up, owned)
     expand = expand.reshape(groups, capacity, columns)

time: 60.3 us -> 59.5 us (0.987); the launches traced: 59.9 us -> 58.4 us
  waiting for transfers between devices: 21 us -> 14.1 us
  starting transfers between devices: 25.7 us -> 30.9 us
  Pallas kernels: 10.3 us -> 11.8 us
  local copies, waits for them, and re-layouts: 2.83 us -> 1.6 us
    ppermute x8 -> x10, waiting for transfers between devices: 12.2 us -> 5.09 us  [along_z(): lax.ppermute(array, 'tensor', [(i, (i + 2 * step) % shards) for i in rang...]
    ppermute x8 -> x10, starting transfers between devices: 14.4 us -> 19.2 us  [along_z(): lax.ppermute(array, 'tensor', [(i, (i + 2 * step) % shards) for i in rang...]
    unnamed x10 -> x8, local copies, waits for them, and re-layouts: 2.83 us -> 1.6 us
    all_to_all x1, waiting for transfers between devices: 3.23 us -> 4.12 us  [body(): lax.all_to_all(expand, 'dp', split_axis=0, concat_axis=0, tiled=True)]
    pallas_call x1, Pallas kernels: 0.22 us -> 0.94 us  [pair_sum(): pl.pallas_call(functools.partial(pair_kernel, chips), out_shape=(jax.Shap...]
    all_to_all x1, waiting for transfers between devices: 3.97 us -> 3.28 us  [body(): lax.all_to_all(outgoing, 'dp', split_axis=0, concat_axis=0, tiled=True)]
    pallas_call x1, Pallas kernels: 5.19 us -> 5.87 us  [product(): pl.pallas_call(product_kernel, out_shape=(jax.ShapeDtypeStruct((chips, ro...]
  transfers between devices with their start and end apart: 12 -> 14, of which waited for: 8 -> 6; matrix products, arithmetic and copies ran while one was open for 0% -> 0% of each run, Pallas kernels for 12% -> 15%
where the time goes in v4:
time: 59.5 us; the launch traced here: 58.4 us
  starting transfers between devices  30.9 us (52%)
  waiting for transfers between devices  14.1 us (24%)
  Pallas kernels  11.8 us (20%)
  local copies, waits for them, and re-layouts  1.6 us (3%)
    ppermute x10, starting transfers between devices, along_z(): lax.ppermute(array, 'tensor', [(i, (i + 2 * step) % shards) for i in rang...  19.2 us
    all_to_all x1, starting transfers between devices, body(): lax.all_to_all(outgoing, 'dp', split_axis=0, concat_axis=0, tiled=True)  7.03 us
    pallas_call x1, Pallas kernels, product(): pl.pallas_call(product_kernel, out_shape=(jax.ShapeDtypeStruct((chips, ro...  5.87 us
    ppermute x10, waiting for transfers between devices, along_z(): lax.ppermute(array, 'tensor', [(i, (i + 2 * step) % shards) for i in rang...  5.09 us
    all_to_all x1, waiting for transfers between devices, body(): lax.all_to_all(expand, 'dp', split_axis=0, concat_axis=0, tiled=True)  4.12 us
    all_to_all x1, starting transfers between devices, body(): lax.all_to_all(expand, 'dp', split_axis=0, concat_axis=0, tiled=True)  4.02 us
    all_to_all x1, waiting for transfers between devices, body(): lax.all_to_all(outgoing, 'dp', split_axis=0, concat_axis=0, tiled=True)  3.28 us
    pallas_call x1, Pallas kernels, dispatch(): pl.pallas_call(functools.partial(dispatch_kernel, owned, capacity), out_s...  2.13 us
  transfers between devices with their start and end apart: 14, of which 6 were waited for; matrix products, arithmetic and copies ran while one was open for 0% of the time, Pallas kernels for 15%

profile of v4, /device:TPU:32, one launch (start us, length us, event | category | flops | bytes accessed | tf_op | source)
XLA Modules:
  0.0 58.4 jit_solution(11704320853232924071)
XLA Ops:
  0.0 2.1 %dispatch.1 = bf16[256,640]{1,0:T(8,128)(2,1)} custom-call(s32[1,128]{1,0:T(1,128)} %bitcast.15, bf16[128,512]{1,0:T(8,128)(2,1)} %x_hbm), custom_call_target="tpu_custom_call" | custom-call | flops 33554432 | bytes 262144 | tf_op jit(solution)/shard_map/dispatch/pallas_call | solution.py:54
  2.1 7.0 %all-to-all-start = ((bf16[16,16,640]{2,1,0:T(8,128)(2,1)}), bf16[16,16,640]{2,1,0:T(8,128)(2,1)S(1)}, u32[]{:S(2)}, u32[]{:S(2)}) async-start(bf16[16,16,640]{2,1,0:T(8,128)(2,1)} %bitcast.18), calls=%async_computation | async-start | bytes 655360 | tf_op jit(solution)/shard_map/all_to_all | solution.py:334
  9.2 5.9 %product.1 = (bf16[8,128,512]{2,1,0:T(8,128)(2,1)}, f32[8,128,512]{2,1,0:T(8,128)}) custom-call(s32[1]{0:T(128)} %bitcast.3.place_ref, bf16[128,512]{1,0:T(8,128)(2,1)} %x_hbm, bf16[128,512]{1,0:T(8,128)(2,1)} %residual_hbm.1, bf16[512,8192]{1,0:T(8,128)(2,1)} %w_hbm.1), custom_call_target="tpu_custom_call" | custom-call | flops 1073741824 | bytes 8388608 | tf_op jit(solution)/shard_map/product/pallas_call | solution.py:121
  15.1 3.3 %all-to-all-done = bf16[16,16,640]{2,1,0:T(8,128)(2,1)S(1)} async-done(((bf16[16,16,640]{2,1,0:T(8,128)(2,1)}), bf16[16,16,640]{2,1,0:T(8,128)(2,1)S(1)}, u32[]{:S(2)}, u32[]{:S(2)}) %all-to-all-start) | async-done | bytes 327712 | tf_op jit(solution)/shard_map/all_to_all | solution.py:334
  18.3 0.0 collective-permute-start
  18.3 0.5 shrink.1
  18.8 0.6 %collective-permute-start.1 = (f32[16,256]{1,0:T(8,128)S(1)}, f32[16,256]{1,0:T(8,128)S(1)}, u32[]{:S(2)}, u32[]{:S(2)}) collective-permute-start(f32[16,256]{1,0:T(8,128)S(1)} %shrink.1), channel_id=1, source_target_pairs={{0,1},{1,0},{2,3},{3,2},{4,5},{5,4},{6,7},{7,6},{8,9},{9,8},{10,11... | collective-permute-start | bytes 49160 | tf_op jit(solution)/shard_map/ppermute | solution.py:343
  19.4 1.6 %collective-permute-done.1 = f32[16,256]{1,0:T(8,128)S(1)} collective-permute-done((f32[16,256]{1,0:T(8,128)S(1)}, f32[16,256]{1,0:T(8,128)S(1)}, u32[]{:S(2)}, u32[]{:S(2)}) %collective-permute-start.1) | collective-permute-done | bytes 16416 | tf_op jit(solution)/shard_map/ppermute | solution.py:343
  21.0 1.9 %collective-permute-start.2 = (f32[16,256]{1,0:T(8,128)S(1)}, f32[16,256]{1,0:T(8,128)S(1)}, u32[]{:S(2)}, u32[]{:S(2)}) collective-permute-start(f32[16,256]{1,0:T(8,128)S(1)} %add.9), channel_id=1, source_target_pairs={{0,2},{1,3},{2,4},{3,5},{4,6},{5,7},{6,8},{7,9},{8,10},{9,11},{10,... | collective-permute-start | bytes 49160 | tf_op jit(solution)/shard_map/ppermute | solution.py:328
  22.9 0.1 collective-permute-start.3
  23.1 0.0 collective-permute-done.other_ref
  23.1 1.6 %copy-done = f32[8,128,512]{2,1,0:T(8,128)S(1)} copy-done((f32[8,128,512]{2,1,0:T(8,128)S(1)}, f32[8,128,512]{2,1,0:T(8,128)}, u32[]{:S(2)}) %copy-start) | copy-done | bytes 2097176
  24.7 0.9 %pair_sum.1 = (bf16[2,128,512]{2,1,0:T(8,128)(2,1)}, bf16[2,128,512]{2,1,0:T(8,128)(2,1)}, bf16[64,512]{1,0:T(8,128)(2,1)S(1)}, bf16[64,512]{1,0:T(8,128)(2,1)S(1)}, f32[3,128,512]{2,1,0:T(8,128)S(1)}) custom-call(s32[1]{0:T(128)} %bitcast.1.z_ref, f32[8,128,512]{2,1,0:T(8,128)S(1)} %copy-done, bf16[8,128,512]{2,1,0:T(8,128)(2,1)S(1)} %collective-permute-done.other_ref), custom_call_target="tpu_custom_call" | custom-call | flops 524288 | bytes 4194304 | tf_op jit(solution)/shard_map/pair_sum/pallas_call | solution.py:170
  25.6 0.0 collective-permute-done.2
  25.6 1.1 %collective-permute-done.3 = f32[16,256]{1,0:T(8,128)S(1)} collective-permute-done((f32[16,256]{1,0:T(8,128)S(1)}, f32[16,256]{1,0:T(8,128)S(1)}, u32[]{:S(2)}, u32[]{:S(2)}) %collective-permute-start.3) | collective-permute-done | bytes 16416 | tf_op jit(solution)/shard_map/ppermute | solution.py:328
  26.7 5.7 %collective-permute-start.7 = (bf16[64,512]{1,0:T(8,128)(2,1)S(1)}, bf16[64,512]{1,0:T(8,128)(2,1)S(1)}, u32[]{:S(2)}, u32[]{:S(2)}) collective-permute-start(bf16[64,512]{1,0:T(8,128)(2,1)S(1)} %get-tuple-element.45), channel_id=1, source_target_pairs={{0,4},{1,5},{2,6},{3,7},{4,8},{5,9},{6,10},{7,11},{8,12},{9,13},{1... | collective-permute-start | bytes 196616 | tf_op jit(solution)/shard_map/ppermute | solution.py:328
  32.4 0.0 collective-permute-start.8
  32.4 4.4 %collective-permute-start.6 = (f32[16,256]{1,0:T(8,128)S(1)}, f32[16,256]{1,0:T(8,128)S(1)}, u32[]{:S(2)}, u32[]{:S(2)}) collective-permute-start(f32[16,256]{1,0:T(8,128)S(1)} %get-tuple-element.53.three_ref), channel_id=1, source_target_pairs={{0,6},{1,7},{2,8},{3,9},{4,10},{5,11},{6,12},{7,13},{8,14},{9,15},... | collective-permute-start | bytes 49160 | tf_op jit(solution)/shard_map/ppermute | solution.py:328
  36.8 0.7 %collective-permute-start.11 = (f32[16,256]{1,0:T(8,128)S(1)}, f32[16,256]{1,0:T(8,128)S(1)}, u32[]{:S(2)}, u32[]{:S(2)}) collective-permute-start(f32[16,256]{1,0:T(8,128)S(1)} %get-tuple-element.54), channel_id=1, source_target_pairs={{0,10},{1,11},{2,12},{3,13},{4,14},{5,15},{6,0},{7,1},{8,2},{9,3},... | collective-permute-start | bytes 49160 | tf_op jit(solution)/shard_map/ppermute | solution.py:328
  37.5 0.9 %collective-permute-start.4 = (bf16[2,128,512]{2,1,0:T(8,128)(2,1)}, bf16[2,128,512]{2,1,0:T(8,128)(2,1)S(1)}, u32[]{:S(2)}, u32[]{:S(2)}) collective-permute-start(bf16[2,128,512]{2,1,0:T(8,128)(2,1)} %get-tuple-element.41), channel_id=1, source_target_pairs={{0,2},{1,3},{2,4},{3,5},{4,6},{5,7},{6,8},{7,9},{8,10},{9,11},{10,... | collective-permute-start | bytes 786440 | tf_op jit(solution)/shard_map/ppermute | solution.py:328
  38.4 0.9 %collective-permute-done.6.right_ref = f32[16,256]{1,0:T(8,128)S(1)} collective-permute-done((f32[16,256]{1,0:T(8,128)S(1)}, f32[16,256]{1,0:T(8,128)S(1)}, u32[]{:S(2)}, u32[]{:S(2)}) %collective-permute-start.6) | collective-permute-done | bytes 16416 | tf_op jit(solution)/shard_map/ppermute | solution.py:328
  39.2 1.3 %collective-permute-start.5 = (bf16[2,128,512]{2,1,0:T(8,128)(2,1)}, bf16[2,128,512]{2,1,0:T(8,128)(2,1)S(1)}, u32[]{:S(2)}, u32[]{:S(2)}) collective-permute-start(bf16[2,128,512]{2,1,0:T(8,128)(2,1)} %get-tuple-element.42), channel_id=1, source_target_pairs={{0,14},{1,15},{2,0},{3,1},{4,2},{5,3},{6,4},{7,5},{8,6},{9,7},{10,... | collective-permute-start | bytes 786440 | tf_op jit(solution)/shard_map/ppermute | solution.py:328
  40.6 0.0 collective-permute-done.7.half_right_ref
  40.6 3.1 %collective-permute-done.11.left_ref = f32[16,256]{1,0:T(8,128)S(1)} collective-permute-done((f32[16,256]{1,0:T(8,128)S(1)}, f32[16,256]{1,0:T(8,128)S(1)}, u32[]{:S(2)}, u32[]{:S(2)}) %collective-permute-start.11) | collective-permute-done | bytes 16416 | tf_op jit(solution)/shard_map/ppermute | solution.py:328
  43.7 1.3 %expand.1 = bf16[256,512]{1,0:T(8,128)(2,1)} custom-call(f32[16,256]{1,0:T(8,128)S(1)} %get-tuple-element.53.three_ref, f32[16,256]{1,0:T(8,128)S(1)} %collective-permute-done.6.right_ref, f32[16,256]{1,0:T(8,128)S(1)} %collective-permute-done.11.left_ref, bf16[256,640]{1,0:T(8,128)(2,1)S(1)} %bitcast.12, bf16[1024,512]{1,0:T(8,128)(2,1)S(1)} %bitcast.17), custom_call_target="tpu_custom_call" | custom-call | flops 99999997952 | bytes 1000000000 | tf_op jit(solution)/shard_map/expand/pallas_call | solution.py:270
  44.9 4.0 %all-to-all-start.1 = ((bf16[16,16,512]{2,1,0:T(8,128)(2,1)}), bf16[16,16,512]{2,1,0:T(8,128)(2,1)S(1)}, u32[]{:S(2)}, u32[]{:S(2)}) async-start(bf16[16,16,512]{2,1,0:T(8,128)(2,1)} %bitcast.8), calls=%async_computation.1 | async-start | bytes 524288 | tf_op jit(solution)/shard_map/all_to_all | solution.py:358
  49.0 0.0 collective-permute-done.4.right_ref
  49.0 0.1 relay.1
  49.1 1.3 %collective-permute-start.9 = (bf16[128,512]{1,0:T(8,128)(2,1)S(1)}, bf16[128,512]{1,0:T(8,128)(2,1)S(1)}, u32[]{:S(2)}, u32[]{:S(2)}) collective-permute-start(bf16[128,512]{1,0:T(8,128)(2,1)S(1)} %get-tuple-element.50), channel_id=1, source_target_pairs={{0,4},{1,5},{2,6},{3,7},{4,8},{5,9},{6,10},{7,11},{8,12},{9,13},{1... | collective-permute-start | bytes 393224 | tf_op jit(solution)/shard_map/ppermute | solution.py:328
  50.4 2.9 %collective-permute-start.10 = (bf16[128,512]{1,0:T(8,128)(2,1)S(1)}, bf16[128,512]{1,0:T(8,128)(2,1)S(1)}, u32[]{:S(2)}, u32[]{:S(2)}) collective-permute-start(bf16[128,512]{1,0:T(8,128)(2,1)S(1)} %get-tuple-element.51), channel_id=1, source_target_pairs={{0,12},{1,13},{2,14},{3,15},{4,0},{5,1},{6,2},{7,3},{8,4},{9,5},{1... | collective-permute-start | bytes 393224 | tf_op jit(solution)/shard_map/ppermute | solution.py:328
  53.3 4.1 %all-to-all-done.1 = bf16[16,16,512]{2,1,0:T(8,128)(2,1)S(1)} async-done(((bf16[16,16,512]{2,1,0:T(8,128)(2,1)}), bf16[16,16,512]{2,1,0:T(8,128)(2,1)S(1)}, u32[]{:S(2)}, u32[]{:S(2)}) %all-to-all-start.1) | async-done | bytes 262176 | tf_op jit(solution)/shard_map/all_to_all | solution.py:358
  57.4 1.0 %finish.1 = bf16[128,512]{1,0:T(8,128)(2,1)} custom-call(s32[1,128]{1,0:T(1,128)S(1)} %bitcast.16, f32[128,512]{1,0:T(8,128)S(1)} %get-tuple-element.49.here_ref, bf16[128,512]{1,0:T(8,128)(2,1)S(1)} %collective-permute-done.9.right_ref, bf16[128,512]{1,0:T(8,128)(2,1)S(1)} %collective-permute-done.10.left_ref, bf16[256,512]{1,0:T(8,128)(2,1)S(1)} %bitcast.13), custom_call_target="tpu_custom_call" | custom-call | flops 33554432 | bytes 524288 | tf_op jit(solution)/shard_map/finish/pallas_call | solution.py:301
  (13 shorter events, 0.0 us)
Async XLA Ops:
  0.0 18.3 %copy-start.1 = (bf16[64,512,16]{1,2,0:T(8,128)(2,1)S(1)}, bf16[64,512,16]{1,2,0:T(8,128)(2,1)}, u32[]{:S(2)}) copy-start(bf16[64,512,16]{1,2,0:T(8,128)(2,1)} %param.9) | copy-start | bytes 3145732
  0.0 43.7 %copy-start.3 = (bf16[64,16,512]{2,1,0:T(8,128)(2,1)S(1)}, bf16[64,16,512]{2,1,0:T(8,128)(2,1)}, u32[]{:S(2)}) copy-start(bf16[64,16,512]{2,1,0:T(8,128)(2,1)} %param.10) | copy-start | bytes 3145732
  2.1 16.2 %all-to-all-start = ((bf16[16,16,640]{2,1,0:T(8,128)(2,1)}), bf16[16,16,640]{2,1,0:T(8,128)(2,1)S(1)}, u32[]{:S(2)}, u32[]{:S(2)}) async-start(bf16[16,16,640]{2,1,0:T(8,128)(2,1)} %bitcast.18), calls=%async_computation | async-start | bytes 655360 | tf_op jit(solution)/shard_map/all_to_all | solution.py:334
  18.3 4.7 %collective-permute-start = (bf16[8,128,512]{2,1,0:T(8,128)(2,1)}, bf16[8,128,512]{2,1,0:T(8,128)(2,1)S(1)}, u32[]{:S(2)}, u32[]{:S(2)}) collective-permute-start(bf16[8,128,512]{2,1,0:T(8,128)(2,1)} %get-tuple-element.34), channel_id=1, source_target_pairs={{0,1},{1,0},{2,3},{3,2},{4,5},{5,4},{6,7},{7,6},{8,9},{9,8},{10,11... | collective-permute-start | bytes 3145736 | tf_op jit(solution)/shard_map/ppermute | solution.py:338
  18.8 2.2 %collective-permute-start.1 = (f32[16,256]{1,0:T(8,128)S(1)}, f32[16,256]{1,0:T(8,128)S(1)}, u32[]{:S(2)}, u32[]{:S(2)}) collective-permute-start(f32[16,256]{1,0:T(8,128)S(1)} %shrink.1), channel_id=1, source_target_pairs={{0,1},{1,0},{2,3},{3,2},{4,5},{5,4},{6,7},{7,6},{8,9},{9,8},{10,11... | collective-permute-start | bytes 49160 | tf_op jit(solution)/shard_map/ppermute | solution.py:343
  21.0 4.6 %collective-permute-start.2 = (f32[16,256]{1,0:T(8,128)S(1)}, f32[16,256]{1,0:T(8,128)S(1)}, u32[]{:S(2)}, u32[]{:S(2)}) collective-permute-start(f32[16,256]{1,0:T(8,128)S(1)} %add.9), channel_id=1, source_target_pairs={{0,2},{1,3},{2,4},{3,5},{4,6},{5,7},{6,8},{7,9},{8,10},{9,11},{10,... | collective-permute-start | bytes 49160 | tf_op jit(solution)/shard_map/ppermute | solution.py:328
  22.9 3.7 %collective-permute-start.3 = (f32[16,256]{1,0:T(8,128)S(1)}, f32[16,256]{1,0:T(8,128)S(1)}, u32[]{:S(2)}, u32[]{:S(2)}) collective-permute-start(f32[16,256]{1,0:T(8,128)S(1)} %add.9), channel_id=1, source_target_pairs={{0,14},{1,15},{2,0},{3,1},{4,2},{5,3},{6,4},{7,5},{8,6},{9,7},{10,... | collective-permute-start | bytes 49160 | tf_op jit(solution)/shard_map/ppermute | solution.py:328
  23.1 1.6 %copy-start = (f32[8,128,512]{2,1,0:T(8,128)S(1)}, f32[8,128,512]{2,1,0:T(8,128)}, u32[]{:S(2)}) copy-start(f32[8,128,512]{2,1,0:T(8,128)} %get-tuple-element.33.mine_ref) | copy-start | bytes 6291460
  26.7 13.9 %collective-permute-start.7 = (bf16[64,512]{1,0:T(8,128)(2,1)S(1)}, bf16[64,512]{1,0:T(8,128)(2,1)S(1)}, u32[]{:S(2)}, u32[]{:S(2)}) collective-permute-start(bf16[64,512]{1,0:T(8,128)(2,1)S(1)} %get-tuple-element.45), channel_id=1, source_target_pairs={{0,4},{1,5},{2,6},{3,7},{4,8},{5,9},{6,10},{7,11},{8,12},{9,13},{1... | collective-permute-start | bytes 196616 | tf_op jit(solution)/shard_map/ppermute | solution.py:328
  32.4 8.2 %collective-permute-start.8 = (bf16[64,512]{1,0:T(8,128)(2,1)S(1)}, bf16[64,512]{1,0:T(8,128)(2,1)S(1)}, u32[]{:S(2)}, u32[]{:S(2)}) collective-permute-start(bf16[64,512]{1,0:T(8,128)(2,1)S(1)} %get-tuple-element.46), channel_id=1, source_target_pairs={{0,12},{1,13},{2,14},{3,15},{4,0},{5,1},{6,2},{7,3},{8,4},{9,5},{1... | collective-permute-start | bytes 196616 | tf_op jit(solution)/shard_map/ppermute | solution.py:328
  32.4 6.8 %collective-permute-start.6 = (f32[16,256]{1,0:T(8,128)S(1)}, f32[16,256]{1,0:T(8,128)S(1)}, u32[]{:S(2)}, u32[]{:S(2)}) collective-permute-start(f32[16,256]{1,0:T(8,128)S(1)} %get-tuple-element.53.three_ref), channel_id=1, source_target_pairs={{0,6},{1,7},{2,8},{3,9},{4,10},{5,11},{6,12},{7,13},{8,14},{9,15},... | collective-permute-start | bytes 49160 | tf_op jit(solution)/shard_map/ppermute | solution.py:328
  36.8 6.9 %collective-permute-start.11 = (f32[16,256]{1,0:T(8,128)S(1)}, f32[16,256]{1,0:T(8,128)S(1)}, u32[]{:S(2)}, u32[]{:S(2)}) collective-permute-start(f32[16,256]{1,0:T(8,128)S(1)} %get-tuple-element.54), channel_id=1, source_target_pairs={{0,10},{1,11},{2,12},{3,13},{4,14},{5,15},{6,0},{7,1},{8,2},{9,3},... | collective-permute-start | bytes 49160 | tf_op jit(solution)/shard_map/ppermute | solution.py:328
  37.5 11.5 %collective-permute-start.4 = (bf16[2,128,512]{2,1,0:T(8,128)(2,1)}, bf16[2,128,512]{2,1,0:T(8,128)(2,1)S(1)}, u32[]{:S(2)}, u32[]{:S(2)}) collective-permute-start(bf16[2,128,512]{2,1,0:T(8,128)(2,1)} %get-tuple-element.41), channel_id=1, source_target_pairs={{0,2},{1,3},{2,4},{3,5},{4,6},{5,7},{6,8},{7,9},{8,10},{9,11},{10,... | collective-permute-start | bytes 786440 | tf_op jit(solution)/shard_map/ppermute | solution.py:328
  39.2 9.7 %collective-permute-start.5 = (bf16[2,128,512]{2,1,0:T(8,128)(2,1)}, bf16[2,128,512]{2,1,0:T(8,128)(2,1)S(1)}, u32[]{:S(2)}, u32[]{:S(2)}) collective-permute-start(bf16[2,128,512]{2,1,0:T(8,128)(2,1)} %get-tuple-element.42), channel_id=1, source_target_pairs={{0,14},{1,15},{2,0},{3,1},{4,2},{5,3},{6,4},{7,5},{8,6},{9,7},{10,... | collective-permute-start | bytes 786440 | tf_op jit(solution)/shard_map/ppermute | solution.py:328
  43.7 13.8 %copy-start.2 = (s32[128]{0:T(128)S(1)}, s32[128]{0:T(128)}, u32[]{:S(2)}) copy-start(s32[128]{0:T(128)} %param.11) | copy-start | bytes 1540
  44.9 12.5 %all-to-all-start.1 = ((bf16[16,16,512]{2,1,0:T(8,128)(2,1)}), bf16[16,16,512]{2,1,0:T(8,128)(2,1)S(1)}, u32[]{:S(2)}, u32[]{:S(2)}) async-start(bf16[16,16,512]{2,1,0:T(8,128)(2,1)} %bitcast.8), calls=%async_computation.1 | async-start | bytes 524288 | tf_op jit(solution)/shard_map/all_to_all | solution.py:358
  49.1 8.3 %collective-permute-start.9 = (bf16[128,512]{1,0:T(8,128)(2,1)S(1)}, bf16[128,512]{1,0:T(8,128)(2,1)S(1)}, u32[]{:S(2)}, u32[]{:S(2)}) collective-permute-start(bf16[128,512]{1,0:T(8,128)(2,1)S(1)} %get-tuple-element.50), channel_id=1, source_target_pairs={{0,4},{1,5},{2,6},{3,7},{4,8},{5,9},{6,10},{7,11},{8,12},{9,13},{1... | collective-permute-start | bytes 393224 | tf_op jit(solution)/shard_map/ppermute | solution.py:328
  50.4 7.0 %collective-permute-start.10 = (bf16[128,512]{1,0:T(8,128)(2,1)S(1)}, bf16[128,512]{1,0:T(8,128)(2,1)S(1)}, u32[]{:S(2)}, u32[]{:S(2)}) collective-permute-start(bf16[128,512]{1,0:T(8,128)(2,1)S(1)} %get-tuple-element.51), channel_id=1, source_target_pairs={{0,12},{1,13},{2,14},{3,15},{4,0},{5,1},{6,2},{7,3},{8,4},{9,5},{1... | collective-permute-start | bytes 393224 | tf_op jit(solution)/shard_map/ppermute | solution.py:328

commit v5 on v4

--- a/solution.py
+++ b/solution.py
@@ -335,12 +335,13 @@
 
     theirs, mine = product(place, x, residual, output_weight, chips)
     slots, theirs, mine = lax.optimization_barrier((slots, theirs, mine))
-    other = lax.ppermute(theirs, "tensor", siblings)
 
     slots = slots.reshape(slot_count, width + LANES)
     down = down_factors.transpose(0, 2, 1).reshape(owned * rank, width)
     shrink = shrink_terms(slots, down, owned)
     both = shrink + lax.ppermute(shrink, "tensor", siblings)
+    both, theirs = lax.optimization_barrier((both, theirs))
+    other = lax.ppermute(theirs, "tensor", siblings)
     *moving, keep = pair_sum(z, mine, other)
     before, after = along_z(both, 1), along_z(both, -1)
     before, after, *moving = lax.optimization_barrier((before, after, *moving))

time: 59.5 us -> 58.8 us (0.988)
  starting transfers between devices: 30.9 us -> 28.9 us
  waiting for transfers between devices: 14.1 us -> 15.4 us
    ppermute x10, starting transfers between devices: 19.2 us -> 17.7 us  [along_z(): lax.ppermute(array, 'tensor', [(i, (i + 2 * step) % shards) for i in rang...]
    all_to_all x1, waiting for transfers between devices: 4.12 us -> 5.33 us  [body(): lax.all_to_all(expand, 'dp', split_axis=0, concat_axis=0, tiled=True)]
    ppermute x1, waiting for transfers between devices: 0.01 us -> 0.68 us  [body(): other = lax.ppermute(theirs, 'tensor', siblings)]
  transfers between devices with their start and end apart: 14 -> 14, of which waited for: 6 -> 7; matrix products, arithmetic and copies ran while one was open for 0% -> 0% of each run, Pallas kernels for 15% -> 14%
where the time goes in v5:
time: 58.8 us; the launch traced here: 57.7 us
  starting transfers between devices  28.9 us (49%)
  waiting for transfers between devices  15.4 us (26%)
  Pallas kernels  11.7 us (20%)
  local copies, waits for them, and re-layouts  1.6 us (3%)
    ppermute x10, starting transfers between devices, along_z(): lax.ppermute(array, 'tensor', [(i, (i + 2 * step) % shards) for i in rang...  17.7 us
    all_to_all x1, starting transfers between devices, body(): lax.all_to_all(outgoing, 'dp', split_axis=0, concat_axis=0, tiled=True)  7.03 us
    pallas_call x1, Pallas kernels, product(): pl.pallas_call(product_kernel, out_shape=(jax.ShapeDtypeStruct((chips, ro...  5.87 us
    all_to_all x1, waiting for transfers between devices, body(): lax.all_to_all(expand, 'dp', split_axis=0, concat_axis=0, tiled=True)  5.33 us
    ppermute x10, waiting for transfers between devices, along_z(): lax.ppermute(array, 'tensor', [(i, (i + 2 * step) % shards) for i in rang...  4.93 us
    all_to_all x1, starting transfers between devices, body(): lax.all_to_all(expand, 'dp', split_axis=0, concat_axis=0, tiled=True)  3.95 us
    all_to_all x1, waiting for transfers between devices, body(): lax.all_to_all(outgoing, 'dp', split_axis=0, concat_axis=0, tiled=True)  3.28 us
    pallas_call x1, Pallas kernels, dispatch(): pl.pallas_call(functools.partial(dispatch_kernel, owned, capacity), out_s...  2.13 us
  transfers between devices with their start and end apart: 14, of which 7 were waited for; matrix products, arithmetic and copies ran while one was open for 0% of the time, Pallas kernels for 14%

profile of v5, /device:TPU:32, one launch (start us, length us, event | category | flops | bytes accessed | tf_op | source)
XLA Modules:
  0.0 57.7 jit_solution(5465260043684194780)
XLA Ops:
  0.0 2.1 %dispatch.1 = bf16[256,640]{1,0:T(8,128)(2,1)} custom-call(s32[1,128]{1,0:T(1,128)} %bitcast.15, bf16[128,512]{1,0:T(8,128)(2,1)} %x_hbm), custom_call_target="tpu_custom_call" | custom-call | flops 33554432 | bytes 262144 | tf_op jit(solution)/shard_map/dispatch/pallas_call | solution.py:54
  2.1 7.0 %all-to-all-start = ((bf16[16,16,640]{2,1,0:T(8,128)(2,1)}), bf16[16,16,640]{2,1,0:T(8,128)(2,1)S(1)}, u32[]{:S(2)}, u32[]{:S(2)}) async-start(bf16[16,16,640]{2,1,0:T(8,128)(2,1)} %bitcast.18), calls=%async_computation | async-start | bytes 655360 | tf_op jit(solution)/shard_map/all_to_all | solution.py:334
  9.2 5.9 %product.1 = (bf16[8,128,512]{2,1,0:T(8,128)(2,1)}, f32[8,128,512]{2,1,0:T(8,128)}) custom-call(s32[1]{0:T(128)} %bitcast.3.place_ref, bf16[128,512]{1,0:T(8,128)(2,1)} %x_hbm, bf16[128,512]{1,0:T(8,128)(2,1)} %residual_hbm.1, bf16[512,8192]{1,0:T(8,128)(2,1)} %w_hbm.1), custom_call_target="tpu_custom_call" | custom-call | flops 1073741824 | bytes 8388608 | tf_op jit(solution)/shard_map/product/pallas_call | solution.py:121
  15.1 3.3 %all-to-all-done = bf16[16,16,640]{2,1,0:T(8,128)(2,1)S(1)} async-done(((bf16[16,16,640]{2,1,0:T(8,128)(2,1)}), bf16[16,16,640]{2,1,0:T(8,128)(2,1)S(1)}, u32[]{:S(2)}, u32[]{:S(2)}) %all-to-all-start) | async-done | bytes 327712 | tf_op jit(solution)/shard_map/all_to_all | solution.py:334
  18.3 0.5 shrink.1
  18.8 0.1 collective-permute-start
  18.9 1.2 %collective-permute-done = f32[16,256]{1,0:T(8,128)S(1)} collective-permute-done((f32[16,256]{1,0:T(8,128)S(1)}, f32[16,256]{1,0:T(8,128)S(1)}, u32[]{:S(2)}, u32[]{:S(2)}) %collective-permute-start) | collective-permute-done | bytes 16416 | tf_op jit(solution)/shard_map/ppermute | solution.py:342
  20.1 0.2 collective-permute-start.1
  20.3 1.9 %collective-permute-start.2 = (f32[16,256]{1,0:T(8,128)S(1)}, f32[16,256]{1,0:T(8,128)S(1)}, u32[]{:S(2)}, u32[]{:S(2)}) collective-permute-start(f32[16,256]{1,0:T(8,128)S(1)} %add.9), channel_id=1, source_target_pairs={{0,2},{1,3},{2,4},{3,5},{4,6},{5,7},{6,8},{7,9},{8,10},{9,11},{10,... | collective-permute-start | bytes 49160 | tf_op jit(solution)/shard_map/ppermute | solution.py:328
  22.2 0.1 collective-permute-start.3
  22.3 0.7 %collective-permute-done.1.other_ref = bf16[8,128,512]{2,1,0:T(8,128)(2,1)S(1)} collective-permute-done((bf16[8,128,512]{2,1,0:T(8,128)(2,1)}, bf16[8,128,512]{2,1,0:T(8,128)(2,1)S(1)}, u32[]{:S(2)}, u32[]{:S(2)}) %collective-permute-start.1) | collective-permute-done | bytes 1048608 | tf_op jit(solution)/shard_map/ppermute | solution.py:344
  23.0 1.6 %copy-done = f32[8,128,512]{2,1,0:T(8,128)S(1)} copy-done((f32[8,128,512]{2,1,0:T(8,128)S(1)}, f32[8,128,512]{2,1,0:T(8,128)}, u32[]{:S(2)}) %copy-start) | copy-done | bytes 2097176
  24.6 0.8 %pair_sum.1 = (bf16[2,128,512]{2,1,0:T(8,128)(2,1)}, bf16[2,128,512]{2,1,0:T(8,128)(2,1)S(1)}, bf16[64,512]{1,0:T(8,128)(2,1)S(1)}, bf16[64,512]{1,0:T(8,128)(2,1)S(1)}, f32[3,128,512]{2,1,0:T(8,128)S(1)}) custom-call(s32[1]{0:T(128)} %bitcast.1.z_ref, f32[8,128,512]{2,1,0:T(8,128)S(1)} %copy-done, bf16[8,128,512]{2,1,0:T(8,128)(2,1)S(1)} %collective-permute-done.1.other_ref), custom_call_target="tpu_custom_call" | custom-call | flops 524288 | bytes 4194304 | tf_op jit(solution)/shard_map/pair_sum/pallas_call | solution.py:170
  25.4 0.0 collective-permute-done.2
  25.4 0.5 collective-permute-done.3
  25.9 5.7 %collective-permute-start.7 = (bf16[64,512]{1,0:T(8,128)(2,1)S(1)}, bf16[64,512]{1,0:T(8,128)(2,1)S(1)}, u32[]{:S(2)}, u32[]{:S(2)}) collective-permute-start(bf16[64,512]{1,0:T(8,128)(2,1)S(1)} %get-tuple-element.49), channel_id=1, source_target_pairs={{0,4},{1,5},{2,6},{3,7},{4,8},{5,9},{6,10},{7,11},{8,12},{9,13},{1... | collective-permute-start | bytes 196616 | tf_op jit(solution)/shard_map/ppermute | solution.py:328
  31.6 0.0 collective-permute-start.8
  31.6 4.3 %collective-permute-start.6 = (f32[16,256]{1,0:T(8,128)S(1)}, f32[16,256]{1,0:T(8,128)S(1)}, u32[]{:S(2)}, u32[]{:S(2)}) collective-permute-start(f32[16,256]{1,0:T(8,128)S(1)} %get-tuple-element.57.three_ref), channel_id=1, source_target_pairs={{0,6},{1,7},{2,8},{3,9},{4,10},{5,11},{6,12},{7,13},{8,14},{9,15},... | collective-permute-start | bytes 49160 | tf_op jit(solution)/shard_map/ppermute | solution.py:328
  35.9 0.8 %collective-permute-start.11 = (f32[16,256]{1,0:T(8,128)S(1)}, f32[16,256]{1,0:T(8,128)S(1)}, u32[]{:S(2)}, u32[]{:S(2)}) collective-permute-start(f32[16,256]{1,0:T(8,128)S(1)} %get-tuple-element.58), channel_id=1, source_target_pairs={{0,10},{1,11},{2,12},{3,13},{4,14},{5,15},{6,0},{7,1},{8,2},{9,3},... | collective-permute-start | bytes 49160 | tf_op jit(solution)/shard_map/ppermute | solution.py:328
  36.7 0.7 %collective-permute-start.4 = (bf16[2,128,512]{2,1,0:T(8,128)(2,1)}, bf16[2,128,512]{2,1,0:T(8,128)(2,1)S(1)}, u32[]{:S(2)}, u32[]{:S(2)}) collective-permute-start(bf16[2,128,512]{2,1,0:T(8,128)(2,1)} %get-tuple-element.45), channel_id=1, source_target_pairs={{0,2},{1,3},{2,4},{3,5},{4,6},{5,7},{6,8},{7,9},{8,10},{9,11},{10,... | collective-permute-start | bytes 786440 | tf_op jit(solution)/shard_map/ppermute | solution.py:328
  37.5 1.0 %collective-permute-done.6.right_ref = f32[16,256]{1,0:T(8,128)S(1)} collective-permute-done((f32[16,256]{1,0:T(8,128)S(1)}, f32[16,256]{1,0:T(8,128)S(1)}, u32[]{:S(2)}, u32[]{:S(2)}) %collective-permute-start.6) | collective-permute-done | bytes 16416 | tf_op jit(solution)/shard_map/ppermute | solution.py:328
  38.5 1.1 %collective-permute-start.5 = (bf16[2,128,512]{2,1,0:T(8,128)(2,1)S(1)}, bf16[2,128,512]{2,1,0:T(8,128)(2,1)S(1)}, u32[]{:S(2)}, u32[]{:S(2)}) collective-permute-start(bf16[2,128,512]{2,1,0:T(8,128)(2,1)S(1)} %get-tuple-element.46), channel_id=1, source_target_pairs={{0,14},{1,15},{2,0},{3,1},{4,2},{5,3},{6,4},{7,5},{8,6},{9,7},{10,... | collective-permute-start | bytes 786440 | tf_op jit(solution)/shard_map/ppermute | solution.py:328
  39.6 0.0 collective-permute-done.7.half_right_ref
  39.6 0.0 collective-permute-done.8.half_left_ref
  39.6 3.4 %collective-permute-done.11.left_ref = f32[16,256]{1,0:T(8,128)S(1)} collective-permute-done((f32[16,256]{1,0:T(8,128)S(1)}, f32[16,256]{1,0:T(8,128)S(1)}, u32[]{:S(2)}, u32[]{:S(2)}) %collective-permute-start.11) | collective-permute-done | bytes 16416 | tf_op jit(solution)/shard_map/ppermute | solution.py:328
  43.0 1.3 %expand.1 = bf16[256,512]{1,0:T(8,128)(2,1)} custom-call(f32[16,256]{1,0:T(8,128)S(1)} %get-tuple-element.57.three_ref, f32[16,256]{1,0:T(8,128)S(1)} %collective-permute-done.6.right_ref, f32[16,256]{1,0:T(8,128)S(1)} %collective-permute-done.11.left_ref, bf16[256,640]{1,0:T(8,128)(2,1)S(1)} %bitcast.12, bf16[1024,512]{1,0:T(8,128)(2,1)S(1)} %bitcast.17), custom_call_target="tpu_custom_call" | custom-call | flops 99999997952 | bytes 1000000000 | tf_op jit(solution)/shard_map/expand/pallas_call | solution.py:270
  44.2 4.0 %all-to-all-start.1 = ((bf16[16,16,512]{2,1,0:T(8,128)(2,1)}), bf16[16,16,512]{2,1,0:T(8,128)(2,1)S(1)}, u32[]{:S(2)}, u32[]{:S(2)}) async-start(bf16[16,16,512]{2,1,0:T(8,128)(2,1)} %bitcast.8), calls=%async_computation.1 | async-start | bytes 524288 | tf_op jit(solution)/shard_map/all_to_all | solution.py:359
  48.2 0.1 relay.1
  48.3 0.5 collective-permute-start.10
  48.8 2.5 %collective-permute-start.9 = (bf16[128,512]{1,0:T(8,128)(2,1)S(1)}, bf16[128,512]{1,0:T(8,128)(2,1)S(1)}, u32[]{:S(2)}, u32[]{:S(2)}) collective-permute-start(bf16[128,512]{1,0:T(8,128)(2,1)S(1)} %get-tuple-element.54), channel_id=1, source_target_pairs={{0,4},{1,5},{2,6},{3,7},{4,8},{5,9},{6,10},{7,11},{8,12},{9,13},{1... | collective-permute-start | bytes 393224 | tf_op jit(solution)/shard_map/ppermute | solution.py:328
  51.3 5.3 %all-to-all-done.1 = bf16[16,16,512]{2,1,0:T(8,128)(2,1)S(1)} async-done(((bf16[16,16,512]{2,1,0:T(8,128)(2,1)}), bf16[16,16,512]{2,1,0:T(8,128)(2,1)S(1)}, u32[]{:S(2)}, u32[]{:S(2)}) %all-to-all-start.1) | async-done | bytes 262176 | tf_op jit(solution)/shard_map/all_to_all | solution.py:359
  56.7 1.0 %finish.1 = bf16[128,512]{1,0:T(8,128)(2,1)} custom-call(s32[1,128]{1,0:T(1,128)S(1)} %bitcast.16, f32[128,512]{1,0:T(8,128)S(1)} %get-tuple-element.53.here_ref, bf16[128,512]{1,0:T(8,128)(2,1)S(1)} %collective-permute-done.9.right_ref, bf16[128,512]{1,0:T(8,128)(2,1)S(1)} %collective-permute-done.10.left_ref, bf16[256,512]{1,0:T(8,128)(2,1)S(1)} %bitcast.13), custom_call_target="tpu_custom_call" | custom-call | flops 33554432 | bytes 524288 | tf_op jit(solution)/shard_map/finish/pallas_call | solution.py:301
  (13 shorter events, 0.0 us)
Async XLA Ops:
  0.0 18.3 %copy-start.1 = (bf16[64,512,16]{1,2,0:T(8,128)(2,1)S(1)}, bf16[64,512,16]{1,2,0:T(8,128)(2,1)}, u32[]{:S(2)}) copy-start(bf16[64,512,16]{1,2,0:T(8,128)(2,1)} %param.9) | copy-start | bytes 3145732
  0.0 43.0 %copy-start.3 = (bf16[64,16,512]{2,1,0:T(8,128)(2,1)S(1)}, bf16[64,16,512]{2,1,0:T(8,128)(2,1)}, u32[]{:S(2)}) copy-start(bf16[64,16,512]{2,1,0:T(8,128)(2,1)} %param.10) | copy-start | bytes 3145732
  2.1 16.2 %all-to-all-start = ((bf16[16,16,640]{2,1,0:T(8,128)(2,1)}), bf16[16,16,640]{2,1,0:T(8,128)(2,1)S(1)}, u32[]{:S(2)}, u32[]{:S(2)}) async-start(bf16[16,16,640]{2,1,0:T(8,128)(2,1)} %bitcast.18), calls=%async_computation | async-start | bytes 655360 | tf_op jit(solution)/shard_map/all_to_all | solution.py:334
  18.8 1.3 %collective-permute-start = (f32[16,256]{1,0:T(8,128)S(1)}, f32[16,256]{1,0:T(8,128)S(1)}, u32[]{:S(2)}, u32[]{:S(2)}) collective-permute-start(f32[16,256]{1,0:T(8,128)S(1)} %shrink.1), channel_id=1, source_target_pairs={{0,1},{1,0},{2,3},{3,2},{4,5},{5,4},{6,7},{7,6},{8,9},{9,8},{10,11... | collective-permute-start | bytes 49160 | tf_op jit(solution)/shard_map/ppermute | solution.py:342
  20.1 2.9 %collective-permute-start.1 = (bf16[8,128,512]{2,1,0:T(8,128)(2,1)}, bf16[8,128,512]{2,1,0:T(8,128)(2,1)S(1)}, u32[]{:S(2)}, u32[]{:S(2)}) collective-permute-start(bf16[8,128,512]{2,1,0:T(8,128)(2,1)} %get-tuple-element.38), channel_id=1, source_target_pairs={{0,1},{1,0},{2,3},{3,2},{4,5},{5,4},{6,7},{7,6},{8,9},{9,8},{10,11... | collective-permute-start | bytes 3145736 | tf_op jit(solution)/shard_map/ppermute | solution.py:344
  20.3 5.1 %collective-permute-start.2 = (f32[16,256]{1,0:T(8,128)S(1)}, f32[16,256]{1,0:T(8,128)S(1)}, u32[]{:S(2)}, u32[]{:S(2)}) collective-permute-start(f32[16,256]{1,0:T(8,128)S(1)} %add.9), channel_id=1, source_target_pairs={{0,2},{1,3},{2,4},{3,5},{4,6},{5,7},{6,8},{7,9},{8,10},{9,11},{10,... | collective-permute-start | bytes 49160 | tf_op jit(solution)/shard_map/ppermute | solution.py:328
  22.2 3.7 %collective-permute-start.3 = (f32[16,256]{1,0:T(8,128)S(1)}, f32[16,256]{1,0:T(8,128)S(1)}, u32[]{:S(2)}, u32[]{:S(2)}) collective-permute-start(f32[16,256]{1,0:T(8,128)S(1)} %add.9), channel_id=1, source_target_pairs={{0,14},{1,15},{2,0},{3,1},{4,2},{5,3},{6,4},{7,5},{8,6},{9,7},{10,... | collective-permute-start | bytes 49160 | tf_op jit(solution)/shard_map/ppermute | solution.py:328
  23.0 1.6 %copy-start = (f32[8,128,512]{2,1,0:T(8,128)S(1)}, f32[8,128,512]{2,1,0:T(8,128)}, u32[]{:S(2)}) copy-start(f32[8,128,512]{2,1,0:T(8,128)} %get-tuple-element.35.mine_ref) | copy-start | bytes 6291460
  25.9 13.7 %collective-permute-start.7 = (bf16[64,512]{1,0:T(8,128)(2,1)S(1)}, bf16[64,512]{1,0:T(8,128)(2,1)S(1)}, u32[]{:S(2)}, u32[]{:S(2)}) collective-permute-start(bf16[64,512]{1,0:T(8,128)(2,1)S(1)} %get-tuple-element.49), channel_id=1, source_target_pairs={{0,4},{1,5},{2,6},{3,7},{4,8},{5,9},{6,10},{7,11},{8,12},{9,13},{1... | collective-permute-start | bytes 196616 | tf_op jit(solution)/shard_map/ppermute | solution.py:328
  31.6 8.0 %collective-permute-start.8 = (bf16[64,512]{1,0:T(8,128)(2,1)S(1)}, bf16[64,512]{1,0:T(8,128)(2,1)S(1)}, u32[]{:S(2)}, u32[]{:S(2)}) collective-permute-start(bf16[64,512]{1,0:T(8,128)(2,1)S(1)} %get-tuple-element.50), channel_id=1, source_target_pairs={{0,12},{1,13},{2,14},{3,15},{4,0},{5,1},{6,2},{7,3},{8,4},{9,5},{1... | collective-permute-start | bytes 196616 | tf_op jit(solution)/shard_map/ppermute | solution.py:328
  31.6 6.8 %collective-permute-start.6 = (f32[16,256]{1,0:T(8,128)S(1)}, f32[16,256]{1,0:T(8,128)S(1)}, u32[]{:S(2)}, u32[]{:S(2)}) collective-permute-start(f32[16,256]{1,0:T(8,128)S(1)} %get-tuple-element.57.three_ref), channel_id=1, source_target_pairs={{0,6},{1,7},{2,8},{3,9},{4,10},{5,11},{6,12},{7,13},{8,14},{9,15},... | collective-permute-start | bytes 49160 | tf_op jit(solution)/shard_map/ppermute | solution.py:328
  35.9 7.1 %collective-permute-start.11 = (f32[16,256]{1,0:T(8,128)S(1)}, f32[16,256]{1,0:T(8,128)S(1)}, u32[]{:S(2)}, u32[]{:S(2)}) collective-permute-start(f32[16,256]{1,0:T(8,128)S(1)} %get-tuple-element.58), channel_id=1, source_target_pairs={{0,10},{1,11},{2,12},{3,13},{4,14},{5,15},{6,0},{7,1},{8,2},{9,3},... | collective-permute-start | bytes 49160 | tf_op jit(solution)/shard_map/ppermute | solution.py:328
  36.7 11.5 %collective-permute-start.4 = (bf16[2,128,512]{2,1,0:T(8,128)(2,1)}, bf16[2,128,512]{2,1,0:T(8,128)(2,1)S(1)}, u32[]{:S(2)}, u32[]{:S(2)}) collective-permute-start(bf16[2,128,512]{2,1,0:T(8,128)(2,1)} %get-tuple-element.45), channel_id=1, source_target_pairs={{0,2},{1,3},{2,4},{3,5},{4,6},{5,7},{6,8},{7,9},{8,10},{9,11},{10,... | collective-permute-start | bytes 786440 | tf_op jit(solution)/shard_map/ppermute | solution.py:328
  38.5 9.7 %collective-permute-start.5 = (bf16[2,128,512]{2,1,0:T(8,128)(2,1)S(1)}, bf16[2,128,512]{2,1,0:T(8,128)(2,1)S(1)}, u32[]{:S(2)}, u32[]{:S(2)}) collective-permute-start(bf16[2,128,512]{2,1,0:T(8,128)(2,1)S(1)} %get-tuple-element.46), channel_id=1, source_target_pairs={{0,14},{1,15},{2,0},{3,1},{4,2},{5,3},{6,4},{7,5},{8,6},{9,7},{10,... | collective-permute-start | bytes 786440 | tf_op jit(solution)/shard_map/ppermute | solution.py:328
  43.0 13.7 %copy-start.2 = (s32[128]{0:T(128)S(1)}, s32[128]{0:T(128)}, u32[]{:S(2)}) copy-start(s32[128]{0:T(128)} %param.11) | copy-start | bytes 1540
  44.2 12.4 %all-to-all-start.1 = ((bf16[16,16,512]{2,1,0:T(8,128)(2,1)}), bf16[16,16,512]{2,1,0:T(8,128)(2,1)S(1)}, u32[]{:S(2)}, u32[]{:S(2)}) async-start(bf16[16,16,512]{2,1,0:T(8,128)(2,1)} %bitcast.8), calls=%async_computation.1 | async-start | bytes 524288 | tf_op jit(solution)/shard_map/all_to_all | solution.py:359
  48.3 8.3 %collective-permute-start.10 = (bf16[128,512]{1,0:T(8,128)(2,1)S(1)}, bf16[128,512]{1,0:T(8,128)(2,1)S(1)}, u32[]{:S(2)}, u32[]{:S(2)}) collective-permute-start(bf16[128,512]{1,0:T(8,128)(2,1)S(1)} %get-tuple-element.55), channel_id=1, source_target_pairs={{0,12},{1,13},{2,14},{3,15},{4,0},{5,1},{6,2},{7,3},{8,4},{9,5},{1... | collective-permute-start | bytes 393224 | tf_op jit(solution)/shard_map/ppermute | solution.py:328
  48.8 7.9 %collective-permute-start.9 = (bf16[128,512]{1,0:T(8,128)(2,1)S(1)}, bf16[128,512]{1,0:T(8,128)(2,1)S(1)}, u32[]{:S(2)}, u32[]{:S(2)}) collective-permute-start(bf16[128,512]{1,0:T(8,128)(2,1)S(1)} %get-tuple-element.54), channel_id=1, source_target_pairs={{0,4},{1,5},{2,6},{3,7},{4,8},{5,9},{6,10},{7,11},{8,12},{9,13},{1... | collective-permute-start | bytes 393224 | tf_op jit(solution)/shard_map/ppermute | solution.py:328

commit v6 on v5

--- a/solution.py
+++ b/solution.py
@@ -13,7 +13,7 @@
 RIGHT = (1, 3)
 LEFT = (-1, -3)
 KEEP = (0, 2, -2)
-PIECES = 2
+PIECES = (0, 4, 6, 8)
 GRANT = pltpu.CompilerParams(vmem_limit_bytes=16 * 2**20)
 WHOLE = pltpu.CompilerParams(vmem_limit_bytes=60 * 2**20)
 
@@ -84,9 +84,9 @@
     here, first = place_ref[0] >> 1, (place_ref[0] & 1) == 0
     chips, _, block = mine_ref.shape
     loads = [pltpu.make_async_copy(x_hbm, x_ref, x_sem)]
-    part = w_ref.shape[1] // PIECES
-    for piece in range(PIECES):
-        columns = slice(piece * part, (piece + 1) * part)
+    part = w_ref.shape[1] // chips
+    for piece, (start, stop) in enumerate(zip(PIECES, PIECES[1:])):
+        columns = slice(start * part, stop * part)
         loads.append(
             pltpu.make_async_copy(w_hbm.at[:, columns], w_ref.at[:, columns], w_sems.at[piece])
         )
@@ -97,8 +97,8 @@
     loads[0].wait()
     stores = []
     for z in range(chips):
-        if z % (chips // PIECES) == 0:
-            loads[1 + z // (chips // PIECES)].wait()
+        if z in PIECES:
+            loads[1 + PIECES.index(z)].wait()
         if z == 0:
             residual_load.wait()
         both = jnp.dot(
@@ -134,7 +134,7 @@
             pltpu.VMEM((chips, rows, block), F32),
             pltpu.SemaphoreType.DMA,
             pltpu.SemaphoreType.DMA,
-            pltpu.SemaphoreType.DMA((PIECES,)),
+            pltpu.SemaphoreType.DMA((len(PIECES) - 1,)),
             pltpu.SemaphoreType.DMA((2, chips)),
         ],
         cost_estimate=pl.CostEstimate(

time: 58.8 us -> 59 us (level)
  no operation moved by 1% of the time
where the time goes in v6:
time: 59 us; the launch traced here: 57.9 us
  starting transfers between devices  29.1 us (49%)
  waiting for transfers between devices  15.2 us (26%)
  Pallas kernels  11.9 us (20%)
  local copies, waits for them, and re-layouts  1.6 us (3%)
    ppermute x10, starting transfers between devices, along_z(): lax.ppermute(array, 'tensor', [(i, (i + 2 * step) % shards) for i in rang...  17.7 us
    all_to_all x1, starting transfers between devices, body(): lax.all_to_all(outgoing, 'dp', split_axis=0, concat_axis=0, tiled=True)  7.03 us
    pallas_call x1, Pallas kernels, product(): pl.pallas_call(product_kernel, out_shape=(jax.ShapeDtypeStruct((chips, ro...  6.08 us
    all_to_all x1, waiting for transfers between devices, body(): lax.all_to_all(expand, 'dp', split_axis=0, concat_axis=0, tiled=True)  5.33 us
    ppermute x10, waiting for transfers between devices, along_z(): lax.ppermute(array, 'tensor', [(i, (i + 2 * step) % shards) for i in rang...  4.93 us
    all_to_all x1, starting transfers between devices, body(): lax.all_to_all(expand, 'dp', split_axis=0, concat_axis=0, tiled=True)  4.13 us
    all_to_all x1, waiting for transfers between devices, body(): lax.all_to_all(outgoing, 'dp', split_axis=0, concat_axis=0, tiled=True)  3.07 us
    pallas_call x1, Pallas kernels, dispatch(): pl.pallas_call(functools.partial(dispatch_kernel, owned, capacity), out_s...  2.13 us
  transfers between devices with their start and end apart: 14, of which 7 were waited for; matrix products, arithmetic and copies ran while one was open for 0% of the time, Pallas kernels for 14%

profile of v6, /device:TPU:32, one launch (start us, length us, event | category | flops | bytes accessed | tf_op | source)
XLA Modules:
  0.0 57.9 jit_solution(12044027293613932435)
XLA Ops:
  0.0 2.1 %dispatch.1 = bf16[256,640]{1,0:T(8,128)(2,1)} custom-call(s32[1,128]{1,0:T(1,128)} %bitcast.15, bf16[128,512]{1,0:T(8,128)(2,1)} %x_hbm), custom_call_target="tpu_custom_call" | custom-call | flops 33554432 | bytes 262144 | tf_op jit(solution)/shard_map/dispatch/pallas_call | solution.py:54
  2.1 7.0 %all-to-all-start = ((bf16[16,16,640]{2,1,0:T(8,128)(2,1)}), bf16[16,16,640]{2,1,0:T(8,128)(2,1)S(1)}, u32[]{:S(2)}, u32[]{:S(2)}) async-start(bf16[16,16,640]{2,1,0:T(8,128)(2,1)} %bitcast.18), calls=%async_computation | async-start | bytes 655360 | tf_op jit(solution)/shard_map/all_to_all | solution.py:334
  9.2 6.1 %product.1 = (bf16[8,128,512]{2,1,0:T(8,128)(2,1)}, f32[8,128,512]{2,1,0:T(8,128)}) custom-call(s32[1]{0:T(128)} %bitcast.3.place_ref, bf16[128,512]{1,0:T(8,128)(2,1)} %x_hbm, bf16[128,512]{1,0:T(8,128)(2,1)} %residual_hbm.1, bf16[512,8192]{1,0:T(8,128)(2,1)} %w_hbm.1), custom_call_target="tpu_custom_call" | custom-call | flops 1073741824 | bytes 8388608 | tf_op jit(solution)/shard_map/product/pallas_call | solution.py:121
  15.3 3.1 %all-to-all-done = bf16[16,16,640]{2,1,0:T(8,128)(2,1)S(1)} async-done(((bf16[16,16,640]{2,1,0:T(8,128)(2,1)}), bf16[16,16,640]{2,1,0:T(8,128)(2,1)S(1)}, u32[]{:S(2)}, u32[]{:S(2)}) %all-to-all-start) | async-done | bytes 327712 | tf_op jit(solution)/shard_map/all_to_all | solution.py:334
  18.3 0.5 shrink.1
  18.8 0.1 collective-permute-start
  18.9 1.2 %collective-permute-done = f32[16,256]{1,0:T(8,128)S(1)} collective-permute-done((f32[16,256]{1,0:T(8,128)S(1)}, f32[16,256]{1,0:T(8,128)S(1)}, u32[]{:S(2)}, u32[]{:S(2)}) %collective-permute-start) | collective-permute-done | bytes 16416 | tf_op jit(solution)/shard_map/ppermute | solution.py:342
  20.1 0.2 collective-permute-start.1
  20.3 1.9 %collective-permute-start.2 = (f32[16,256]{1,0:T(8,128)S(1)}, f32[16,256]{1,0:T(8,128)S(1)}, u32[]{:S(2)}, u32[]{:S(2)}) collective-permute-start(f32[16,256]{1,0:T(8,128)S(1)} %add.9), channel_id=1, source_target_pairs={{0,2},{1,3},{2,4},{3,5},{4,6},{5,7},{6,8},{7,9},{8,10},{9,11},{10,... | collective-permute-start | bytes 49160 | tf_op jit(solution)/shard_map/ppermute | solution.py:328
  22.2 0.1 collective-permute-start.3
  22.3 0.7 %collective-permute-done.1.other_ref = bf16[8,128,512]{2,1,0:T(8,128)(2,1)S(1)} collective-permute-done((bf16[8,128,512]{2,1,0:T(8,128)(2,1)}, bf16[8,128,512]{2,1,0:T(8,128)(2,1)S(1)}, u32[]{:S(2)}, u32[]{:S(2)}) %collective-permute-start.1) | collective-permute-done | bytes 1048608 | tf_op jit(solution)/shard_map/ppermute | solution.py:344
  23.0 1.6 %copy-done = f32[8,128,512]{2,1,0:T(8,128)S(1)} copy-done((f32[8,128,512]{2,1,0:T(8,128)S(1)}, f32[8,128,512]{2,1,0:T(8,128)}, u32[]{:S(2)}) %copy-start) | copy-done | bytes 2097176
  24.6 0.8 %pair_sum.1 = (bf16[2,128,512]{2,1,0:T(8,128)(2,1)}, bf16[2,128,512]{2,1,0:T(8,128)(2,1)S(1)}, bf16[64,512]{1,0:T(8,128)(2,1)S(1)}, bf16[64,512]{1,0:T(8,128)(2,1)S(1)}, f32[3,128,512]{2,1,0:T(8,128)S(1)}) custom-call(s32[1]{0:T(128)} %bitcast.1.z_ref, f32[8,128,512]{2,1,0:T(8,128)S(1)} %copy-done, bf16[8,128,512]{2,1,0:T(8,128)(2,1)S(1)} %collective-permute-done.1.other_ref), custom_call_target="tpu_custom_call" | custom-call | flops 524288 | bytes 4194304 | tf_op jit(solution)/shard_map/pair_sum/pallas_call | solution.py:170
  25.4 0.0 collective-permute-done.2
  25.4 0.5 collective-permute-done.3
  25.9 5.7 %collective-permute-start.7 = (bf16[64,512]{1,0:T(8,128)(2,1)S(1)}, bf16[64,512]{1,0:T(8,128)(2,1)S(1)}, u32[]{:S(2)}, u32[]{:S(2)}) collective-permute-start(bf16[64,512]{1,0:T(8,128)(2,1)S(1)} %get-tuple-element.49), channel_id=1, source_target_pairs={{0,4},{1,5},{2,6},{3,7},{4,8},{5,9},{6,10},{7,11},{8,12},{9,13},{1... | collective-permute-start | bytes 196616 | tf_op jit(solution)/shard_map/ppermute | solution.py:328
  31.6 0.0 collective-permute-start.8
  31.6 4.3 %collective-permute-start.6 = (f32[16,256]{1,0:T(8,128)S(1)}, f32[16,256]{1,0:T(8,128)S(1)}, u32[]{:S(2)}, u32[]{:S(2)}) collective-permute-start(f32[16,256]{1,0:T(8,128)S(1)} %get-tuple-element.57.three_ref), channel_id=1, source_target_pairs={{0,6},{1,7},{2,8},{3,9},{4,10},{5,11},{6,12},{7,13},{8,14},{9,15},... | collective-permute-start | bytes 49160 | tf_op jit(solution)/shard_map/ppermute | solution.py:328
  35.9 0.8 %collective-permute-start.11 = (f32[16,256]{1,0:T(8,128)S(1)}, f32[16,256]{1,0:T(8,128)S(1)}, u32[]{:S(2)}, u32[]{:S(2)}) collective-permute-start(f32[16,256]{1,0:T(8,128)S(1)} %get-tuple-element.58), channel_id=1, source_target_pairs={{0,10},{1,11},{2,12},{3,13},{4,14},{5,15},{6,0},{7,1},{8,2},{9,3},... | collective-permute-start | bytes 49160 | tf_op jit(solution)/shard_map/ppermute | solution.py:328
  36.7 0.7 %collective-permute-start.4 = (bf16[2,128,512]{2,1,0:T(8,128)(2,1)}, bf16[2,128,512]{2,1,0:T(8,128)(2,1)S(1)}, u32[]{:S(2)}, u32[]{:S(2)}) collective-permute-start(bf16[2,128,512]{2,1,0:T(8,128)(2,1)} %get-tuple-element.45), channel_id=1, source_target_pairs={{0,2},{1,3},{2,4},{3,5},{4,6},{5,7},{6,8},{7,9},{8,10},{9,11},{10,... | collective-permute-start | bytes 786440 | tf_op jit(solution)/shard_map/ppermute | solution.py:328
  37.5 1.0 %collective-permute-done.6.right_ref = f32[16,256]{1,0:T(8,128)S(1)} collective-permute-done((f32[16,256]{1,0:T(8,128)S(1)}, f32[16,256]{1,0:T(8,128)S(1)}, u32[]{:S(2)}, u32[]{:S(2)}) %collective-permute-start.6) | collective-permute-done | bytes 16416 | tf_op jit(solution)/shard_map/ppermute | solution.py:328
  38.5 1.1 %collective-permute-start.5 = (bf16[2,128,512]{2,1,0:T(8,128)(2,1)S(1)}, bf16[2,128,512]{2,1,0:T(8,128)(2,1)S(1)}, u32[]{:S(2)}, u32[]{:S(2)}) collective-permute-start(bf16[2,128,512]{2,1,0:T(8,128)(2,1)S(1)} %get-tuple-element.46), channel_id=1, source_target_pairs={{0,14},{1,15},{2,0},{3,1},{4,2},{5,3},{6,4},{7,5},{8,6},{9,7},{10,... | collective-permute-start | bytes 786440 | tf_op jit(solution)/shard_map/ppermute | solution.py:328
  39.6 0.0 collective-permute-done.7.half_right_ref
  39.6 0.0 collective-permute-done.8.half_left_ref
  39.6 3.4 %collective-permute-done.11.left_ref = f32[16,256]{1,0:T(8,128)S(1)} collective-permute-done((f32[16,256]{1,0:T(8,128)S(1)}, f32[16,256]{1,0:T(8,128)S(1)}, u32[]{:S(2)}, u32[]{:S(2)}) %collective-permute-start.11) | collective-permute-done | bytes 16416 | tf_op jit(solution)/shard_map/ppermute | solution.py:328
  43.0 1.3 %expand.1 = bf16[256,512]{1,0:T(8,128)(2,1)} custom-call(f32[16,256]{1,0:T(8,128)S(1)} %get-tuple-element.57.three_ref, f32[16,256]{1,0:T(8,128)S(1)} %collective-permute-done.6.right_ref, f32[16,256]{1,0:T(8,128)S(1)} %collective-permute-done.11.left_ref, bf16[256,640]{1,0:T(8,128)(2,1)S(1)} %bitcast.12, bf16[1024,512]{1,0:T(8,128)(2,1)S(1)} %bitcast.17), custom_call_target="tpu_custom_call" | custom-call | flops 99999997952 | bytes 1000000000 | tf_op jit(solution)/shard_map/expand/pallas_call | solution.py:270
  44.2 4.1 %all-to-all-start.1 = ((bf16[16,16,512]{2,1,0:T(8,128)(2,1)}), bf16[16,16,512]{2,1,0:T(8,128)(2,1)S(1)}, u32[]{:S(2)}, u32[]{:S(2)}) async-start(bf16[16,16,512]{2,1,0:T(8,128)(2,1)} %bitcast.8), calls=%async_computation.1 | async-start | bytes 524288 | tf_op jit(solution)/shard_map/all_to_all | solution.py:359
  48.4 0.1 relay.1
  48.5 0.3 collective-permute-start.10
  48.8 2.7 %collective-permute-start.9 = (bf16[128,512]{1,0:T(8,128)(2,1)S(1)}, bf16[128,512]{1,0:T(8,128)(2,1)S(1)}, u32[]{:S(2)}, u32[]{:S(2)}) collective-permute-start(bf16[128,512]{1,0:T(8,128)(2,1)S(1)} %get-tuple-element.54), channel_id=1, source_target_pairs={{0,4},{1,5},{2,6},{3,7},{4,8},{5,9},{6,10},{7,11},{8,12},{9,13},{1... | collective-permute-start | bytes 393224 | tf_op jit(solution)/shard_map/ppermute | solution.py:328
  51.5 5.3 %all-to-all-done.1 = bf16[16,16,512]{2,1,0:T(8,128)(2,1)S(1)} async-done(((bf16[16,16,512]{2,1,0:T(8,128)(2,1)}), bf16[16,16,512]{2,1,0:T(8,128)(2,1)S(1)}, u32[]{:S(2)}, u32[]{:S(2)}) %all-to-all-start.1) | async-done | bytes 262176 | tf_op jit(solution)/shard_map/all_to_all | solution.py:359
  56.9 1.0 %finish.1 = bf16[128,512]{1,0:T(8,128)(2,1)} custom-call(s32[1,128]{1,0:T(1,128)S(1)} %bitcast.16, f32[128,512]{1,0:T(8,128)S(1)} %get-tuple-element.53.here_ref, bf16[128,512]{1,0:T(8,128)(2,1)S(1)} %collective-permute-done.9.right_ref, bf16[128,512]{1,0:T(8,128)(2,1)S(1)} %collective-permute-done.10.left_ref, bf16[256,512]{1,0:T(8,128)(2,1)S(1)} %bitcast.13), custom_call_target="tpu_custom_call" | custom-call | flops 33554432 | bytes 524288 | tf_op jit(solution)/shard_map/finish/pallas_call | solution.py:301
  (13 shorter events, 0.0 us)
Async XLA Ops:
  0.0 18.3 %copy-start.1 = (bf16[64,512,16]{1,2,0:T(8,128)(2,1)S(1)}, bf16[64,512,16]{1,2,0:T(8,128)(2,1)}, u32[]{:S(2)}) copy-start(bf16[64,512,16]{1,2,0:T(8,128)(2,1)} %param.9) | copy-start | bytes 3145732
  0.0 43.0 %copy-start.3 = (bf16[64,16,512]{2,1,0:T(8,128)(2,1)S(1)}, bf16[64,16,512]{2,1,0:T(8,128)(2,1)}, u32[]{:S(2)}) copy-start(bf16[64,16,512]{2,1,0:T(8,128)(2,1)} %param.10) | copy-start | bytes 3145732
  2.1 16.2 %all-to-all-start = ((bf16[16,16,640]{2,1,0:T(8,128)(2,1)}), bf16[16,16,640]{2,1,0:T(8,128)(2,1)S(1)}, u32[]{:S(2)}, u32[]{:S(2)}) async-start(bf16[16,16,640]{2,1,0:T(8,128)(2,1)} %bitcast.18), calls=%async_computation | async-start | bytes 655360 | tf_op jit(solution)/shard_map/all_to_all | solution.py:334
  18.8 1.3 %collective-permute-start = (f32[16,256]{1,0:T(8,128)S(1)}, f32[16,256]{1,0:T(8,128)S(1)}, u32[]{:S(2)}, u32[]{:S(2)}) collective-permute-start(f32[16,256]{1,0:T(8,128)S(1)} %shrink.1), channel_id=1, source_target_pairs={{0,1},{1,0},{2,3},{3,2},{4,5},{5,4},{6,7},{7,6},{8,9},{9,8},{10,11... | collective-permute-start | bytes 49160 | tf_op jit(solution)/shard_map/ppermute | solution.py:342
  20.1 2.9 %collective-permute-start.1 = (bf16[8,128,512]{2,1,0:T(8,128)(2,1)}, bf16[8,128,512]{2,1,0:T(8,128)(2,1)S(1)}, u32[]{:S(2)}, u32[]{:S(2)}) collective-permute-start(bf16[8,128,512]{2,1,0:T(8,128)(2,1)} %get-tuple-element.38), channel_id=1, source_target_pairs={{0,1},{1,0},{2,3},{3,2},{4,5},{5,4},{6,7},{7,6},{8,9},{9,8},{10,11... | collective-permute-start | bytes 3145736 | tf_op jit(solution)/shard_map/ppermute | solution.py:344
  20.3 5.1 %collective-permute-start.2 = (f32[16,256]{1,0:T(8,128)S(1)}, f32[16,256]{1,0:T(8,128)S(1)}, u32[]{:S(2)}, u32[]{:S(2)}) collective-permute-start(f32[16,256]{1,0:T(8,128)S(1)} %add.9), channel_id=1, source_target_pairs={{0,2},{1,3},{2,4},{3,5},{4,6},{5,7},{6,8},{7,9},{8,10},{9,11},{10,... | collective-permute-start | bytes 49160 | tf_op jit(solution)/shard_map/ppermute | solution.py:328
  22.2 3.7 %collective-permute-start.3 = (f32[16,256]{1,0:T(8,128)S(1)}, f32[16,256]{1,0:T(8,128)S(1)}, u32[]{:S(2)}, u32[]{:S(2)}) collective-permute-start(f32[16,256]{1,0:T(8,128)S(1)} %add.9), channel_id=1, source_target_pairs={{0,14},{1,15},{2,0},{3,1},{4,2},{5,3},{6,4},{7,5},{8,6},{9,7},{10,... | collective-permute-start | bytes 49160 | tf_op jit(solution)/shard_map/ppermute | solution.py:328
  23.0 1.6 %copy-start = (f32[8,128,512]{2,1,0:T(8,128)S(1)}, f32[8,128,512]{2,1,0:T(8,128)}, u32[]{:S(2)}) copy-start(f32[8,128,512]{2,1,0:T(8,128)} %get-tuple-element.35.mine_ref) | copy-start | bytes 6291460
  25.9 13.7 %collective-permute-start.7 = (bf16[64,512]{1,0:T(8,128)(2,1)S(1)}, bf16[64,512]{1,0:T(8,128)(2,1)S(1)}, u32[]{:S(2)}, u32[]{:S(2)}) collective-permute-start(bf16[64,512]{1,0:T(8,128)(2,1)S(1)} %get-tuple-element.49), channel_id=1, source_target_pairs={{0,4},{1,5},{2,6},{3,7},{4,8},{5,9},{6,10},{7,11},{8,12},{9,13},{1... | collective-permute-start | bytes 196616 | tf_op jit(solution)/shard_map/ppermute | solution.py:328
  31.6 8.0 %collective-permute-start.8 = (bf16[64,512]{1,0:T(8,128)(2,1)S(1)}, bf16[64,512]{1,0:T(8,128)(2,1)S(1)}, u32[]{:S(2)}, u32[]{:S(2)}) collective-permute-start(bf16[64,512]{1,0:T(8,128)(2,1)S(1)} %get-tuple-element.50), channel_id=1, source_target_pairs={{0,12},{1,13},{2,14},{3,15},{4,0},{5,1},{6,2},{7,3},{8,4},{9,5},{1... | collective-permute-start | bytes 196616 | tf_op jit(solution)/shard_map/ppermute | solution.py:328
  31.6 6.8 %collective-permute-start.6 = (f32[16,256]{1,0:T(8,128)S(1)}, f32[16,256]{1,0:T(8,128)S(1)}, u32[]{:S(2)}, u32[]{:S(2)}) collective-permute-start(f32[16,256]{1,0:T(8,128)S(1)} %get-tuple-element.57.three_ref), channel_id=1, source_target_pairs={{0,6},{1,7},{2,8},{3,9},{4,10},{5,11},{6,12},{7,13},{8,14},{9,15},... | collective-permute-start | bytes 49160 | tf_op jit(solution)/shard_map/ppermute | solution.py:328
  35.9 7.1 %collective-permute-start.11 = (f32[16,256]{1,0:T(8,128)S(1)}, f32[16,256]{1,0:T(8,128)S(1)}, u32[]{:S(2)}, u32[]{:S(2)}) collective-permute-start(f32[16,256]{1,0:T(8,128)S(1)} %get-tuple-element.58), channel_id=1, source_target_pairs={{0,10},{1,11},{2,12},{3,13},{4,14},{5,15},{6,0},{7,1},{8,2},{9,3},... | collective-permute-start | bytes 49160 | tf_op jit(solution)/shard_map/ppermute | solution.py:328
  36.7 11.7 %collective-permute-start.4 = (bf16[2,128,512]{2,1,0:T(8,128)(2,1)}, bf16[2,128,512]{2,1,0:T(8,128)(2,1)S(1)}, u32[]{:S(2)}, u32[]{:S(2)}) collective-permute-start(bf16[2,128,512]{2,1,0:T(8,128)(2,1)} %get-tuple-element.45), channel_id=1, source_target_pairs={{0,2},{1,3},{2,4},{3,5},{4,6},{5,7},{6,8},{7,9},{8,10},{9,11},{10,... | collective-permute-start | bytes 786440 | tf_op jit(solution)/shard_map/ppermute | solution.py:328
  38.5 9.9 %collective-permute-start.5 = (bf16[2,128,512]{2,1,0:T(8,128)(2,1)S(1)}, bf16[2,128,512]{2,1,0:T(8,128)(2,1)S(1)}, u32[]{:S(2)}, u32[]{:S(2)}) collective-permute-start(bf16[2,128,512]{2,1,0:T(8,128)(2,1)S(1)} %get-tuple-element.46), channel_id=1, source_target_pairs={{0,14},{1,15},{2,0},{3,1},{4,2},{5,3},{6,4},{7,5},{8,6},{9,7},{10,... | collective-permute-start | bytes 786440 | tf_op jit(solution)/shard_map/ppermute | solution.py:328
  43.0 13.9 %copy-start.2 = (s32[128]{0:T(128)S(1)}, s32[128]{0:T(128)}, u32[]{:S(2)}) copy-start(s32[128]{0:T(128)} %param.11) | copy-start | bytes 1540
  44.2 12.6 %all-to-all-start.1 = ((bf16[16,16,512]{2,1,0:T(8,128)(2,1)}), bf16[16,16,512]{2,1,0:T(8,128)(2,1)S(1)}, u32[]{:S(2)}, u32[]{:S(2)}) async-start(bf16[16,16,512]{2,1,0:T(8,128)(2,1)} %bitcast.8), calls=%async_computation.1 | async-start | bytes 524288 | tf_op jit(solution)/shard_map/all_to_all | solution.py:359
  48.5 8.3 %collective-permute-start.10 = (bf16[128,512]{1,0:T(8,128)(2,1)S(1)}, bf16[128,512]{1,0:T(8,128)(2,1)S(1)}, u32[]{:S(2)}, u32[]{:S(2)}) collective-permute-start(bf16[128,512]{1,0:T(8,128)(2,1)S(1)} %get-tuple-element.55), channel_id=1, source_target_pairs={{0,12},{1,13},{2,14},{3,15},{4,0},{5,1},{6,2},{7,3},{8,4},{9,5},{1... | collective-permute-start | bytes 393224 | tf_op jit(solution)/shard_map/ppermute | solution.py:328
  48.8 8.1 %collective-permute-start.9 = (bf16[128,512]{1,0:T(8,128)(2,1)S(1)}, bf16[128,512]{1,0:T(8,128)(2,1)S(1)}, u32[]{:S(2)}, u32[]{:S(2)}) collective-permute-start(bf16[128,512]{1,0:T(8,128)(2,1)S(1)} %get-tuple-element.54), channel_id=1, source_target_pairs={{0,4},{1,5},{2,6},{3,7},{4,8},{5,9},{6,10},{7,11},{8,12},{9,13},{1... | collective-permute-start | bytes 393224 | tf_op jit(solution)/shard_map/ppermute | solution.py:328
